TPU v7x, 32 devices: a whole 2x2x4 slice. The times are simulated.
32 devices in a mesh: rep: 4 (over x, core), shard: 8 (over z, y).
Axes of the slice: x: 2, y: 2, z: 4, core: 2. Of those that a mesh axis runs over, the one named last changes fastest.
Arguments:
- block_input: bfloat16 [16384, 2048], P(('rep', 'shard')), may hold values from -6 to 6
- cotangent: bfloat16 [16384, 2048], P(('rep', 'shard')), may hold values from -6 to 6
- seq_lengths: int32 [4], replicated, may hold values from 1024 to 4096, as said below
- slot_order: int32 [4], replicated, may hold values from 0 to 3, each once
- norm_gain: bfloat16 [2048], P('shard'), may hold values from 0.5 to 1.5
- in_proj: bfloat16 [2048, 8192], P('shard'), may hold values from -0.125 to 0.125
- conv_weight: bfloat16 [4, 4096], P(None, 'shard'), may hold values from -3 to 3
- conv_bias: bfloat16 [4096], P('shard'), may hold values from -3 to 3
- x_proj: bfloat16 [4096, 160], P('shard'), may hold values from -0.09375 to 0.09375
- dt_proj: bfloat16 [128, 4096], P(None, 'shard'), may hold values from -0.5 to 0.5
- dt_bias: bfloat16 [4096], P('shard'), may hold values from -7 to -3
- a_log: bfloat16 [16, 4096], P(None, 'shard'), may hold values from -4 to 0.5
- d_skip: bfloat16 [4096], P('shard'), may hold values from 0.5 to 1.5
- out_proj: bfloat16 [4096, 2048], P('shard'), may hold values from -0.375 to 0.375
Outputs:
- activations: bfloat16 [16384, 2048], P(('rep', 'shard'))
- input_grad: float32 [16384, 2048], P(('rep', 'shard'))
- grad_norm_gain: float32 [2048], P('shard')
- grad_in_proj: float32 [2048, 8192], P('shard')
- grad_conv_weight: float32 [4, 4096], P(None, 'shard')
- grad_conv_bias: float32 [4096], P('shard')
- grad_x_proj: float32 [4096, 160], P('shard')
- grad_dt_proj: float32 [128, 4096], P(None, 'shard')
- grad_dt_bias: float32 [4096], P('shard')
- grad_a_log: float32 [16, 4096], P(None, 'shard')
- grad_d_skip: float32 [4096], P('shard')
- grad_out_proj: float32 [4096, 2048], P('shard')
Inputs may be any that keep to these rules, and one draw needn't show every extreme that they name: `seq_lengths`: each sequence has 1024 to 4096 tokens; one sequence has exactly 4096 and one exactly 1024.
All inputs are finite; a program needn't handle non-finite values.
Results may differ from a plain program's by a relative error of at most 0.015.
Values may be sent and summed in bfloat16 or wider, within the bound.
A program may use at most 384 MiB of HBM per device.

v0:
```python
from functools import partial

import jax
import jax.numpy as jnp
from jax import lax
from jax.sharding import PartitionSpec as P

STRETCH = 32


EPSILON = 1e-05
HIGHEST = lax.Precision.HIGHEST


def shifted(value, axis, steps):
    count = lax.axis_size(axis)
    first, last = (max(0, -steps), min(count, count - steps))
    return lax.ppermute(value, axis, [(source, source + steps) for source in range(first, last)])


def prefix(value, axis, combine, identity, reverse):
    devices, mine = (lax.axis_size(axis), lax.axis_index(axis))
    everything = jax.tree.map(lambda part: lax.all_gather(part, axis), value)
    start = jax.tree.map(
        lambda part, zero: jnp.broadcast_to(jnp.asarray(zero, part.dtype), part.shape),
        value,
        identity,
    )

    def lap(k, before):
        at = devices - 1 - k if reverse else k
        reached = at > mine if reverse else at < mine
        new = combine(before, jax.tree.map(lambda part: part[at], everything))
        return jax.tree.map(lambda a, b: jnp.where(reached, a, b), new, before)

    return lax.fori_loop(0, devices, lap, start)


def split_blocks(values, width):
    return values.reshape((values.shape[0] // width, width) + values.shape[1:])


def combine_maps(earlier, later):
    return (earlier[0] * later[0], later[0] * earlier[1] + later[1])


def contract_rows(left, right):
    return lax.dot_general(
        left, right, (((0,), (0,)), ((), ())), preferred_element_type=jnp.float32
    )


def contract_cols(left, right):
    return lax.dot_general(
        left, right, (((1,), (1,)), ((), ())), preferred_element_type=jnp.float32
    )


def selective(step_size, conv_out, input_coeff, output_coeff, rates, start_state):

    @jax.checkpoint
    def selective_block_step(state, pieces):
        step_block, conv_block, input_block, output_block = pieces
        running = jnp.cumsum(step_block, axis=0)
        exponent = rates[None, :, :] * running[:, None, :]
        feeding = (step_block * conv_block)[:, None, :] * input_block[:, :, None]
        summed = jnp.cumsum(jnp.exp(-exponent) * feeding, axis=0)
        states = jnp.exp(exponent) * (state[None, :, :] + summed)
        emitted = jnp.einsum("qn,qne->qe", output_block, states, precision=HIGHEST)
        return (states[-1], emitted)

    final_state, emitted = lax.scan(
        selective_block_step,
        start_state,
        (
            split_blocks(step_size, STRETCH),
            split_blocks(conv_out, STRETCH),
            split_blocks(input_coeff, STRETCH),
            split_blocks(output_coeff, STRETCH),
        ),
    )
    return (emitted.reshape(step_size.shape), final_state)


def end_state(step_size, conv_out, input_coeff, rates):

    def end_block_step(state, pieces):
        step_block, conv_block, input_block = pieces
        running = jnp.cumsum(step_block, axis=0)
        total = running[-1]
        weighting = jnp.exp(rates[None, :, :] * (total[None, None, :] - running[:, None, :]))
        feeding = (step_block * conv_block)[:, None, :] * input_block[:, :, None]
        return (
            jnp.exp(rates * total[None, :]) * state + jnp.sum(weighting * feeding, axis=0),
            None,
        )

    start_state = jnp.zeros(rates.shape, jnp.float32)
    final_state, unused = lax.scan(
        end_block_step,
        start_state,
        (
            split_blocks(step_size, STRETCH),
            split_blocks(conv_out, STRETCH),
            split_blocks(input_coeff, STRETCH),
        ),
    )
    return final_state


def start_weight(step_size, output_coeff, g_scanned, rates):

    def start_block_step(carry, pieces):
        total, before = carry
        step_block, output_block, grad_block = pieces
        running = before[None, :] + jnp.cumsum(step_block, axis=0)
        weighting = jnp.exp(rates[None, :, :] * running[:, None, :])
        total = total + jnp.sum(
            weighting * output_block[:, :, None] * grad_block[:, None, :], axis=0
        )
        return ((total, running[-1]), None)

    initial = (jnp.zeros(rates.shape, jnp.float32), jnp.zeros((rates.shape[1],), jnp.float32))
    result, unused = lax.scan(
        start_block_step,
        initial,
        (
            split_blocks(step_size, STRETCH),
            split_blocks(output_coeff, STRETCH),
            split_blocks(g_scanned, STRETCH),
        ),
    )
    return result[0]


def conv_local(edge_rows, conv_in, taps, bias_row, keep_prev):
    tok_rows = conv_in.shape[0]
    padded = jnp.concatenate([edge_rows * keep_prev, conv_in], axis=0)
    total = bias_row[None, :]
    for offset in range(taps.shape[0]):
        total = total + taps[offset][None, :] * padded[offset : offset + tok_rows]
    return jax.nn.silu(total)


def mixer_scan(
    step_size, conv_low, input_coeff, output_coeff, log_rates, skip_gain, gate_in, start_state
):
    rates = -jnp.exp(log_rates)
    scanned, final_state = selective(
        step_size, conv_low, input_coeff, output_coeff, rates, start_state
    )
    scanned = scanned + skip_gain[None, :] * conv_low
    return (scanned * jax.nn.silu(gate_in), final_state)


def on_device(
    block_input,
    cotangent,
    seq_lengths,
    slot_order,
    norm_gain,
    in_proj,
    conv_weight,
    conv_bias,
    x_proj,
    dt_proj,
    dt_bias,
    a_log,
    d_skip,
    out_proj,
):
    n_shard = lax.axis_size("shard")
    tok_rows = block_input.shape[0]
    inner_width = conv_bias.shape[0] * n_shard
    rank_width = dt_proj.shape[0]
    state_width = a_log.shape[0]
    kernel_taps = conv_weight.shape[0]
    span_devs = max(1, min(n_shard, 4096 // tok_rows))
    shard_at = lax.axis_index("shard")
    rep_at = lax.axis_index("rep")
    in_slot = shard_at % span_devs
    keep_prev = (in_slot != 0).astype(jnp.float32)
    slot_at = (rep_at * n_shard + shard_at) // span_devs
    slot_len = jnp.sum(jnp.where(slot_order == slot_at, seq_lengths, 0))
    places = in_slot * tok_rows + jnp.arange(tok_rows, dtype=jnp.int32)
    valid_rows = (places < slot_len).astype(jnp.float32)[:, None]
    gathered = (
        lax.all_gather(norm_gain, "shard", axis=0, tiled=True),
        lax.all_gather(in_proj, "shard", axis=0, tiled=True),
        lax.all_gather(conv_weight, "shard", axis=1, tiled=True),
        lax.all_gather(conv_bias, "shard", axis=0, tiled=True),
        lax.all_gather(x_proj, "shard", axis=0, tiled=True),
        lax.all_gather(dt_proj, "shard", axis=1, tiled=True),
        lax.all_gather(dt_bias, "shard", axis=0, tiled=True),
        lax.all_gather(a_log, "shard", axis=1, tiled=True),
        lax.all_gather(d_skip, "shard", axis=0, tiled=True),
        lax.all_gather(out_proj, "shard", axis=0, tiled=True),
    )
    (
        gain_all,
        in_all,
        taps_all,
        bias_all,
        xproj_all,
        dtproj_all,
        dtbias_all,
        alog_all,
        skip_all,
        out_all,
    ) = gathered
    gain_f = gain_all.astype(jnp.float32)
    input_f = block_input.astype(jnp.float32)
    scale = lax.rsqrt(jnp.mean(input_f * input_f, axis=1, keepdims=True) + EPSILON)
    normed = (input_f * scale * gain_f[None, :]).astype(jnp.bfloat16)
    mixed_in = jnp.dot(normed, in_all, preferred_element_type=jnp.float32)
    conv_in = mixed_in[:, :inner_width].astype(jnp.bfloat16)
    gate_in = mixed_in[:, inner_width:]
    edge_rows = shifted(conv_in[tok_rows - (kernel_taps - 1) :], "shard", 1)
    conv_f, conv_back = jax.vjp(
        partial(conv_local, keep_prev=keep_prev),
        edge_rows.astype(jnp.float32),
        conv_in.astype(jnp.float32),
        taps_all.astype(jnp.float32),
        bias_all.astype(jnp.float32),
    )
    conv_out = conv_f.astype(jnp.bfloat16)
    conv_low = conv_out.astype(jnp.float32)
    projected = jnp.dot(conv_out, xproj_all, preferred_element_type=jnp.float32)
    step_low = projected[:, :rank_width].astype(jnp.bfloat16)
    input_coeff = projected[:, rank_width : rank_width + state_width]
    output_coeff = projected[:, rank_width + state_width :]
    step_pre = (
        jnp.dot(step_low, dtproj_all, preferred_element_type=jnp.float32)
        + dtbias_all.astype(jnp.float32)[None, :]
    )
    step_size = jax.nn.softplus(step_pre)
    log_rates = alog_all.astype(jnp.float32)
    rates = -jnp.exp(log_rates)
    local_end = end_state(step_size, conv_low, input_coeff, rates)
    through = jnp.exp(rates * jnp.sum(step_size, axis=0)[None, :])
    carried = prefix(
        (through * keep_prev, local_end),
        "shard",
        combine_maps,
        (jnp.ones_like(through), jnp.zeros_like(local_end)),
        False,
    )
    start_state = carried[1] * keep_prev
    mixer_out, scan_back = jax.vjp(
        mixer_scan,
        step_size,
        conv_low,
        input_coeff,
        output_coeff,
        log_rates,
        skip_all.astype(jnp.float32),
        gate_in,
        start_state,
    )
    gated = mixer_out[0].astype(jnp.bfloat16)
    branch = jnp.dot(gated, out_all, preferred_element_type=jnp.float32)
    activations = (input_f + valid_rows * branch).astype(jnp.bfloat16)
    in_back, xproj_back, dtproj_back, out_back = (
        lax.all_gather(in_proj, "shard", axis=0, tiled=True),
        lax.all_gather(x_proj, "shard", axis=0, tiled=True),
        lax.all_gather(dt_proj, "shard", axis=1, tiled=True),
        lax.all_gather(out_proj, "shard", axis=0, tiled=True),
    )
    cot_f = cotangent.astype(jnp.float32)
    back_rows = (cot_f * valid_rows).astype(jnp.bfloat16)
    grad_out_proj = contract_rows(gated, back_rows)
    g_gated = contract_cols(back_rows, out_back)
    g_scanned = g_gated * jax.nn.silu(gate_in)
    local_grad = start_weight(step_size, output_coeff, g_scanned, rates)
    returned = prefix(
        (through * keep_prev, local_grad * keep_prev),
        "shard",
        combine_maps,
        (jnp.ones_like(through), jnp.zeros_like(local_grad)),
        True,
    )
    end_grad = returned[1]
    (
        g_step,
        g_conv_scan,
        g_input_coeff,
        g_output_coeff,
        grad_a_log,
        grad_d_skip,
        g_gate_in,
        unused_grad,
    ) = scan_back((g_gated, end_grad))
    g_pre_step = g_step * jax.nn.sigmoid(step_pre)
    grad_dt_bias = jnp.sum(g_pre_step, axis=0)
    g_lin = g_pre_step.astype(jnp.bfloat16)
    grad_dt_proj = contract_rows(step_low, g_lin)
    g_step_low = contract_cols(g_lin, dtproj_back)
    g_projected = jnp.concatenate([g_step_low, g_input_coeff, g_output_coeff], axis=1).astype(
        jnp.bfloat16
    )
    grad_x_proj = contract_rows(conv_out, g_projected)
    g_conv_out = contract_cols(g_projected, xproj_back) + g_conv_scan
    g_edge, g_conv_in, grad_conv_weight, grad_conv_bias = conv_back(g_conv_out)
    from_next = shifted(g_edge.astype(jnp.bfloat16), "shard", -1).astype(g_edge.dtype)
    split_at = tok_rows - (kernel_taps - 1)
    g_conv_in = jnp.concatenate([g_conv_in[:split_at], g_conv_in[split_at:] + from_next], axis=0)
    g_mixed = jnp.concatenate([g_conv_in, g_gate_in], axis=1).astype(jnp.bfloat16)
    grad_in_proj = contract_rows(normed, g_mixed)
    g_normed = contract_cols(g_mixed, in_back)
    grad_norm_gain = jnp.sum(g_normed * input_f * scale, axis=0)
    g_hat = g_normed * gain_f[None, :]
    input_grad = (
        cot_f
        + scale * g_hat
        - input_f * (scale * scale * scale) * jnp.mean(g_hat * input_f, axis=1, keepdims=True)
    )
    shares = (
        lax.psum_scatter(
            grad_norm_gain.astype(jnp.bfloat16), "shard", scatter_dimension=0, tiled=True
        ).astype(jnp.float32),
        lax.psum_scatter(
            grad_in_proj.astype(jnp.bfloat16), "shard", scatter_dimension=0, tiled=True
        ).astype(jnp.float32),
        lax.psum_scatter(
            grad_conv_weight.astype(jnp.bfloat16), "shard", scatter_dimension=1, tiled=True
        ).astype(jnp.float32),
        lax.psum_scatter(
            grad_conv_bias.astype(jnp.bfloat16), "shard", scatter_dimension=0, tiled=True
        ).astype(jnp.float32),
        lax.psum_scatter(
            grad_x_proj.astype(jnp.bfloat16), "shard", scatter_dimension=0, tiled=True
        ).astype(jnp.float32),
        lax.psum_scatter(
            grad_dt_proj.astype(jnp.bfloat16), "shard", scatter_dimension=1, tiled=True
        ).astype(jnp.float32),
        lax.psum_scatter(
            grad_dt_bias.astype(jnp.bfloat16), "shard", scatter_dimension=0, tiled=True
        ).astype(jnp.float32),
        lax.psum_scatter(
            grad_a_log.astype(jnp.bfloat16), "shard", scatter_dimension=1, tiled=True
        ).astype(jnp.float32),
        lax.psum_scatter(
            grad_d_skip.astype(jnp.bfloat16), "shard", scatter_dimension=0, tiled=True
        ).astype(jnp.float32),
        lax.psum_scatter(
            grad_out_proj.astype(jnp.bfloat16), "shard", scatter_dimension=0, tiled=True
        ).astype(jnp.float32),
    )
    totals = (
        lax.psum(shares[0].astype(jnp.bfloat16), "rep").astype(jnp.float32),
        lax.psum(shares[1].astype(jnp.bfloat16), "rep").astype(jnp.float32),
        lax.psum(shares[2].astype(jnp.bfloat16), "rep").astype(jnp.float32),
        lax.psum(shares[3].astype(jnp.bfloat16), "rep").astype(jnp.float32),
        lax.psum(shares[4].astype(jnp.bfloat16), "rep").astype(jnp.float32),
        lax.psum(shares[5].astype(jnp.bfloat16), "rep").astype(jnp.float32),
        lax.psum(shares[6].astype(jnp.bfloat16), "rep").astype(jnp.float32),
        lax.psum(shares[7].astype(jnp.bfloat16), "rep").astype(jnp.float32),
        lax.psum(shares[8].astype(jnp.bfloat16), "rep").astype(jnp.float32),
        lax.psum(shares[9].astype(jnp.bfloat16), "rep").astype(jnp.float32),
    )
    return (
        activations,
        input_grad,
        totals[0],
        totals[1],
        totals[2],
        totals[3],
        totals[4],
        totals[5],
        totals[6],
        totals[7],
        totals[8],
        totals[9],
    )


def solution(mesh):
    in_specs = (
        P(("rep", "shard"), None),
        P(("rep", "shard"), None),
        P(),
        P(),
        P("shard"),
        P("shard", None),
        P(None, "shard"),
        P("shard"),
        P("shard", None),
        P(None, "shard"),
        P("shard"),
        P(None, "shard"),
        P("shard"),
        P("shard", None),
    )
    out_specs = (
        P(("rep", "shard"), None),
        P(("rep", "shard"), None),
        P("shard"),
        P("shard", None),
        P(None, "shard"),
        P("shard"),
        P("shard", None),
        P(None, "shard"),
        P("shard"),
        P(None, "shard"),
        P("shard"),
        P("shard", None),
    )
    return jax.shard_map(
        on_device, mesh=mesh, in_specs=in_specs, out_specs=out_specs, check_vma=False
    )
```

profile of v0, /device:TPU:0, one launch (start us, length us, event | category | flops | bytes accessed | tf_op | source)
XLA Modules:
  0.0 3641.3 jit_solution(2845981846549221471)
XLA Ops:
  10.8 62.7 %all-gather.4 = bf16[8,1,256]{2,1,0:T(2,128)(2,1)S(1)} all-gather(bf16[1,1,256]{2,1,0:T(2,128)(2,1)S(1)} %reshape.226), channel_id=1, replica_groups=mesh['rep'=4,'shard'=8] {'shard'}, dimensions={0}, use_global_device_ids=true | all-gather | bytes 4608 | tf_op jit(solution)/shard_map/all_gather | solution.py:188
  76.2 44.4 %all_gather.56 = bf16[4,4096]{1,0:T(4,128)(2,1)S(1)} all-gather(bf16[4,512]{1,0:T(4,128)(2,1)S(1)} %copy-done.41), channel_id=1, replica_groups=mesh['rep'=4,'shard'=8] {'shard'}, dimensions={1}, use_global_device_ids=true | all-gather | bytes 36864 | tf_op jit(solution)/shard_map/all_gather | solution.py:190
  120.7 43.0 %all-gather.3 = bf16[8,1,512]{2,1,0:T(2,128)(2,1)S(1)} all-gather(bf16[1,1,512]{2,1,0:T(2,128)(2,1)S(1)} %reshape.224), channel_id=1, replica_groups=mesh['rep'=4,'shard'=8] {'shard'}, dimensions={0}, use_global_device_ids=true | all-gather | bytes 9216 | tf_op jit(solution)/shard_map/all_gather | solution.py:191
  163.8 47.1 %all_gather.54 = bf16[16,4096]{1,0:T(8,128)(2,1)S(1)} all-gather(bf16[16,512]{1,0:T(8,128)(2,1)S(1)} %copy-done.28), channel_id=1, replica_groups=mesh['rep'=4,'shard'=8] {'shard'}, dimensions={1}, use_global_device_ids=true | all-gather | bytes 147456 | tf_op jit(solution)/shard_map/all_gather | solution.py:195
  210.9 41.2 %all-gather.5 = bf16[8,1,512]{2,1,0:T(2,128)(2,1)S(1)} all-gather(bf16[1,1,512]{2,1,0:T(2,128)(2,1)S(1)} %reshape.228), channel_id=1, replica_groups=mesh['rep'=4,'shard'=8] {'shard'}, dimensions={0}, use_global_device_ids=true | all-gather | bytes 9216 | tf_op jit(solution)/shard_map/all_gather | solution.py:194
  253.5 400.3 %all-gather.15.cloned.1.call-done = bf16[2048,8192]{1,0:T(8,128)(2,1)} async-done(((bf16[256,8192]{1,0:T(8,128)(2,1)}), bf16[2048,8192]{1,0:T(8,128)(2,1)}) %all-gather.15.cloned.1.call-update) | async-done | bytes 33554448 | tf_op jit(solution)/shard_map/all_gather | solution.py:189
  653.8 27.6 fusion.92
  692.0 191.7 %all-gather.21.cloned.1.call-done = bf16[4096,2048]{1,0:T(8,128)(2,1)} async-done(((bf16[512,2048]{1,0:T(8,128)(2,1)}), bf16[4096,2048]{1,0:T(8,128)(2,1)}) %all-gather.21.cloned.1.call-update) | async-done | bytes 16777232 | tf_op jit(solution)/shard_map/all_gather | solution.py:197
  883.8 32.5 multiply_reduce_fusion.6
  929.7 35.5 all-gather.19.cloned.1.call-done
  982.8 78.1 %while.94 = (s32[]{:T(128)}, f32[16,4096]{1,0:T(8,128)S(1)}, f32[16,32,4096]{2,1,0:T(8,128)}, f32[16,4096]{1,0:T(8,128)S(1)}, f32[16,32,4096]{2,1,0:T(8,128)}, /...) while((s32[]{:T(128)}, f32[16,4096]{1,0:T(8,128)S(1)}, ...), condition=%wide.region_6.7_spmd.clone, body=%wide.region_3.6_spmd.clone.sunk | while | flops 12910595 | bytes 7415935 | solution.py:99
  1063.1 60.4 %while.96 = (s32[]{:T(128)}, f32[16,4096]{1,0:T(8,128)S(1)}, f32[4096]{0:T(1024)S(1)}, f32[16,4096]{1,0:T(8,128)S(1)}, f32[16,32,4096]{2,1,0:T(8,128)}, /*index=...) while((s32[]{:T(128)}, f32[16,4096]{1,0:T(8,128)S(1)}, ...), condition=%wide.region_16.17_spmd.clone, body=%wide.region_13.16_spmd.clone.sunk | while | flops 12648451 | bytes 6613123 | solution.py:124
  1139.0 276.5 %while.93 = (s32[]{:T(128)}, f32[16,4096]{1,0:T(8,128)S(1)}, f32[16,32,4096]{2,1,0:T(8,128)}, f32[16,16,4096]{2,1,0:T(8,128)}, f32[1,16,4096]{2,1,0:T(8,128)S(1)...) while((s32[]{:T(128)}, f32[16,4096]{1,0:T(8,128)S(1)}, ...), condition=%wide.region_12.13_spmd, body=%wide.region_9.12_spmd.sunk | while | flops 109051904 | bytes 58212524 | solution.py:72
  1434.9 962.9 %while.98 = (s32[]{:T(128)}, f32[16,4096]{1,0:T(8,128)}, f32[16,4096]{1,0:T(8,128)S(1)}, f32[16,32,4096]{2,1,0:T(8,128)}, f32[16,32,4096]{2,1,0:T(8,128)}, /*ind...) while((s32[]{:T(128)}, f32[16,4096]{1,0:T(8,128)}, ...), condition=%wide.region_29.30_spmd.clone, body=%wide.region_19.29_spmd.clone.sunk | while | flops 243269120 | bytes 81833296 | solution.py:72
  1746.6 15.1 fusion.135
  2409.4 26.3 all-gather.6
  2473.6 33.0 multiply_reduce_fusion.9
  2525.4 24.6 convolution_convert_fusion
  2569.8 254.5 %reduce-scatter.17.cloned.1.call-done = bf16[512,2048]{1,0:T(8,128)(2,1)} async-done(((bf16[4096,2048]{1,0:T(8,128)(2,1)}), bf16[512,2048]{1,0:T(8,128)(2,1)}) %reduce-scatter.17.cloned.1.call-update) | async-done | bytes 2097168 | tf_op jit(solution)/shard_map/reduce_scatter | solution.py:345
  2824.3 541.7 %reduce-scatter.9.cloned.1.call-done = bf16[256,8192]{1,0:T(8,128)(2,1)} async-done(((bf16[2048,8192]{1,0:T(8,128)(2,1)}), bf16[256,8192]{1,0:T(8,128)(2,1)}) %reduce-scatter.9.cloned.1.call-update) | async-done | bytes 4194320 | tf_op jit(solution)/shard_map/reduce_scatter | solution.py:321
  3366.1 25.3 fusion.61
  3391.4 35.5 all-reduce.13
  3434.2 63.6 %reduce-scatter.15.cloned.1.call-done = bf16[16,512]{1,0:T(8,128)(2,1)} async-done(((bf16[16,4096]{1,0:T(8,128)(2,1)}), bf16[16,512]{1,0:T(8,128)(2,1)}) %reduce-scatter.15.cloned.1.call-update) | async-done | bytes 16400 | tf_op jit(solution)/shard_map/reduce_scatter | solution.py:339
  3512.2 111.5 %all-reduce.18.cloned.1.call-done = (bf16[256,8192]{1,0:T(8,128)(2,1)}, bf16[512,160]{0,1:T(8,128)(2,1)}, bf16[128,512]{1,0:T(8,128)(2,1)}, bf16[512,2048]{1,0:T(8,128)(2,1)}) async-done(((bf16[256,8192]{1,0:T(8,128)(2,1)}, bf16[512,160]{0,1:T(8,128)(2,1)}, bf16[128,512]{1,0:T(8,128)(2,1)}, bf16[512,2048]{1,0:T(8,128)(2,1)}), (bf16[256,8192]{1,0:T(8,128)(2,1)}, bf16[512,160]{0,1:T(8,128)(2,1)}, ...) | async-done | bytes 6586384 | tf_op jit(solution)/shard_map/psum | solution.py:351
  (1119 shorter events, 1583.3 us)
Async XLA Ops:
  7.2 646.6 %all-gather.15.cloned.1.call-start = ((), (), s32[]{:S(2)}) async-start(), calls=%async_computation.6 | async-start | bytes 37748736 | tf_op jit(solution)/shard_map/all_gather | solution.py:189
  8.0 875.8 %all-gather.21.cloned.1.call-start = ((), (), s32[]{:S(2)}) async-start(), calls=%async_computation.9 | async-start | bytes 18874368 | tf_op jit(solution)/shard_map/all_gather | solution.py:197
  8.7 916.8 %all-gather.17.cloned.1.call-start = ((), (), s32[]{:S(2)}) async-start(), calls=%async_computation.7 | async-start | bytes 1474560 | tf_op jit(solution)/shard_map/all_gather | solution.py:192
  9.5 955.8 %all-gather.19.cloned.1.call-start = ((), (), s32[]{:S(2)}) async-start(), calls=%async_computation.8 | async-start | bytes 1179648 | tf_op jit(solution)/shard_map/all_gather | solution.py:193
  10.0 1114.5 %all-gather.23.cloned.1.call-start = ((), (), s32[]{:S(2)}) async-start(), calls=%async_computation.15 | async-start | bytes 2359296 | tf_op jit(solution)/shard_map/all_gather | solution.py:23
  120.6 763.1 %copy-start.29 = (f32[1,4096]{1,0:T(1,128)}, f32[1,4096]{1,0:T(1,128)S(1)}, u32[]{:S(2)}) copy-start(f32[1,4096]{1,0:T(1,128)S(1)} %get-tuple-element.1079) | copy-start | bytes 49156
  120.6 763.1 %copy-start.31 = (f32[1,4096]{1,0:T(1,128)}, f32[1,4096]{1,0:T(1,128)S(1)}, u32[]{:S(2)}) copy-start(f32[1,4096]{1,0:T(1,128)S(1)} %get-tuple-element.1080) | copy-start | bytes 49156
  120.6 763.1 %copy-start.33 = (f32[1,4096]{1,0:T(1,128)}, f32[1,4096]{1,0:T(1,128)S(1)}, u32[]{:S(2)}) copy-start(f32[1,4096]{1,0:T(1,128)S(1)} %get-tuple-element.1081) | copy-start | bytes 49156
  120.6 763.1 %copy-start.35 = (f32[1,4096]{1,0:T(1,128)}, f32[1,4096]{1,0:T(1,128)S(1)}, u32[]{:S(2)}) copy-start(f32[1,4096]{1,0:T(1,128)S(1)} %get-tuple-element.1082) | copy-start | bytes 49156
  210.9 764.4 %copy-start.12 = (bf16[16,4096]{1,0:T(8,128)(2,1)}, bf16[16,4096]{1,0:T(8,128)(2,1)S(1)}, u32[]{:S(2)}) copy-start(bf16[16,4096]{1,0:T(8,128)(2,1)S(1)} %all_gather.54) | copy-start | bytes 393220
  252.1 713.1 %copy-start.23 = (f32[8,1,512]{2,1,0:T(1,128)}, f32[8,1,512]{2,1,0:T(1,128)S(1)}, u32[]{:S(2)}) copy-start(f32[8,1,512]{2,1,0:T(1,128)S(1)} %convert_element_type.194) | copy-start | bytes 49156
  253.5 630.3 %copy-start.42 = (f32[512]{0:T(512)}, f32[512]{0:T(512)S(1)}, u32[]{:S(2)}) copy-start(f32[512]{0:T(512)S(1)} %fusion.81) | copy-start | bytes 6148
  682.3 9.7 collective-permute-start
  976.1 148.4 %all-gather.25.cloned.1.call-start = ((), (), s32[]{:S(2)}) async-start(), calls=%async_computation.16 | async-start | bytes 2359296 | tf_op jit(solution)/shard_map/all_gather | solution.py:23
  1062.6 352.9 %all-gather.27.cloned.1.call-start = ((), (), s32[]{:S(2)}) async-start(), calls=%async_computation.17 | async-start | bytes 2359296 | tf_op jit(solution)/shard_map/all_gather | solution.py:23
  1124.4 1445.4 %reduce-scatter.13.cloned.1.call-start = ((), (), s32[]{:S(2)}) async-start(), calls=%async_computation.12 | async-start | bytes 1179648 | tf_op jit(solution)/shard_map/reduce_scatter | solution.py:333
  1434.9 963.0 %copy-start.24 = (f32[8,1,512]{2,1,0:T(1,128)S(1)}, f32[8,1,512]{2,1,0:T(1,128)}, u32[]{:S(2)}) copy-start(f32[8,1,512]{2,1,0:T(1,128)} %copy-done.23) | copy-start | bytes 49156
  2409.4 160.5 %reduce-scatter.11.cloned.1.call-start = ((), (), s32[]{:S(2)}) async-start(), calls=%async_computation.11 | async-start | bytes 1474560 | tf_op jit(solution)/shard_map/reduce_scatter | solution.py:330
  2443.9 380.4 %reduce-scatter.17.cloned.1.call-start = ((), (), s32[]{:S(2)}) async-start(), calls=%async_computation.14 | async-start | bytes 18874368 | tf_op jit(solution)/shard_map/reduce_scatter | solution.py:345
  2472.8 893.2 %reduce-scatter.9.cloned.1.call-start = ((), (), s32[]{:S(2)}) async-start(), calls=%async_computation.10 | async-start | bytes 37748736 | tf_op jit(solution)/shard_map/reduce_scatter | solution.py:321
  2507.7 15.0 collective-permute-start.1
  2550.1 883.1 %reduce-scatter.19.cloned.1.call-start = ((), (), s32[]{:S(2)}) async-start(), calls=%async_computation.18 | async-start | bytes 1179648
  2554.1 943.6 %reduce-scatter.15.cloned.1.call-start = ((), (), s32[]{:S(2)}) async-start(), calls=%async_computation.13 | async-start | bytes 147456 | tf_op jit(solution)/shard_map/reduce_scatter | solution.py:339
  2554.9 1068.8 %all-reduce.18.cloned.1.call-start = ((), (), s32[]{:S(2)}) async-start(), calls=%async_computation.19 | async-start | bytes 13172736 | tf_op jit(solution)/shard_map/psum | solution.py:351
  (118 other events, 3847.6 us)
Sparse Core Ops, SparseCore 0:
  9.6 644.1 all-gather.14
  655.9 227.7 all-gather.20
  885.8 39.7 all-gather.16
  927.5 37.7 all-gather.18
  976.2 48.0 all-gather.22
  1062.7 48.2 all-gather.24
  1124.6 48.2 all-gather.26
  2409.5 63.7 reduce-scatter.12
  2476.7 64.6 reduce-scatter.10
  2545.1 279.2 reduce-scatter.16
  2828.1 537.8 reduce-scatter.8
  3369.3 63.4 reduce-scatter.18
  3436.6 61.1 reduce-scatter.14
  3500.2 123.4 all-reduce.17
where the time goes:
time: 3660 us; the launch traced here: 3640 us
  waiting for transfers between devices  1610 us (44%)
  other arithmetic  890 us (24%)
  matrix products  522 us (14%)
  blocking collectives  311 us (8%)
  local copies, waits for them, and re-layouts  281 us (8%)
    reduce_scatter x1, waiting for transfers between devices, on_device(): lax.psum_scatter(grad_in_proj.astype(jnp.bfloat16), 'shard', scatter_dime...  542 us
    all_gather x1, waiting for transfers between devices, on_device(): lax.all_gather(in_proj, 'shard', axis=0, tiled=True)  400 us
    another operation x48, other arithmetic, selective_block_step(): summed = jnp.cumsum(jnp.exp(-exponent) * feeding, axis=0)  352 us
    dot_general x32, matrix products, selective_block_step(): emitted = jnp.einsum('qn,qne->qe', output_block, states, precision=HIGHEST)  327 us
    reduce_scatter x1, waiting for transfers between devices, on_device(): lax.psum_scatter(grad_out_proj.astype(jnp.bfloat16), 'shard', scatter_dim...  255 us
    reduce_sum x16, other arithmetic, selective_block_step(): exponent = rates[None, :, :] * running[:, None, :]  196 us
    all_gather x1, waiting for transfers between devices, on_device(): lax.all_gather(out_proj, 'shard', axis=0, tiled=True)  192 us
    psum x1, waiting for transfers between devices, on_device(): lax.psum(shares[1].astype(jnp.bfloat16), 'rep').astype(jnp.float32)  112 us
  transfers between devices with their start and end apart: 16, of which 8 were waited for; matrix products, arithmetic and copies ran while one was open for 17% of the time, Pallas kernels for 0%

commit v1 on v0

v1 whole, which is shorter than its diff:
```python
from functools import partial

import jax
import jax.numpy as jnp
from jax import lax
from jax.experimental import pallas as pl
from jax.experimental.pallas import tpu as pltpu
from jax.sharding import PartitionSpec as P

EPSILON = 1e-05
SPAN_TOKENS = 4096
F32=jnp.float32; BF16=jnp.bfloat16
LN=128
def pick(n, opts):
    for o in opts:
        if n % o == 0: return o
    return n

def first_kernel(U, dt_ref, x_ref, g_ref, b_ref, c_ref, a_ref, hend_ref, adj_ref, h_s, p_s, r_s, dtx_s):
    TC, EG = dt_ref.shape
    NT = EG//LN
    c = pl.program_id(2)
    @pl.when(c == 0)
    def _():
        h_s[...] = jnp.zeros_like(h_s); p_s[...] = jnp.ones_like(p_s); r_s[...] = jnp.zeros_like(r_s)
    dtx_s[...] = dt_ref[...]*x_ref[...].astype(F32)
    sl = [slice(j*LN,(j+1)*LN) for j in range(NT)]
    A = [a_ref[:, s] for s in sl]
    def body(i, carry):
        h, p, r = [list(v) for v in carry]
        rows = pl.ds(pl.multiple_of(i*U,U),U)
        dv, xv, gv = dt_ref.at[rows], dtx_s.at[rows], g_ref.at[rows]
        for k in range(U):
            t = i*U+k
            bt = b_ref[t]; ct = c_ref[t]
            for j in range(NT):
                d = dv[k:k+1, sl[j]]
                a = jnp.exp2(d*A[j])
                h[j] = a*h[j] + xv[k:k+1, sl[j]]*bt
                p[j] = p[j]*a
                r[j] = r[j] + p[j]*(ct*gv[k:k+1, sl[j]])
        return tuple(h), tuple(p), tuple(r)
    init = tuple(tuple(s_[:, s] for s in sl) for s_ in (h_s,p_s,r_s))
    h,p,r = lax.fori_loop(0, TC//U, body, init)
    for j in range(NT):
        h_s[:, sl[j]] = h[j]; p_s[:, sl[j]] = p[j]; r_s[:, sl[j]] = r[j]
    @pl.when(c == pl.num_programs(2)-1)
    def _():
        hend_ref[...] = h_s[...]; adj_ref[...] = r_s[...]

def first_pass(dt, x, g, bx, cx, a2, Q, TC=128, EG=512, U=8):
    T,E = dt.shape; N = a2.shape[0]; L=T//Q; NC=L//TC; NE=E//EG
    row = pl.BlockSpec((TC,EG), lambda q,e,c:(q*NC+c, e))
    sp = pl.BlockSpec((TC,N,LN), lambda q,e,c:(q*NC+c,0,0))
    st = pl.BlockSpec((None,N,EG), lambda q,e,c:(q,0,e))
    return pl.pallas_call(partial(first_kernel,U), grid=(Q,NE,NC),
        in_specs=[row,row,row,sp,sp,pl.BlockSpec((N,EG), lambda q,e,c:(0,e))],
        out_specs=[st,st],
        out_shape=[jax.ShapeDtypeStruct((Q,N,E),F32)]*2,
        scratch_shapes=[pltpu.VMEM((N,EG),F32)]*3+[pltpu.VMEM((TC,EG),F32)],
        compiler_params=pltpu.CompilerParams(dimension_semantics=("arbitrary",)*3, vmem_limit_bytes=60<<20),
        name="first_pass",
        cost_estimate=pl.CostEstimate(flops=9*T*E*N, bytes_accessed=10*T*E, transcendentals=T*E*N))(dt,x,g,bx,cx,a2)

def sums(tb):
    return (lax.broadcasted_iota(jnp.int32,(tb,tb*8),1)//8 == lax.broadcasted_iota(jnp.int32,(tb,tb*8),0)).astype(BF16)

def fwd_kernel(U, TB, dt_ref, x_ref, b_ref, c_ref, a_ref, h0_ref, y_ref, ck_ref, h_s, q_s, dtx_s):
    TC, EG = dt_ref.shape
    NT = EG//LN
    c = pl.program_id(2)
    @pl.when(c == 0)
    def _(): h_s[...] = h0_ref[...]
    ck_ref[...] = h_s[...]
    dtx_s[...] = dt_ref[...]*x_ref[...].astype(F32)
    sl = [slice(j*LN,(j+1)*LN) for j in range(NT)]
    A = [a_ref[:, s] for s in sl]
    S = sums(TB)
    def block(m, h):
        def body(i, carry):
            h = list(carry)
            rows = pl.ds(pl.multiple_of(m*TB+i*U,U),U)
            dv, xv = dt_ref.at[rows], dtx_s.at[rows]
            for k in range(U):
                t = m*TB+i*U+k
                bt = b_ref[t]; ct = c_ref[t]
                for j in range(NT):
                    a = jnp.exp2(dv[k:k+1, sl[j]]*A[j])
                    h[j] = a*h[j] + xv[k:k+1, sl[j]]*bt
                    q = h[j]*ct
                    q_s[pl.ds(pl.multiple_of((i*U+k)*8,8),8), sl[j]] = q[:8]+q[8:]
            return tuple(h)
        h = lax.fori_loop(0, TB//U, body, h)
        y_ref[pl.ds(pl.multiple_of(m*TB,TB),TB),:] = jnp.dot(S, q_s[...].astype(BF16), preferred_element_type=F32)
        return h
    h = lax.fori_loop(0, TC//TB, block, tuple(h_s[:, s] for s in sl))
    for j in range(NT): h_s[:, sl[j]] = h[j]

def fwd_pass(dt, x, bx, cx, a2, h0, Q, TC=64, EG=512, U=8, TB=32):
    T,E = dt.shape; N = a2.shape[0]; L=T//Q; NC=L//TC; NE=E//EG
    row = pl.BlockSpec((TC,EG), lambda q,e,c:(q*NC+c, e))
    sp = pl.BlockSpec((TC,N,LN), lambda q,e,c:(q*NC+c,0,0))
    return pl.pallas_call(partial(fwd_kernel,U,TB), grid=(Q,NE,NC),
        in_specs=[row,row,sp,sp,pl.BlockSpec((N,EG), lambda q,e,c:(0,e)), pl.BlockSpec((None,N,EG), lambda q,e,c:(q,0,e))],
        out_specs=[row, pl.BlockSpec((None,N,EG), lambda q,e,c:(q*NC+c,0,e))],
        out_shape=[jax.ShapeDtypeStruct((T,E),F32), jax.ShapeDtypeStruct((Q*NC,N,E),F32)],
        scratch_shapes=[pltpu.VMEM((N,EG),F32), pltpu.VMEM((TB*8,EG),F32), pltpu.VMEM((TC,EG),F32)],
        compiler_params=pltpu.CompilerParams(dimension_semantics=("arbitrary",)*3, vmem_limit_bytes=60<<20),
        name="fwd_pass",
        cost_estimate=pl.CostEstimate(flops=7*T*E*N, bytes_accessed=10*T*E, transcendentals=T*E*N))(dt,x,bx,cx,a2,h0)

def bwd_kernel(U, TB, dt_ref, x_ref, g_ref, b_ref, c_ref, a_ref, ck_ref, mu0_ref,
               gs_ref, gx_ref, gb_ref, gc_ref, ga_ref,
               mu_s, ga_s, qa_s, qb_s, lam_s, dtx_s, a_s, h_s):
    TC, EG = dt_ref.shape
    N = a_ref.shape[0]
    NT = EG//LN
    q_id = pl.program_id(0); c = pl.program_id(2)
    @pl.when(c == 0)
    def _():
        mu_s[...] = mu0_ref[...]
        ga_s[...] = jnp.zeros_like(ga_s)
    dtx_s[...] = dt_ref[...]*x_ref[...].astype(F32)
    sl = [slice(j*LN,(j+1)*LN) for j in range(NT)]
    A = [a_ref[:, s] for s in sl]
    h_s[0] = ck_ref[...]
    def up(i, carry):
        h = list(carry)
        rows = pl.ds(pl.multiple_of(i*U,U),U)
        dv, xv = dt_ref.at[rows], dtx_s.at[rows]
        for k in range(U):
            t = i*U+k
            bt = b_ref[t]
            for j in range(NT):
                a = jnp.exp2(dv[k:k+1, sl[j]]*A[j])
                h[j] = a*h[j] + xv[k:k+1, sl[j]]*bt
                a_s[t, :, sl[j]] = a
                h_s[t+1, :, sl[j]] = h[j]
        return tuple(h)
    lax.fori_loop(0, TC//U, up, tuple(ck_ref[:, s] for s in sl))
    S = sums(TB)
    tn_t = lax.broadcasted_iota(jnp.int32,(TB,TB*N),1)//N == lax.broadcasted_iota(jnp.int32,(TB,TB*N),0)
    sel = (lax.broadcasted_iota(jnp.int32,(TB*N,N),0)%N == lax.broadcasted_iota(jnp.int32,(TB*N,N),1)).astype(BF16)
    def block(mm, mu):
        m = TC//TB-1-mm
        def body(ii, carry):
            mu, ga = [list(v) for v in carry]
            i = TB//U-1-ii
            rows = pl.ds(pl.multiple_of(m*TB+i*U,U),U)
            dv, gv = dt_ref.at[rows], g_ref.at[rows]
            for kk in range(U):
                k = U-1-kk
                tl = i*U+k
                t = m*TB+tl
                bt = b_ref[t]; ct = c_ref[t]
                for j in range(NT):
                    lam = mu[j] + ct*gv[k:k+1, sl[j]]
                    mu[j] = a_s[t,:,sl[j]]*lam
                    w = mu[j]*h_s[t,:,sl[j]]
                    ga[j] = ga[j] + dv[k:k+1, sl[j]]*w
                    qa = A[j]*w
                    qb = lam*bt
                    r8 = pl.ds(pl.multiple_of(tl*8,8),8)
                    qa_s[r8, sl[j]] = qa[:8]+qa[8:]
                    qb_s[r8, sl[j]] = qb[:8]+qb[8:]
                    lam_s[pl.ds(pl.multiple_of(tl*N,8),N), sl[j]] = lam
            return tuple(mu), tuple(ga)
        ga = tuple(ga_s[:, s] for s in sl)
        mu, ga = lax.fori_loop(0, TB//U, body, (mu, ga))
        for j in range(NT): ga_s[:, sl[j]] = ga[j]
        rows = pl.ds(pl.multiple_of(m*TB,TB),TB)
        sa = jnp.dot(S, qa_s[...].astype(BF16), preferred_element_type=F32)
        sb = jnp.dot(S, qb_s[...].astype(BF16), preferred_element_type=F32)
        d = dt_ref[rows,:]; xx = x_ref[rows,:].astype(F32); dx = dtx_s[rows,:]
        gs_ref[rows,:] = sa*(1.0/LOG2E) + xx*sb
        gx_ref[rows,:] = d*sb
        hb = h_s[pl.ds(m*TB+1,TB)].reshape(TB*N,EG).astype(BF16)
        nt = (((1,),(1,)),((),()))
        zc = lax.dot_general(g_ref[rows,:].astype(BF16), hb, nt, preferred_element_type=F32)
        zb = lax.dot_general(dx.astype(BF16), lam_s[...].astype(BF16), nt, preferred_element_type=F32)
        def take(z):
            z = jnp.where(tn_t, z, 0.0)
            hi = z.astype(BF16); lo = (z-hi.astype(F32)).astype(BF16)
            return jnp.dot(hi, sel, preferred_element_type=F32)+jnp.dot(lo, sel, preferred_element_type=F32)
        gc_ref[rows,:] = take(zc)
        gb_ref[rows,:] = take(zb)
        return mu
    mu = lax.fori_loop(0, TC//TB, block, tuple(mu_s[:, s] for s in sl))
    for j in range(NT): mu_s[:, sl[j]] = mu[j]
    @pl.when(c == pl.num_programs(2)-1)
    def _(): ga_ref[...] = ga_s[...]

LOG2E=1.4426950408889634
def bwd_pass(dt, x, g, bx, cx, a2, ck, mu0, Q, TC=64, EG=512, U=8, TB=32):
    T,E = dt.shape; N = a2.shape[0]; L=T//Q; NC=L//TC; NE=E//EG
    CK = ck.shape[0]//(Q*NC)
    row = pl.BlockSpec((TC,EG), lambda q,e,c:(q*NC+NC-1-c, e))
    sp = pl.BlockSpec((TC,N,LN), lambda q,e,c:(q*NC+NC-1-c,0,0))
    st = pl.BlockSpec((None,N,EG), lambda q,e,c:(q,0,e))
    nb = pl.BlockSpec((None,TC,N), lambda q,e,c:(e,q*NC+NC-1-c,0))
    return pl.pallas_call(partial(bwd_kernel,U,TB), grid=(Q,NE,NC),
        in_specs=[row,row,row,sp,sp,pl.BlockSpec((N,EG), lambda q,e,c:(0,e)), pl.BlockSpec((None,N,EG), lambda q,e,c:(q*NC+NC-1-c,0,e)), st],
        out_specs=[row,row,nb,nb,st],
        out_shape=[jax.ShapeDtypeStruct((T,E),F32)]*2+[jax.ShapeDtypeStruct((NE,T,N),F32)]*2+[jax.ShapeDtypeStruct((Q,N,E),F32)],
        scratch_shapes=[pltpu.VMEM((N,EG),F32)]*2+[pltpu.VMEM((TB*8,EG),F32)]*2+[pltpu.VMEM((TB*N,EG),F32)]+[pltpu.VMEM((TC,EG),F32)]
           +[pltpu.VMEM((TC,N,EG),F32), pltpu.VMEM((TC+1,N,EG),F32)],
        compiler_params=pltpu.CompilerParams(dimension_semantics=("arbitrary",)*3, vmem_limit_bytes=62<<20),
        name="bwd_pass",
        cost_estimate=pl.CostEstimate(flops=20*T*E*N, bytes_accessed=22*T*E, transcendentals=T*E*N))(dt,x,g,bx,cx,a2,ck,mu0)


def conv_kernel(x_ref, edge_ref, w_ref, o_ref, x_s):
    L = x_ref.shape[0]
    taps = w_ref.shape[0] - 1
    x_s[0:8, :] = edge_ref[...]
    x_s[8:, :] = x_ref[...].astype(F32)
    pre = jnp.broadcast_to(w_ref[taps:taps + 1, :], x_ref.shape)
    for k in range(taps):
        at = 8 - (taps - 1) + k
        pre = pre + w_ref[k:k + 1, :] * x_s[at:at + L, :]
    o_ref[...] = (pre * jax.nn.sigmoid(pre)).astype(BF16)


def conv_pass(conv_in, edge, wb, Q, EB=256):
    T, E = conv_in.shape
    L = T // Q
    row = pl.BlockSpec((L, EB), lambda q, e: (q, e))
    return pl.pallas_call(
        conv_kernel,
        grid=(Q, E // EB),
        in_specs=[
            row,
            pl.BlockSpec((None, 8, EB), lambda q, e: (q, 0, e)),
            pl.BlockSpec((wb.shape[0], EB), lambda q, e: (0, e)),
        ],
        out_specs=row,
        out_shape=jax.ShapeDtypeStruct((T, E), BF16),
        scratch_shapes=[pltpu.VMEM((L + 8, EB), F32)],
        compiler_params=pltpu.CompilerParams(dimension_semantics=("arbitrary",) * 2),
        name="conv_pass",
        cost_estimate=pl.CostEstimate(flops=12 * T * E, bytes_accessed=4 * T * E, transcendentals=T * E),
    )(conv_in, edge, wb)


def conv_back_kernel(gp_ref, xp_ref, gx_ref, x_ref, edge_ref, w_ref, gi_ref, head_ref, tail_ref, gw_ref, x_s, g_s):
    L = x_ref.shape[0]
    taps = w_ref.shape[0] - 1
    x_s[0:8, :] = edge_ref[...]
    x_s[8:, :] = x_ref[...].astype(F32)
    at = [8 - (taps - 1) + k for k in range(taps)]
    pre = jnp.broadcast_to(w_ref[taps:taps + 1, :], x_ref.shape)
    for k in range(taps):
        pre = pre + w_ref[k:k + 1, :] * x_s[at[k]:at[k] + L, :]
    s = jax.nn.sigmoid(pre)
    g_out = contract_cols(gp_ref[...], xp_ref[...]) + gx_ref[...]
    g_pre = g_out * s * (1.0 + pre * (1.0 - s))
    g_s[0:L, :] = g_pre
    g_s[L:, :] = jnp.zeros((8, x_ref.shape[1]), F32)
    gw = [jnp.sum(g_pre * x_s[at[k]:at[k] + L, :], axis=0, keepdims=True) for k in range(taps)]
    gw.append(jnp.sum(g_pre, axis=0, keepdims=True))
    gw_ref[...] = jnp.concatenate(gw, axis=0)
    head_ref[...] = g_s[0:8, :]
    g_in = jnp.zeros(x_ref.shape, F32)
    for k in range(taps):
        g_in = g_in + w_ref[k:k + 1, :] * g_s[taps - 1 - k:taps - 1 - k + L, :]
    gi_ref[...] = g_in.astype(BF16)
    tail_ref[...] = g_in[L - 8:, :]


def conv_back(g_projected, x_proj, gx, conv_in, edge, wb, Q, EB=256):
    T, E = conv_in.shape
    L = T // Q
    row = pl.BlockSpec((L, EB), lambda q, e: (q, e))
    edges = pl.BlockSpec((None, 8, EB), lambda q, e: (q, 0, e))
    rows = wb.shape[0]
    return pl.pallas_call(
        conv_back_kernel,
        grid=(Q, E // EB),
        in_specs=[
            pl.BlockSpec((L, g_projected.shape[1]), lambda q, e: (q, 0)),
            pl.BlockSpec((EB, x_proj.shape[1]), lambda q, e: (e, 0)),
            row,
            row,
            edges,
            pl.BlockSpec((rows, EB), lambda q, e: (0, e)),
        ],
        out_specs=[row, edges, edges, pl.BlockSpec((None, rows, EB), lambda q, e: (q, 0, e))],
        out_shape=[
            jax.ShapeDtypeStruct((T, E), BF16),
            jax.ShapeDtypeStruct((Q, 8, E), F32),
            jax.ShapeDtypeStruct((Q, 8, E), F32),
            jax.ShapeDtypeStruct((Q, rows, E), F32),
        ],
        scratch_shapes=[pltpu.VMEM((L + 8, EB), F32)] * 2,
        compiler_params=pltpu.CompilerParams(dimension_semantics=("arbitrary",) * 2),
        name="conv_back",
        cost_estimate=pl.CostEstimate(flops=400 * T * E, bytes_accessed=10 * T * E, transcendentals=T * E),
    )(g_projected, x_proj, gx, conv_in, edge, wb)


def contract_rows(left, right):
    return lax.dot_general(left, right, (((0,), (0,)), ((), ())), preferred_element_type=F32)


def contract_cols(left, right):
    return lax.dot_general(left, right, (((1,), (1,)), ((), ())), preferred_element_type=F32)


def swap(value, flip):
    return lax.ppermute(value, "rep", [(i, i ^ flip) for i in range(lax.axis_size("rep"))])


def shifted(value, steps):
    count = lax.axis_size("shard")
    first, last = (max(0, -steps), min(count, count - steps))
    return lax.ppermute(value, "shard", [(i, i + steps) for i in range(first, last)])


def rep_gather(value):
    far = swap(value, 2)
    return [value, swap(value, 1), far, swap(far, 1)]


def rep_scatter(parts):
    low = [part.astype(BF16) for part in parts]
    near = swap(jnp.stack([low[1], low[3]]), 1).astype(F32)
    mine, other = (parts[0] + near[0], parts[2] + near[1])
    return mine + swap(other.astype(BF16), 2).astype(F32)


def rep_sum(parts):
    near = swap(jnp.stack([parts[1], parts[3]]), 1)
    pair = jnp.stack([parts[0] + near[0], parts[2] + near[1]])
    far = swap(pair, 2)
    full = jnp.stack([pair[0] + far[1], pair[1] + far[0]])
    over = swap(full, 1)
    return [full[0], over[0], full[1], over[1]]


def carry_in(total, state, rates, place, reverse):
    sign = -1 if reverse else 1
    span = lax.axis_size("shard")
    total, state = (shifted(total, sign), shifted(state, sign))
    known = jnp.where(place >= 1, 1.0, 0.0)
    total, state = (total * known, state * known)
    step = 1
    while step < min(span, 8):
        far_total, far_state = (shifted(total, sign * step), shifted(state, sign * step))
        known = jnp.where(place >= step, 1.0, 0.0)
        state = state + jnp.exp(rates[None] * total[:, None, :]) * (far_state * known)
        total = total + far_total * known
        step *= 2
    return state


def on_device(
    block_input,
    cotangent,
    seq_lengths,
    slot_order,
    norm_gain,
    in_proj,
    conv_weight,
    conv_bias,
    x_proj,
    dt_proj,
    dt_bias,
    a_log,
    d_skip,
    out_proj,
):
    n_shard, n_rep = (lax.axis_size("shard"), lax.axis_size("rep"))
    shard_at, rep_at = (lax.axis_index("shard"), lax.axis_index("rep"))
    rows, width = block_input.shape
    tokens = n_rep * rows
    taps, wide = conv_weight.shape
    part = wide // n_rep
    chans = part * n_shard
    rank = dt_proj.shape[0]
    states = a_log.shape[0]
    span = max(1, min(n_shard, SPAN_TOKENS // rows))
    in_slot = shard_at % span
    keep_prev = (in_slot != 0).astype(F32)
    keep_next = (in_slot != span - 1).astype(F32)
    places = in_slot * rows + jnp.arange(rows, dtype=jnp.int32)

    def valid_of(flip):
        slot_at = ((rep_at ^ flip) * n_shard + shard_at) // span
        slot_len = jnp.sum(jnp.where(slot_order == slot_at, seq_lengths, 0))
        return (places < slot_len).astype(F32)[:, None]

    valid = [valid_of(k) for k in range(n_rep)]

    def mine(value, axis):
        return lax.dynamic_slice_in_dim(value, rep_at * part, part, axis)

    x_all = rep_gather(block_input)
    small = jnp.concatenate(
        [
            mine(x_proj, 0),
            mine(dt_proj, 1).T,
            mine(a_log, 1).T,
            mine(conv_weight, 1).T,
            mine(conv_bias, 0)[:, None],
            mine(dt_bias, 0)[:, None],
            mine(d_skip, 0)[:, None],
            norm_gain.reshape(part, -1),
        ],
        axis=1,
    )
    in_mine = lax.dynamic_index_in_dim(
        in_proj.reshape(in_proj.shape[0], 2, n_shard, n_rep, part), rep_at, 3, keepdims=False
    ).reshape(in_proj.shape[0], 2 * chans)
    small_all = lax.all_gather(small, "shard", axis=0, tiled=True)
    in_all = lax.all_gather(in_mine, "shard", axis=0, tiled=True)
    out_all = lax.all_gather(mine(out_proj, 0), "shard", axis=0, tiled=True)
    cot_all = rep_gather(cotangent)

    cut = [x_proj.shape[1], rank, states, taps, 1, 1, 1]
    ends = [sum(cut[:i + 1]) for i in range(len(cut))]
    xproj_all = small_all[:, :ends[0]]
    dtproj_all = small_all[:, ends[0]:ends[1]].T
    log_rates = small_all[:, ends[1]:ends[2]].T.astype(F32)
    wb = small_all[:, ends[2]:ends[4]].T.astype(F32)
    dtbias_all = small_all[:, ends[4]].astype(F32)
    skip_all = small_all[:, ends[5]].astype(F32)
    gain_f = small_all[:, ends[6]:].reshape(width).astype(F32)

    def norm(value):
        value = value.astype(F32)
        scale = lax.rsqrt(jnp.mean(value * value, axis=1, keepdims=True) + EPSILON)
        return (value * scale * gain_f[None, :]).astype(BF16)

    normed = jnp.concatenate([norm(value) for value in x_all], axis=0)
    conv_in = jnp.dot(normed, in_all[:, :chans], preferred_element_type=F32).astype(BF16)
    gate_in = jnp.dot(normed, in_all[:, chans:], preferred_element_type=F32)
    last = conv_in.reshape(n_rep, rows, chans)[:, rows - (taps - 1):]
    edge = shifted(last, 1).astype(F32) * keep_prev
    edge = jnp.concatenate([jnp.zeros((n_rep, 8 - (taps - 1), chans), F32), edge], axis=1)
    conv_out = conv_pass(conv_in, edge, wb, n_rep)
    proj = lax.dot_general(xproj_all, conv_out, (((0,), (1,)), ((), ())), preferred_element_type=F32)
    proj = jnp.concatenate(
        rep_sum([proj[:, k * rows:(k + 1) * rows] for k in range(n_rep)]), axis=1
    )
    step_low = proj[:rank].astype(BF16)
    b_all = jnp.broadcast_to(proj[rank:rank + states].T[:, :, None], (tokens, states, LN))
    c_all = jnp.broadcast_to(proj[rank + states:].T[:, :, None], (tokens, states, LN))
    step_pre = contract_rows(step_low, dtproj_all) + dtbias_all[None, :]
    step = jax.nn.softplus(step_pre)
    rates = -jnp.exp(log_rates)
    rates2 = rates * LOG2E
    back = jnp.concatenate(
        [(cot_all[k].astype(F32) * valid[k]).astype(BF16) for k in range(n_rep)], axis=0
    )
    sig = jax.nn.sigmoid(gate_in)
    g_gated = contract_cols(back, out_all)
    g_scanned = g_gated * (gate_in * sig)
    local_end, local_adj = first_pass(step, conv_out, g_scanned, b_all, c_all, rates2, n_rep)
    total = jnp.sum(step.reshape(n_rep, rows, chans), axis=1)
    start_state = carry_in(total, local_end, rates, in_slot, False)
    end_grad = carry_in(total, local_adj, rates, span - 1 - in_slot, True)
    scanned, kept = fwd_pass(step, conv_out, b_all, c_all, rates2, start_state, n_rep)
    scanned = scanned + skip_all[None, :] * conv_out.astype(F32)
    gated = (scanned * (gate_in * sig)).astype(BF16)
    g_gate = (g_gated * scanned * sig * (1.0 + gate_in * (1.0 - sig))).astype(BF16)
    branch = jnp.dot(gated, out_all, preferred_element_type=F32)
    branch = rep_scatter([branch[k * rows:(k + 1) * rows] for k in range(n_rep)])
    input_f = block_input.astype(F32)
    activations = (input_f + valid[0] * branch).astype(BF16)

    def scatter(value):
        return lax.psum_scatter(value.astype(BF16), "shard", scatter_dimension=0, tiled=True)

    grad_out = scatter(contract_rows(gated, back))
    grad_gate = scatter(contract_rows(normed, g_gate))
    g_step, g_scan_in, g_b, g_c, g_a = bwd_pass(
        step, conv_out, g_scanned, b_all, c_all, rates2, kept, end_grad, n_rep
    )
    g_pre_step = g_step * jax.nn.sigmoid(step_pre)
    grad_dt_bias = jnp.sum(g_pre_step, axis=0)
    g_lin = g_pre_step.astype(BF16)
    grad_dt_proj = contract_rows(g_lin, step_low.T)
    g_low = contract_cols(dtproj_all, g_lin)
    g_proj = jnp.concatenate([g_low, jnp.sum(g_b, axis=0).T, jnp.sum(g_c, axis=0).T], axis=0)
    g_proj = jnp.concatenate(
        rep_sum([g_proj[:, k * rows:(k + 1) * rows] for k in range(n_rep)]), axis=1
    )
    g_proj = g_proj.T.astype(BF16)
    grad_x_proj = contract_rows(conv_out, g_proj)
    conv_f = conv_out.astype(F32)
    g_scan_in = g_scan_in + skip_all[None, :] * g_scanned
    grad_skip = jnp.sum(g_scanned * conv_f, axis=0)
    g_in, head, tail, grad_wb = conv_back(g_proj, xproj_all, g_scan_in, conv_in, edge, wb, n_rep)
    after = shifted(head, -1) * keep_next
    joined = jnp.concatenate([jnp.zeros_like(after), after], axis=1)
    fix = tail
    for k in range(taps - 1):
        at = taps - 1 - k
        fix = fix + wb[k][None, None, :] * joined[:, at:at + 8]
    g_in = g_in.reshape(n_rep, rows, chans).at[:, rows - 8:].set(fix.astype(BF16))
    g_in = g_in.reshape(tokens, chans)
    grad_conv = scatter(contract_rows(normed, g_in))
    g_normed = contract_cols(g_in, in_all[:, :chans]) + contract_cols(g_gate, in_all[:, chans:])
    g_normed = rep_scatter([g_normed[k * rows:(k + 1) * rows] for k in range(n_rep)])
    scale = lax.rsqrt(jnp.mean(input_f * input_f, axis=1, keepdims=True) + EPSILON)
    grad_gain = jnp.sum(g_normed * input_f * scale, axis=0)
    g_hat = g_normed * gain_f[None, :]
    input_grad = (
        cotangent.astype(F32)
        + scale * g_hat
        - input_f * (scale * scale * scale) * jnp.mean(g_hat * input_f, axis=1, keepdims=True)
    )
    grad_a_log = rates * jnp.sum(g_a, axis=0)
    grad_small = scatter(
        jnp.concatenate(
            [
                grad_x_proj,
                grad_dt_proj,
                grad_a_log.T,
                jnp.sum(grad_wb, axis=0).T,
                grad_dt_bias[:, None],
                grad_skip[:, None],
                grad_gain.reshape(chans, -1),
            ],
            axis=1,
        )
    )

    def everyone(value):
        return lax.all_gather(value, "rep", axis=0)

    all_out = everyone(grad_out).reshape(wide, width).astype(F32)
    all_in = jnp.stack([everyone(grad_conv), everyone(grad_gate)], axis=0)
    all_in = all_in.reshape(2, n_rep, -1, n_shard, part).transpose(2, 0, 3, 1, 4)
    all_in = all_in.reshape(in_proj.shape).astype(F32)
    all_small = everyone(grad_small).astype(F32)
    all_gain = jnp.sum(all_small[:, :, ends[6]:], axis=0).reshape(norm_gain.shape)
    all_small = all_small.reshape(wide, -1)
    return (
        activations,
        input_grad,
        all_gain,
        all_in,
        all_small[:, ends[2]:ends[3]].T,
        all_small[:, ends[3]],
        all_small[:, :ends[0]],
        all_small[:, ends[0]:ends[1]].T,
        all_small[:, ends[4]],
        all_small[:, ends[1]:ends[2]].T,
        all_small[:, ends[5]],
        all_out,
    )


def solution(mesh):
    tokens = P(("rep", "shard"), None)
    rows, cols, line, full = (P("shard", None), P(None, "shard"), P("shard"), P())
    return jax.shard_map(
        on_device,
        mesh=mesh,
        in_specs=(tokens, tokens, full, full, line, rows, cols, line, rows, cols, line, cols, line, rows),
        out_specs=(tokens, tokens, line, rows, cols, line, rows, cols, line, cols, line, rows),
        check_vma=False,
    )
```

time: 3660 us -> 1150 us (0.31)
  waiting for transfers between devices: 1610 us -> 280 us
  other arithmetic: 890 us -> 130 us
  matrix products: 522 us -> 165 us
  Pallas kernels: 0 us -> 347 us
  blocking collectives: 311 us -> 44.6 us
  local copies, waits for them, and re-layouts: 281 us -> 97.1 us
  starting transfers between devices: 5.44 us -> 54.2 us
    reduce_scatter x5 -> x3, waiting for transfers between devices: 860 us -> 0.01 us  [scatter(): lax.psum_scatter(value.astype(BF16), 'shard', scatter_dimension=0, tiled=...]
    all_gather x7 -> x5, waiting for transfers between devices: 637 us -> 91.6 us  [the longest x3 53.6 us: everyone(): return lax.all_gather(value, 'rep', axis=0)]
    another operation x130 -> x13, other arithmetic: 451 us -> 12.9 us  [the longest x2 5.38 us: rep_scatter(): near = swap(jnp.stack([low[1], low[3]]), 1).astype(F32)]
    pallas_call x0 -> x5, Pallas kernels: none -> 347 us  [the longest x1 181 us: bwd_pass(): pl.pallas_call(partial(bwd_kernel, U, TB), grid=(Q, NE, NC), in_specs=[ro...]
    dot_general x36 -> x4, matrix products: 384 us -> 49.4 us  [the longest x1 15.9 us: on_device(): gate_in = jnp.dot(normed, in_all[:, chans:], preferred_element_type=F32)]
    reduce_sum x50 -> x11, other arithmetic: 255 us -> 18.4 us  [the longest x4 6.75 us: norm(): scale = lax.rsqrt(jnp.mean(value * value, axis=1, keepdims=True) + EPSILON)]
    all_gather x6 -> x2, blocking collectives: 265 us -> 44.6 us  [the longest x1 38.4 us: on_device(): small_all = lax.all_gather(small, 'shard', axis=0, tiled=True)]
    ppermute x2 -> x32, waiting for transfers between devices: 0.01 us -> 182 us  [the longest x16 153 us: swap(): lax.ppermute(value, 'rep', [(i, i ^ flip) for i in range(lax.axis_size('r...]
  transfers between devices with their start and end apart: 16 -> 41, of which waited for: 8 -> 20; matrix products, arithmetic and copies ran while one was open for 17% -> 25% of each run, Pallas kernels for 0% -> 3%
where the time goes in v1:
time: 1150 us; the launch traced here: 1130 us
  Pallas kernels  347 us (30%)
  waiting for transfers between devices  280 us (24%)
  matrix products  165 us (14%)
  other arithmetic  130 us (11%)
  local copies, waits for them, and re-layouts  97.1 us (8%)
  starting transfers between devices  54.2 us (5%)
  blocking collectives  44.6 us (4%)
  between operations  15.5 us (1%)
    pallas_call x1, Pallas kernels, bwd_pass(): pl.pallas_call(partial(bwd_kernel, U, TB), grid=(Q, NE, NC), in_specs=[ro...  181 us
    ppermute x16, waiting for transfers between devices, swap(): lax.ppermute(value, 'rep', [(i, i ^ flip) for i in range(lax.axis_size('r...  153 us
    pallas_call x1, Pallas kernels, fwd_pass(): pl.pallas_call(partial(fwd_kernel, U, TB), grid=(Q, NE, NC), in_specs=[ro...  74.1 us
    dot_general x4, matrix products, contract_cols(): lax.dot_general(left, right, (((1,), (1,)), ((), ())), preferred_element_...  60.2 us
    dot_general x6, matrix products, contract_rows(): lax.dot_general(left, right, (((0,), (0,)), ((), ())), preferred_element_...  55.6 us
    all_gather x3, waiting for transfers between devices, everyone(): return lax.all_gather(value, 'rep', axis=0)  53.6 us
    pallas_call x1, Pallas kernels, first_pass(): pl.pallas_call(partial(first_kernel, U), grid=(Q, NE, NC), in_specs=[row,...  53 us
    ppermute x16, starting transfers between devices, shifted(): lax.ppermute(value, 'shard', [(i, i + steps) for i in range(first, last)])  44.2 us
  transfers between devices with their start and end apart: 41, of which 20 were waited for; matrix products, arithmetic and copies ran while one was open for 25% of the time, Pallas kernels for 3%

profile of v1, /device:TPU:0, one launch (start us, length us, event | category | flops | bytes accessed | tf_op | source)
XLA Modules:
  0.0 1134.2 jit_solution(15901268347279303694)
XLA Ops:
  25.2 38.4 %all_gather.33 = bf16[1024,313]{0,1:T(8,128)(2,1)S(1)} all-gather(bf16[128,313]{0,1:T(8,128)(2,1)S(1)} %concatenate.32), channel_id=1, replica_groups=mesh['rep'=4,'shard'=8] {'shard'}, dimensions={0}, use_global_device_ids=true | all-gather | bytes 721152 | tf_op jit(solution)/shard_map/all_gather | solution.py:414
  73.6 36.4 %collective-permute-done.8 = bf16[512,2048]{1,0:T(8,128)(2,1)} collective-permute-done((bf16[512,2048]{1,0:T(8,128)(2,1)}, bf16[512,2048]{1,0:T(8,128)(2,1)}, u32[]{:S(2)}, u32[]{:S(2)}) %collective-permute-start.8) | collective-permute-done | bytes 2097184 | tf_op jit(solution)/shard_map/ppermute | solution.py:310
  122.3 32.9 %all-gather.10.cloned.1.call-done = bf16[2048,2048]{0,1:T(8,128)(2,1)} async-done(((bf16[256,2048]{0,1:T(8,128)(2,1)}), bf16[2048,2048]{0,1:T(8,128)(2,1)}) %all-gather.10.cloned.1.call-update) | async-done | bytes 8388624 | tf_op jit(solution)/shard_map/all_gather | solution.py:415
  155.1 14.6 %convolution_convert_fusion.1.x_ref = bf16[2048,1024]{1,0:T(8,128)(2,1)S(1)} fusion(bf16[2048,2048]{0,1:T(8,128)(2,1)} %all-gather.10.cloned.1.call-done, bf16[512,2048]{1,0:T(8,128)(2,1)} %get-tuple-element.110, bf16[512,2048]{1,0:T(8,128)(2,1)} %get-tuple-element.109, bf16[512,2048]{1,0:T(8,128)(2,1)} %get-tuple-element.108, ...), kind=kOutput, calls=%fused_computation.68 | convolution fusion | flops 8625586176 | bytes 16777216 | tf_op jit(solution)/shard_map/dot_general | solution.py:435
  179.6 14.5 %conv_pass.1.x_ref = bf16[2048,1024]{1,0:T(8,128)(2,1)} custom-call(bf16[2048,1024]{1,0:T(8,128)(2,1)} %copy-done.7, f32[4,8,1024]{2,1,0:T(8,128)} %concatenate.34.edge_ref, f32[5,1024]{1,0:T(8,128)} %convert_bitcast_fusion.1.w_ref), custom_call_target="tpu_custom_call" | custom-call | flops 25165824 | bytes 8388608 | tf_op jit(solution)/shard_map/conv_pass/pallas_call | solution.py:228
  207.3 15.9 %fusion.32 = f32[2048,1024]{1,0:T(8,128)} fusion(bf16[2048,2048]{0,1:T(8,128)(2,1)} %all-gather.10.cloned.1.call-done, bf16[512,2048]{1,0:T(8,128)(2,1)} %get-tuple-element.110, bf16[512,2048]{1,0:T(8,128)(2,1)} %get-tuple-element.109, bf16[512,2048]{1,0:T(8,128)(2,1)} %get-tuple-element.108, bf16[512,2048]{1,0:T(8,128)(2,1)S(1)} %copy-done.13), kind=kOutput, calls=%fused_computation.72 | convolution fusion | flops 8623489024 | bytes 20971520 | tf_op jit(solution)/shard_map/dot_general | solution.py:436
  229.0 21.9 %fusion.1 = (bf16[1024]{0:T(1024)(128)(2,1)}, f32[2048,1024]{1,0:T(8,128)}, f32[2048,1024]{1,0:T(8,128)}) fusion(bf16[2048,1024]{1,0:T(8,128)(2,1)} %conv_pass.1.x_ref, f32[2048,1024]{1,0:T(8,128)} %fusion.32, bf16[1024,2048]{1,0:T(8,128)(2,1)} %all-gather.12.cloned.1.call-done, bf16[512,2048]{1,0:T(8,128)(2,1)} %multiply_convert_fusion.2, ...), kind=kOutput, calls=%fused_computation.10 | convolution fusion | flops 8640265216 | bytes 41945088 | tf_op jit(solution)/shard_map/dot_general | solution.py:306
  280.1 53.0 %first_pass.1 = (f32[4,16,1024]{2,1,0:T(8,128)}, f32[4,16,1024]{2,1,0:T(8,128)}) custom-call(f32[2048,1024]{1,0:T(8,128)} %get-tuple-element.62.dt_ref, bf16[2048,1024]{1,0:T(8,128)(2,1)} %conv_pass.1.x_ref, f32[2048,1024]{1,0:T(8,128)} %get-tuple-element.57.g_ref, f32[2048,16,128]{2,1,0:T(8,128)} %broadcast_in_dim.27.b_ref, ...), custom_call_target="tpu_custom_call" | custom-call | flops 301989888 | bytes 20971520 | tf_op jit(solution)/shard_map/first_pass/pallas_call | solution.py:56
  396.4 74.1 %fwd_pass.1 = (f32[2048,1024]{1,0:T(8,128)}, f32[32,16,1024]{2,1,0:T(8,128)}) custom-call(f32[2048,1024]{1,0:T(8,128)} %get-tuple-element.62.dt_ref, bf16[2048,1024]{1,0:T(8,128)(2,1)} %conv_pass.1.x_ref, f32[2048,16,128]{2,1,0:T(8,128)} %broadcast_in_dim.27.b_ref, f32[2048,16,128]{2,1,0:T(8,128)} %broadcast_in_dim.28.c_ref, ...), custom_call_target="tpu_custom_call" | custom-call | flops 234881024 | bytes 20971520 | tf_op jit(solution)/shard_map/fwd_pass/pallas_call | solution.py:103
  470.5 180.9 %bwd_pass.1 = (f32[2048,1024]{1,0:T(8,128)}, f32[2048,1024]{1,0:T(8,128)}, f32[2,2048,16]{2,1,0:T(8,128)}, f32[2,2048,16]{2,1,0:T(8,128)}, f32[4,16,1024]{2,1,0:T(8,128)}) custom-call(f32[2048,1024]{1,0:T(8,128)} %get-tuple-element.62.dt_ref, bf16[2048,1024]{1,0:T(8,128)(2,1)} %conv_pass.1.x_ref, f32[2048,1024]{1,0:T(8,128)} %get-tuple-element.57.g_ref, ...), custom_call_target="tpu_custom_call" | custom-call | flops 671088640 | bytes 46137344 | tf_op jit(solution)/shard_map/bwd_pass/pallas_call | solution.py:201
  651.5 21.8 %multiply_convert_fusion = (bf16[2048,1024]{1,0:T(8,128)(2,1)S(1)}, bf16[2048,1024]{1,0:T(8,128)(2,1)}, f32[2048,1024]{1,0:T(8,128)}) fusion(f32[2048,1024]{1,0:T(8,128)} %fusion.32, f32[2048,1024]{1,0:T(8,128)} %get-tuple-element.115, f32[2048,1024]{1,0:T(8,128)} %get-tuple-element.38, bf16[2048,1024]{1,0:T(8,128)(2,1)} %conv_pass.1.x_ref, ...), kind=kLoop, calls=%fused_computation.15 | loop fusion | flops 37748736 | bytes 62918656 | tf_op jit(solution)/shard_map/convert_element_type | solution.py:465
  687.4 13.8 %convolution_convert_fusion = bf16[1024,2048]{1,0:T(8,128)(2,1)} fusion(bf16[2048,1024]{1,0:T(8,128)(2,1)} %get-tuple-element.64, bf16[512,2048]{1,0:T(8,128)(2,1)} %multiply_convert_fusion.2, bf16[512,2048]{1,0:T(8,128)(2,1)} %multiply_convert_fusion.3, bf16[512,2048]{1,0:T(8,128)(2,1)} %multiply_convert_fusion.4, bf16[512,2048]{1,0:T(8,128)(2,1)S(1)} %copy-done.20), kind=kOutput, calls=%fused_computation.67 | convolution fusion | flops 8625586176 | bytes 16777216 | tf_op jit(solution)/shard_map/dot_general | solution.py:302
  730.3 15.5 %collective-permute-done.27 = f32[2,160,512]{2,1,0:T(8,128)S(1)} collective-permute-done((f32[2,160,512]{2,1,0:T(8,128)}, f32[2,160,512]{2,1,0:T(8,128)S(1)}, u32[]{:S(2)}, u32[]{:S(2)}) %collective-permute-start.27) | collective-permute-done | bytes 655392 | tf_op jit(solution)/shard_map/ppermute | solution.py:310
  764.3 24.4 %conv_back.1 = (bf16[2048,1024]{1,0:T(8,128)(2,1)}, f32[4,8,1024]{2,1,0:T(8,128)}, f32[4,8,1024]{2,1,0:T(8,128)}, f32[4,5,1024]{2,1,0:T(8,128)}) custom-call(bf16[2048,160]{1,0:T(8,128)(2,1)} %fusion.57.gp_ref, bf16[1024,160]{1,0:T(8,128)(2,1)} %copy.62.xp_ref, f32[2048,1024]{1,0:T(8,128)} %get-tuple-element.111.gx_ref, bf16[2048,1024]{1,0:T(8,128)(2,1)} %copy-done.7, ...), custom_call_target="tpu_custom_call" | custom-call | flops 838860800 | bytes 20971520 | tf_op jit(solution)/shard_map/conv_back/pallas_call | solution.py:276
  798.7 13.8 %convolution_convert_fusion.3 = bf16[2048,1024]{1,0:T(8,128)(2,1)} fusion(bf16[2048,1024]{1,0:T(8,128)(2,1)} %bitcast.218, bf16[512,2048]{1,0:T(8,128)(2,1)} %get-tuple-element.110, bf16[512,2048]{1,0:T(8,128)(2,1)} %get-tuple-element.109, bf16[512,2048]{1,0:T(8,128)(2,1)} %get-tuple-element.108, bf16[512,2048]{1,0:T(8,128)(2,1)S(1)} %copy-done.15), kind=kOutput, calls=%fused_computation.70 | convolution fusion | flops 8625586176 | bytes 16777216 | tf_op jit(solution)/shard_map/dot_general | solution.py:302
  812.5 15.3 %fusion.34 = f32[2048,2048]{1,0:T(8,128)} fusion(bf16[2048,1024]{1,0:T(8,128)(2,1)} %bitcast.219, bf16[2048,2048]{0,1:T(8,128)(2,1)} %all-gather.10.cloned.1.call-done), kind=kOutput, calls=%fused_computation.74 | convolution fusion | flops 8589934592 | bytes 25165824 | tf_op jit(solution)/shard_map/dot_general | solution.py:306
  827.9 19.3 %fusion.97 = (bf16[2048,2048]{1,0:T(8,128)(2,1)}, f32[2048,2048]{1,0:T(8,128)}) fusion(f32[2048,2048]{1,0:T(8,128)} %fusion.34, bf16[2048,1024]{1,0:T(8,128)(2,1)} %copy-done.9, bf16[2048,2048]{0,1:T(8,128)(2,1)} %all-gather.10.cloned.1.call-done), kind=kOutput, calls=%fused_computation.217 | convolution fusion | flops 8598323200 | bytes 50331648 | tf_op jit(solution)/shard_map/dot_general | solution.py:306
  876.8 37.0 %collective-permute-done.31 = bf16[512,2048]{1,0:T(8,128)(2,1)} collective-permute-done((bf16[512,2048]{1,0:T(8,128)(2,1)}, bf16[512,2048]{1,0:T(8,128)(2,1)}, u32[]{:S(2)}, u32[]{:S(2)}) %collective-permute-start.31) | collective-permute-done | bytes 2097184 | tf_op jit(solution)/shard_map/ppermute | solution.py:310
  921.8 15.2 %fusion.98 = (bf16[2048,2048]{1,0:T(8,128)(2,1)S(1)}, f32[2048,2048]{1,0:T(8,128)}) fusion(bf16[2048,1024]{1,0:T(8,128)(2,1)} %get-tuple-element.64, bf16[1024,2048]{1,0:T(8,128)(2,1)} %all-gather.12.cloned.1.call-done), kind=kOutput, calls=%fused_computation.218 | convolution fusion | flops 8594128896 | bytes 33554432 | tf_op jit(solution)/shard_map/dot_general | solution.py:466
  963.7 46.7 %collective-permute-done.18 = bf16[512,2048]{1,0:T(8,128)(2,1)} collective-permute-done((bf16[512,2048]{1,0:T(8,128)(2,1)}, bf16[512,2048]{1,0:T(8,128)(2,1)}, u32[]{:S(2)}, u32[]{:S(2)}) %collective-permute-start.18) | collective-permute-done | bytes 2097184 | tf_op jit(solution)/shard_map/ppermute | solution.py:310
  1038.5 11.6 %all-gather.16.cloned.1.call-done = bf16[1024,1024]{1,0:T(8,128)(2,1)} async-done(((bf16[256,1024]{1,0:T(8,128)(2,1)}), bf16[1024,1024]{1,0:T(8,128)(2,1)}) %all-gather.16.cloned.1.call-update) | async-done | bytes 2097168 | tf_op jit(solution)/shard_map/all_gather | solution.py:530
  1052.3 21.9 %all-gather.18.cloned.1.call-done = bf16[512,2048]{1,0:T(8,128)(2,1)} async-done(((bf16[128,2048]{1,0:T(8,128)(2,1)}), bf16[512,2048]{1,0:T(8,128)(2,1)}) %all-gather.18.cloned.1.call-update) | async-done | bytes 2097168 | tf_op jit(solution)/shard_map/all_gather | solution.py:530
  1078.4 20.0 %all-gather.14.cloned.1.call-done = bf16[1024,1024]{1,0:T(8,128)(2,1)} async-done(((bf16[256,1024]{1,0:T(8,128)(2,1)}), bf16[1024,1024]{1,0:T(8,128)(2,1)}) %all-gather.14.cloned.1.call-update) | async-done | bytes 2097168 | tf_op jit(solution)/shard_map/all_gather | solution.py:530
  1104.6 12.1 %copy.65 = f32[256,2,8,4,128]{4,3,2,1,0:T(4,128)} copy(f32[256,2,8,4,128]{4,2,0,3,1:T(8,128)} %convert_bitcast_fusion) | data formatting | bytes 16777216 | tf_op jit(solution)/shard_map/convert_element_type | solution.py:535
  (303 shorter events, 347.7 us)
Async XLA Ops:
  7.2 147.9 %all-gather.10.cloned.1.call-start = ((), (), s32[]{:S(2)}) async-start(), calls=%async_computation.4 | async-start | bytes 9437184 | tf_op jit(solution)/shard_map/all_gather | solution.py:415
  16.2 212.8 %all-gather.12.cloned.1.call-start = ((), (), s32[]{:S(2)}) async-start(), calls=%async_computation.5 | async-start | bytes 4718592 | tf_op jit(solution)/shard_map/all_gather | solution.py:416
  16.2 49.6 %collective-permute-start.1 = (bf16[512,2048]{1,0:T(8,128)(2,1)S(1)}, bf16[512,2048]{1,0:T(8,128)(2,1)}, u32[]{:S(2)}, u32[]{:S(2)}) collective-permute-start(bf16[512,2048]{1,0:T(8,128)(2,1)S(1)} %copy-done.5), channel_id=1, source_target_pairs={{0,16},{8,24},{16,0},{24,8},{1,17},{9,25},{17,1},{25,9},{2,18},{10... | collective-permute-start | bytes 6291464 | tf_op jit(solution)/shard_map/ppermute | solution.py:310
  19.2 92.8 %collective-permute-start = (bf16[512,2048]{1,0:T(8,128)(2,1)S(1)}, bf16[512,2048]{1,0:T(8,128)(2,1)}, u32[]{:S(2)}, u32[]{:S(2)}) collective-permute-start(bf16[512,2048]{1,0:T(8,128)(2,1)S(1)} %copy-done.5), channel_id=1, source_target_pairs={{0,8},{8,0},{16,24},{24,16},{1,9},{9,1},{17,25},{25,17},{2,10},{10... | collective-permute-start | bytes 6291464 | tf_op jit(solution)/shard_map/ppermute | solution.py:310
  19.3 90.7 %collective-permute-start.8 = (bf16[512,2048]{1,0:T(8,128)(2,1)}, bf16[512,2048]{1,0:T(8,128)(2,1)}, u32[]{:S(2)}, u32[]{:S(2)}) collective-permute-start(bf16[512,2048]{1,0:T(8,128)(2,1)} %param.17), channel_id=1, source_target_pairs={{0,16},{8,24},{16,0},{24,8},{1,17},{9,25},{17,1},{25,9},{2,18},{10... | collective-permute-start | bytes 6291464 | tf_op jit(solution)/shard_map/ppermute | solution.py:310
  19.4 178.6 %collective-permute-start.7 = (bf16[512,2048]{1,0:T(8,128)(2,1)}, bf16[512,2048]{1,0:T(8,128)(2,1)}, u32[]{:S(2)}, u32[]{:S(2)}) collective-permute-start(bf16[512,2048]{1,0:T(8,128)(2,1)} %param.17), channel_id=1, source_target_pairs={{0,8},{8,0},{16,24},{24,16},{1,9},{9,1},{17,25},{25,17},{2,10},{10... | collective-permute-start | bytes 6291464 | tf_op jit(solution)/shard_map/ppermute | solution.py:310
  21.7 917.7 %reduce-scatter.9.cloned.1.call-start = ((), (), s32[]{:S(2)}) async-start(), calls=%async_computation.7 | async-start | bytes 4718592 | tf_op jit(solution)/shard_map/reduce_scatter | solution.py:472
  65.8 48.3 %collective-permute-start.2 = (bf16[512,2048]{1,0:T(8,128)(2,1)}, bf16[512,2048]{1,0:T(8,128)(2,1)}, u32[]{:S(2)}, u32[]{:S(2)}) collective-permute-start(bf16[512,2048]{1,0:T(8,128)(2,1)} %collective-permute-done.1), channel_id=1, source_target_pairs={{0,8},{8,0},{16,24},{24,16},{1,9},{9,1},{17,25},{25,17},{2,10},{10... | collective-permute-start | bytes 6291464 | tf_op jit(solution)/shard_map/ppermute | solution.py:310
  109.9 91.4 %collective-permute-start.9 = (bf16[512,2048]{1,0:T(8,128)(2,1)}, bf16[512,2048]{1,0:T(8,128)(2,1)}, u32[]{:S(2)}, u32[]{:S(2)}) collective-permute-start(bf16[512,2048]{1,0:T(8,128)(2,1)} %collective-permute-done.8), channel_id=1, source_target_pairs={{0,8},{8,0},{16,24},{24,16},{1,9},{9,1},{17,25},{25,17},{2,10},{10... | collective-permute-start | bytes 6291464 | tf_op jit(solution)/shard_map/ppermute | solution.py:310
  205.8 17.4 %collective-permute-start.5 = (f32[2,160,512]{2,1,0:T(8,128)}, f32[2,160,512]{2,1,0:T(8,128)S(1)}, u32[]{:S(2)}, u32[]{:S(2)}) collective-permute-start(f32[2,160,512]{2,1,0:T(8,128)} %pad_maximum_fusion.13), channel_id=1, source_target_pairs={{0,16},{8,24},{16,0},{24,8},{1,17},{9,25},{17,1},{25,9},{2,18},{10... | collective-permute-start | bytes 1966088 | tf_op jit(solution)/shard_map/ppermute | solution.py:310
  223.5 27.4 %collective-permute-start.6 = (f32[2,160,512]{2,1,0:T(8,128)S(1)}, f32[2,160,512]{2,1,0:T(8,128)S(1)}, u32[]{:S(2)}, u32[]{:S(2)}) collective-permute-start(f32[2,160,512]{2,1,0:T(8,128)S(1)} %pad_maximum_fusion.14), channel_id=1, source_target_pairs={{0,8},{8,0},{16,24},{24,16},{1,9},{9,1},{17,25},{25,17},{2,10},{10... | collective-permute-start | bytes 1966088 | tf_op jit(solution)/shard_map/ppermute | solution.py:310
  334.5 27.5 %collective-permute-start.11 = (f32[4,1024]{1,0:T(4,128)S(1)}, f32[4,1024]{1,0:T(4,128)S(1)}, u32[]{:S(2)}, u32[]{:S(2)}) collective-permute-start(f32[4,1024]{1,0:T(4,128)S(1)} %get-tuple-element.61), channel_id=1, source_target_pairs={{0,1},{1,2},{2,3},{3,4},{4,5},{5,6},{6,7},{8,9},{9,10},{10,11},{11... | collective-permute-start | bytes 49160 | tf_op jit(solution)/shard_map/ppermute | solution.py:316
  340.3 15.9 %collective-permute-start.10 = (f32[4,16,1024]{2,1,0:T(8,128)}, f32[4,16,1024]{2,1,0:T(8,128)S(1)}, u32[]{:S(2)}, u32[]{:S(2)}) collective-permute-start(f32[4,16,1024]{2,1,0:T(8,128)} %get-tuple-element.37), channel_id=1, source_target_pairs={{0,1},{1,2},{2,3},{3,4},{4,5},{5,6},{6,7},{8,9},{9,10},{10,11},{11... | collective-permute-start | bytes 786440 | tf_op jit(solution)/shard_map/ppermute | solution.py:316
  344.9 15.6 %collective-permute-start.21 = (f32[4,16,1024]{2,1,0:T(8,128)S(1)}, f32[4,16,1024]{2,1,0:T(8,128)S(1)}, u32[]{:S(2)}, u32[]{:S(2)}) collective-permute-start(f32[4,16,1024]{2,1,0:T(8,128)S(1)} %broadcast_multiply_fusion), channel_id=1, source_target_pairs={{1,0},{2,1},{3,2},{4,3},{5,4},{6,5},{7,6},{9,8},{10,9},{11,10},{12... | collective-permute-start | bytes 786440 | tf_op jit(solution)/shard_map/ppermute | solution.py:316
  346.3 15.7 %collective-permute-start.22 = (f32[4,1024]{1,0:T(4,128)S(1)}, f32[4,1024]{1,0:T(4,128)S(1)}, u32[]{:S(2)}, u32[]{:S(2)}) collective-permute-start(f32[4,1024]{1,0:T(4,128)S(1)} %broadcast_multiply_fusion.4), channel_id=1, source_target_pairs={{1,0},{2,1},{3,2},{4,3},{5,4},{6,5},{7,6},{9,8},{10,9},{11,10},{12... | collective-permute-start | bytes 49160 | tf_op jit(solution)/shard_map/ppermute | solution.py:316
  685.9 258.6 %reduce-scatter.11.cloned.1.call-start = ((), (), s32[]{:S(2)}) async-start(), calls=%async_computation.8 | async-start | bytes 4718592 | tf_op jit(solution)/shard_map/reduce_scatter | solution.py:472
  701.2 262.4 %reduce-scatter.7.cloned.1.call-start = ((), (), s32[]{:S(2)}) async-start(), calls=%async_computation.6 | async-start | bytes 4718592 | tf_op jit(solution)/shard_map/reduce_scatter | solution.py:472
  728.8 17.0 %collective-permute-start.27 = (f32[2,160,512]{2,1,0:T(8,128)}, f32[2,160,512]{2,1,0:T(8,128)S(1)}, u32[]{:S(2)}, u32[]{:S(2)}) collective-permute-start(f32[2,160,512]{2,1,0:T(8,128)} %copy.57), channel_id=1, source_target_pairs={{0,16},{8,24},{16,0},{24,8},{1,17},{9,25},{17,1},{25,9},{2,18},{10... | collective-permute-start | bytes 1966088 | tf_op jit(solution)/shard_map/ppermute | solution.py:310
  812.5 214.4 %reduce-scatter.13.cloned.1.call-start = ((), (), s32[]{:S(2)}) async-start(), calls=%async_computation.12 | async-start | bytes 884736
  865.9 48.0 %collective-permute-start.31 = (bf16[512,2048]{1,0:T(8,128)(2,1)}, bf16[512,2048]{1,0:T(8,128)(2,1)}, u32[]{:S(2)}, u32[]{:S(2)}) collective-permute-start(bf16[512,2048]{1,0:T(8,128)(2,1)} %fusion.23), channel_id=1, source_target_pairs={{0,16},{8,24},{16,0},{24,8},{1,17},{9,25},{17,1},{25,9},{2,18},{10... | collective-permute-start | bytes 6291464 | tf_op jit(solution)/shard_map/ppermute | solution.py:310
  921.8 128.3 %all-gather.16.cloned.1.call-start = ((), (), s32[]{:S(2)}) async-start(), calls=%async_computation.10 | async-start | bytes 2621440 | tf_op jit(solution)/shard_map/all_gather | solution.py:530
  939.4 134.8 %all-gather.18.cloned.1.call-start = ((), (), s32[]{:S(2)}) async-start(), calls=%async_computation.11 | async-start | bytes 2621440 | tf_op jit(solution)/shard_map/all_gather | solution.py:530
  944.5 153.9 %all-gather.14.cloned.1.call-start = ((), (), s32[]{:S(2)}) async-start(), calls=%async_computation.9 | async-start | bytes 2621440 | tf_op jit(solution)/shard_map/all_gather | solution.py:530
  962.5 48.0 %collective-permute-start.18 = (bf16[512,2048]{1,0:T(8,128)(2,1)}, bf16[512,2048]{1,0:T(8,128)(2,1)}, u32[]{:S(2)}, u32[]{:S(2)}) collective-permute-start(bf16[512,2048]{1,0:T(8,128)(2,1)} %fusion.27), channel_id=1, source_target_pairs={{0,16},{8,24},{16,0},{24,8},{1,17},{9,25},{17,1},{25,9},{2,18},{10... | collective-permute-start | bytes 6291464 | tf_op jit(solution)/shard_map/ppermute | solution.py:310
  (60 other events, 1797.8 us)
Sparse Core Ops, SparseCore 0:
  16.3 138.8 all-gather.9
  157.3 71.6 all-gather.11
  686.0 90.3 reduce-scatter.8
  779.9 89.4 reduce-scatter.10
  872.9 87.9 reduce-scatter.6
  964.0 62.8 reduce-scatter.12
  1028.5 21.5 all-gather.15
  1051.7 22.5 all-gather.17
  1075.8 22.5 all-gather.13

commit v2 on v1

v2 whole, which is shorter than its diff:
```python
from functools import partial

import jax
import jax.numpy as jnp
from jax import lax
from jax.experimental import pallas as pl
from jax.experimental.pallas import tpu as pltpu
from jax.sharding import PartitionSpec as P

EPSILON = 1e-05
SPAN_TOKENS = 4096
F32=jnp.float32; BF16=jnp.bfloat16
LN=128
def first_kernel(U, dt_ref, x_ref, b_ref, a_ref, hend_ref, h_s, dtx_s):
    TC, EG = dt_ref.shape
    NT = EG//LN
    c = pl.program_id(2)
    @pl.when(c == 0)
    def _():
        h_s[...] = jnp.zeros_like(h_s)
    dtx_s[...] = dt_ref[...]*x_ref[...].astype(F32)
    sl = [slice(j*LN,(j+1)*LN) for j in range(NT)]
    A = [a_ref[:, s] for s in sl]
    def body(i, carry):
        h = list(carry)
        rows = pl.ds(pl.multiple_of(i*U,U),U)
        dv, xv = dt_ref.at[rows], dtx_s.at[rows]
        for k in range(U):
            bt = b_ref[i*U+k]
            for j in range(NT):
                a = jnp.exp2(dv[k:k+1, sl[j]]*A[j])
                h[j] = a*h[j] + xv[k:k+1, sl[j]]*bt
        return tuple(h)
    h = lax.fori_loop(0, TC//U, body, tuple(h_s[:, s] for s in sl))
    for j in range(NT): h_s[:, sl[j]] = h[j]
    @pl.when(c == pl.num_programs(2)-1)
    def _():
        hend_ref[...] = h_s[...]

def first_pass(dt, x, bx, a2, Q, TC=128, EG=512, U=8):
    T,E = dt.shape; N = a2.shape[0]; L=T//Q; NC=L//TC; NE=E//EG
    row = pl.BlockSpec((TC,EG), lambda q,e,c:(q*NC+c, e))
    sp = pl.BlockSpec((TC,N,LN), lambda q,e,c:(q*NC+c,0,0))
    st = pl.BlockSpec((None,N,EG), lambda q,e,c:(q,0,e))
    return pl.pallas_call(partial(first_kernel,U), grid=(Q,NE,NC),
        in_specs=[row,row,sp,pl.BlockSpec((N,EG), lambda q,e,c:(0,e))],
        out_specs=st,
        out_shape=jax.ShapeDtypeStruct((Q,N,E),F32),
        scratch_shapes=[pltpu.VMEM((N,EG),F32),pltpu.VMEM((TC,EG),F32)],
        compiler_params=pltpu.CompilerParams(dimension_semantics=("arbitrary",)*3, vmem_limit_bytes=60<<20),
        name="first_pass",
        cost_estimate=pl.CostEstimate(flops=5*T*E*N, bytes_accessed=10*T*E, transcendentals=T*E*N))(dt,x,bx,a2)

LOG2E = 1.4426950408889634


def sums(tb):
    return (lax.broadcasted_iota(jnp.int32,(tb,tb*8),1)//8 == lax.broadcasted_iota(jnp.int32,(tb,tb*8),0)).astype(BF16)

def fwd_kernel(U, dt_ref, x_ref, gate_ref, gg_ref, b_ref, c_ref, a_ref, skip_ref, h0_ref,
               out_ref, gz_ref, g_ref, ck_ref, adj_ref, h_s, p_s, r_s, q_s, y_s, dtx_s):
    TC, EG = dt_ref.shape
    NT = EG//LN
    c = pl.program_id(2)
    @pl.when(c == 0)
    def _():
        h_s[...] = h0_ref[...]; p_s[...] = jnp.ones_like(p_s); r_s[...] = jnp.zeros_like(r_s)
        q_s[...] = jnp.zeros_like(q_s)
    ck_ref[...] = h_s[...]
    dtx_s[...] = dt_ref[...]*x_ref[...].astype(F32)
    gate = gate_ref[...]
    g_ref[...] = gg_ref[...]*(gate*jax.nn.sigmoid(gate))
    sl = [slice(j*LN,(j+1)*LN) for j in range(NT)]
    A = [a_ref[:, s] for s in sl]
    S = sums(U)
    G = TC//U
    def reduce(i):
        y_s[pl.ds(pl.multiple_of(i*U,U),U),:] = jnp.dot(S, q_s[...], preferred_element_type=F32)
    def body(i, carry):
        reduce(jnp.maximum(i-1,0))
        h, p, r = [list(v) for v in carry]
        rows = pl.ds(pl.multiple_of(i*U,U),U)
        dv, xv, gv = dt_ref.at[rows], dtx_s.at[rows], g_ref.at[rows]
        low = [None]*NT
        for k in range(U):
            t = i*U+k
            bt = b_ref[t]; ct = c_ref[t]
            for j in range(NT):
                a = jnp.exp2(dv[k:k+1, sl[j]]*A[j])
                h[j] = a*h[j] + xv[k:k+1, sl[j]]*bt
                p[j] = p[j]*a
                r[j] = r[j] + p[j]*(ct*gv[k:k+1, sl[j]])
                q = h[j]*ct
                q = q[:8]+q[8:]
                if k % 2 == 0: low[j] = q
                else: q_s[k*8-8:k*8+8, sl[j]] = jnp.concatenate([low[j],q],axis=0).astype(BF16)
        return tuple(h), tuple(p), tuple(r)
    init = tuple(tuple(s_[:, s] for s in sl) for s_ in (h_s, p_s, r_s))
    h, p, r = lax.fori_loop(0, G, body, init)
    reduce(G-1)
    for j in range(NT):
        h_s[:, sl[j]] = h[j]; p_s[:, sl[j]] = p[j]; r_s[:, sl[j]] = r[j]
    gate = gate_ref[...]
    sig = jax.nn.sigmoid(gate)
    y = y_s[...] + skip_ref[...]*x_ref[...].astype(F32)
    out_ref[...] = (y*(gate*sig)).astype(BF16)
    gz_ref[...] = (gg_ref[...]*y*sig*(1.0+gate*(1.0-sig))).astype(BF16)
    @pl.when(c == pl.num_programs(2)-1)
    def _(): adj_ref[...] = r_s[...]

def fwd_pass(dt, x, gate, gg, bx, cx, a2, skip, h0, Q, TC=64, EG=512, U=8):
    T,E = dt.shape; N = a2.shape[0]; L=T//Q; NC=L//TC; NE=E//EG
    row = pl.BlockSpec((TC,EG), lambda q,e,c:(q*NC+c, e))
    sp = pl.BlockSpec((TC,N,LN), lambda q,e,c:(q*NC+c,0,0))
    st = pl.BlockSpec((None,N,EG), lambda q,e,c:(q,0,e))
    return pl.pallas_call(partial(fwd_kernel,U), grid=(Q,NE,NC),
        in_specs=[row,row,row,row,sp,sp,pl.BlockSpec((N,EG), lambda q,e,c:(0,e)), pl.BlockSpec((1,EG), lambda q,e,c:(0,e)), st],
        out_specs=[row, row, row, pl.BlockSpec((None,N,EG), lambda q,e,c:(q*NC+c,0,e)), st],
        out_shape=[jax.ShapeDtypeStruct((T,E),BF16)]*2 + [jax.ShapeDtypeStruct((T,E),F32),
            jax.ShapeDtypeStruct((Q*NC,N,E),F32), jax.ShapeDtypeStruct((Q,N,E),F32)],
        scratch_shapes=[pltpu.VMEM((N,EG),F32)]*3 + [pltpu.VMEM((U*8,EG),BF16)] + [pltpu.VMEM((TC,EG),F32)]*2,
        compiler_params=pltpu.CompilerParams(dimension_semantics=("arbitrary",)*3, vmem_limit_bytes=60<<20),
        name="fwd_pass",
        cost_estimate=pl.CostEstimate(flops=11*T*E*N, bytes_accessed=22*T*E, transcendentals=T*E*N))(dt,x,gate,gg,bx,cx,a2,skip,h0)

def bwd_kernel(U, n_in, *refs):
    dt_ref, x_ref, g_ref, b_ref, c_ref, a_ref, skip_ref, ck_ref, mu0_ref = refs[:9]
    (gl_ref, gx_ref, gb_ref, gc_ref, ga_ref, su_ref,
     mu_s, ga_s, su_s, qa_s, qb_s, zb_s, zc_s, sa_s, sb_s, dtx_s, a_s, h_s) = refs[n_in:]
    TC, EG = dt_ref.shape
    N = a_ref.shape[0]
    NT = EG//LN
    c = pl.program_id(2)
    @pl.when(c == 0)
    def _():
        mu_s[...] = mu0_ref[...]
        for v in (ga_s, su_s, qa_s, qb_s, zb_s, zc_s): v[...] = jnp.zeros_like(v)
    dtx_s[...] = dt_ref[...]*x_ref[...].astype(F32)
    sl = [slice(j*LN,(j+1)*LN) for j in range(NT)]
    A = [a_ref[:, s] for s in sl]
    h_s[0] = ck_ref[...]
    G = TC//U
    def up(i, carry):
        h = list(carry)
        rows = pl.ds(pl.multiple_of(i*U,U),U)
        dv, xv = dt_ref.at[rows], dtx_s.at[rows]
        for k in range(U):
            t = i*U+k
            bt = b_ref[t]
            for j in range(NT):
                a = jnp.exp2(dv[k:k+1, sl[j]]*A[j])
                h[j] = a*h[j] + xv[k:k+1, sl[j]]*bt
                a_s[t, :, sl[j]] = a
                h_s[t+1, :, sl[j]] = h[j]
        return tuple(h)
    h = lax.fori_loop(0, G, up, tuple(ck_ref[:, s] for s in sl))
    S = sums(U)
    ones = jnp.ones((8,LN),BF16)
    nt = (((1,),(1,)),((),()))
    def reduce(i):
        rows = pl.ds(pl.multiple_of(i*U,U),U)
        sa_s[rows,:] = jnp.dot(S, qa_s[...], preferred_element_type=F32)
        sb_s[rows,:] = jnp.dot(S, qb_s[...], preferred_element_type=F32)
        cols = pl.ds(pl.multiple_of(i*(U*N),U*N),U*N)
        gb_ref[:,cols] = lax.dot_general(ones, zb_s[...], nt, preferred_element_type=F32)[:1]
        gc_ref[:,cols] = lax.dot_general(ones, zc_s[...], nt, preferred_element_type=F32)[:1]
    def down(ii, carry):
        i = G-1-ii
        reduce(jnp.minimum(i+1,G-1))
        mu, ga, h = [list(v) for v in carry]
        rows = pl.ds(pl.multiple_of(i*U,U),U)
        dv, gv, xv = dt_ref.at[rows], g_ref.at[rows], dtx_s.at[rows]
        la, lb = [None]*NT, [None]*NT
        for k in reversed(range(U)):
            t = i*U+k
            bt = b_ref[t]; ct = c_ref[t]
            zb = zc = None
            for j in range(NT):
                gr = gv[k:k+1, sl[j]]
                lam = mu[j] + ct*gr
                zcj = h[j]*gr
                zbj = lam*xv[k:k+1, sl[j]]
                zc = zcj if j == 0 else zc+zcj
                zb = zbj if j == 0 else zb+zbj
                mu[j] = a_s[t,:,sl[j]]*lam
                h[j] = h_s[t,:,sl[j]]
                w = mu[j]*h[j]
                ga[j] = ga[j] + dv[k:k+1, sl[j]]*w
                qa = A[j]*w
                qb = lam*bt
                qa = qa[:8]+qa[8:]
                qb = qb[:8]+qb[8:]
                if k % 2: la[j], lb[j] = qa, qb
                else:
                    qa_s[k*8:k*8+16, sl[j]] = jnp.concatenate([qa,la[j]],axis=0).astype(BF16)
                    qb_s[k*8:k*8+16, sl[j]] = jnp.concatenate([qb,lb[j]],axis=0).astype(BF16)
            zb_s[k*N:k*N+N,:] = zb.astype(BF16)
            zc_s[k*N:k*N+N,:] = zc.astype(BF16)
        return tuple(mu), tuple(ga), tuple(h)
    init = tuple(tuple(s_[:, s] for s in sl) for s_ in (mu_s, ga_s)) + (h,)
    mu, ga, h = lax.fori_loop(0, G, down, init)
    reduce(0)
    for j in range(NT): ga_s[:, sl[j]] = ga[j]; mu_s[:, sl[j]] = mu[j]
    d = dt_ref[...]; x = x_ref[...].astype(F32); g = g_ref[...]
    sb = sb_s[...]
    gx_ref[...] = d*sb + skip_ref[...]*g
    sig = jnp.where(d < 0.03, d*(1.0-d*(0.5-d*(1.0/6.0-d*(1.0/24.0)))), 1.0-jnp.exp(-d))
    gp = (sa_s[...]*(1.0/LOG2E) + x*sb)*sig
    gl_ref[...] = gp.astype(BF16)
    su_s[...] = su_s[...] + jnp.concatenate([jnp.sum(gp,axis=0,keepdims=True), jnp.sum(g*x,axis=0,keepdims=True)],axis=0)
    @pl.when(c == pl.num_programs(2)-1)
    def _():
        ga_ref[...] = ga_s[...]; su_ref[...] = su_s[...]

def bwd_pass(dt, x, g, bx, cx, a2, skip, ck, mu0, Q, at, prev, waits, TC=64, EG=512, U=8):
    T,E = dt.shape; N = a2.shape[0]; L=T//Q; NC=L//TC; NE=E//EG
    row = pl.BlockSpec((TC,EG), lambda q,e,c:(q*NC+NC-1-c, at))
    sp = pl.BlockSpec((TC,N,LN), lambda q,e,c:(q*NC+NC-1-c,0,0))
    st = pl.BlockSpec((None,N,EG), lambda q,e,c:(q,0,at))
    nb = pl.BlockSpec((None,1,TC*N), lambda q,e,c:(at,0,q*NC+NC-1-c))
    args = (dt,x,g,bx,cx,a2,skip,ck,mu0)
    n_in = len(args)+len(prev)+len(waits)
    return pl.pallas_call(partial(bwd_kernel,U,n_in), grid=(Q,1,NC),
        in_specs=[row,row,row,sp,sp,pl.BlockSpec((N,EG), lambda q,e,c:(0,at)), pl.BlockSpec((1,EG), lambda q,e,c:(0,at)),
            pl.BlockSpec((None,N,EG), lambda q,e,c:(q*NC+NC-1-c,0,at)), st]+[pl.BlockSpec(memory_space=pl.ANY)]*(len(prev)+len(waits)),
        out_specs=[row,row,nb,nb,st,pl.BlockSpec((None,2,EG), lambda q,e,c:(q,0,at))],
        out_shape=[jax.ShapeDtypeStruct((T,E),BF16), jax.ShapeDtypeStruct((T,E),F32)]+[jax.ShapeDtypeStruct((NE,1,T*N),F32)]*2
            +[jax.ShapeDtypeStruct((Q,N,E),F32), jax.ShapeDtypeStruct((Q,2,E),F32)],
        input_output_aliases={len(args)+i: i for i in range(len(prev))},
        scratch_shapes=[pltpu.VMEM((N,EG),F32)]*2+[pltpu.VMEM((2,EG),F32)]+[pltpu.VMEM((U*8,EG),BF16)]*2+[pltpu.VMEM((U*N,LN),BF16)]*2
            +[pltpu.VMEM((TC,EG),F32)]*3+[pltpu.VMEM((TC,N,EG),F32), pltpu.VMEM((TC+1,N,EG),F32)],
        compiler_params=pltpu.CompilerParams(dimension_semantics=("arbitrary",)*3, vmem_limit_bytes=62<<20),
        name="bwd_pass",
        cost_estimate=pl.CostEstimate(flops=20*T*EG*N, bytes_accessed=22*T*EG, transcendentals=T*EG*N))(*args,*prev,*waits)


def spread_kernel(in_ref, *refs):
    refs[-1][...] = jnp.concatenate([in_ref[r].astype(F32) for r in range(in_ref.shape[0])], axis=1)


def spread(pieces, rows, cols, part, half, prev):
    n_rep, n_shard = (pieces.shape[0], pieces.shape[2] // part)
    return pl.pallas_call(
        spread_kernel,
        grid=(n_shard,),
        in_specs=[pl.BlockSpec((n_rep, rows, part), lambda s: (0, 0, s))] + [pl.BlockSpec(memory_space=pl.ANY)] * len(prev),
        out_specs=pl.BlockSpec((rows, n_rep * part), lambda s: (0, half * n_shard + s)),
        out_shape=jax.ShapeDtypeStruct((rows, cols), F32),
        input_output_aliases={1 + i: i for i in range(len(prev))},
        compiler_params=pltpu.CompilerParams(dimension_semantics=("arbitrary",)),
        name="spread",
        cost_estimate=pl.CostEstimate(flops=0, bytes_accessed=3 * rows * cols, transcendentals=0),
    )(pieces, *prev)


def pick_kernel(count, at_ref, in_ref, out_ref):
    part = out_ref.shape[1] // count
    wide = in_ref.shape[1] // count
    at = at_ref[0] * part
    for k in range(count):
        out_ref[:, k * part:(k + 1) * part] = in_ref[:, pl.ds(pl.multiple_of(k * wide + at, part), part)]


def pick(value, at, n_shard, part, half):
    rows, cols = value.shape
    count = 4 if n_shard % 4 == 0 else n_shard
    steps = n_shard // count
    wide = cols // (2 * steps)
    return pl.pallas_call(
        partial(pick_kernel, count),
        grid_spec=pltpu.PrefetchScalarGridSpec(
            num_scalar_prefetch=1,
            grid=(steps,),
            in_specs=[pl.BlockSpec((rows, wide), lambda s, a: (0, half * steps + s))],
            out_specs=pl.BlockSpec((rows, count * part), lambda s, a: (0, s)),
        ),
        out_shape=jax.ShapeDtypeStruct((rows, n_shard * part), value.dtype),
        compiler_params=pltpu.CompilerParams(dimension_semantics=("arbitrary",)),
        name="pick",
        cost_estimate=pl.CostEstimate(flops=0, bytes_accessed=2 * rows * cols, transcendentals=0),
    )(at, value)


def conv_kernel(x_ref, edge_ref, w_ref, o_ref, x_s):
    L = x_ref.shape[0]
    taps = w_ref.shape[0] - 1
    x_s[0:8, :] = edge_ref[...]
    x_s[8:, :] = x_ref[...].astype(F32)
    pre = jnp.broadcast_to(w_ref[taps:taps + 1, :], x_ref.shape)
    for k in range(taps):
        at = 8 - (taps - 1) + k
        pre = pre + w_ref[k:k + 1, :] * x_s[at:at + L, :]
    o_ref[...] = (pre * jax.nn.sigmoid(pre)).astype(BF16)


def conv_pass(conv_in, edge, wb, Q, EB=256):
    T, E = conv_in.shape
    L = T // Q
    row = pl.BlockSpec((L, EB), lambda q, e: (q, e))
    return pl.pallas_call(
        conv_kernel,
        grid=(Q, E // EB),
        in_specs=[
            row,
            pl.BlockSpec((None, 8, EB), lambda q, e: (q, 0, e)),
            pl.BlockSpec((wb.shape[0], EB), lambda q, e: (0, e)),
        ],
        out_specs=row,
        out_shape=jax.ShapeDtypeStruct((T, E), BF16),
        scratch_shapes=[pltpu.VMEM((L + 8, EB), F32)],
        compiler_params=pltpu.CompilerParams(dimension_semantics=("arbitrary",) * 2),
        name="conv_pass",
        cost_estimate=pl.CostEstimate(flops=12 * T * E, bytes_accessed=4 * T * E, transcendentals=T * E),
    )(conv_in, edge, wb)


def conv_back_kernel(n_in, *refs):
    gp_ref, xp_ref, gx_ref, x_ref, edge_ref, w_ref = refs[:6]
    gi_ref, head_ref, tail_ref, gw_ref, x_s, g_s = refs[n_in:]
    L = x_ref.shape[0]
    taps = w_ref.shape[0] - 1
    x_s[0:8, :] = edge_ref[...]
    x_s[8:, :] = x_ref[...].astype(F32)
    at = [8 - (taps - 1) + k for k in range(taps)]
    pre = jnp.broadcast_to(w_ref[taps:taps + 1, :], x_ref.shape)
    for k in range(taps):
        pre = pre + w_ref[k:k + 1, :] * x_s[at[k]:at[k] + L, :]
    s = jax.nn.sigmoid(pre)
    g_out = contract_cols(gp_ref[...], xp_ref[...]) + gx_ref[...]
    g_pre = g_out * s * (1.0 + pre * (1.0 - s))
    g_s[0:L, :] = g_pre
    g_s[L:, :] = jnp.zeros((8, x_ref.shape[1]), F32)
    gw = [jnp.sum(g_pre * x_s[at[k]:at[k] + L, :], axis=0, keepdims=True) for k in range(taps)]
    gw.append(jnp.sum(g_pre, axis=0, keepdims=True))
    gw_ref[...] = jnp.concatenate(gw, axis=0)
    head_ref[...] = g_s[0:8, :]
    g_in = jnp.zeros(x_ref.shape, F32)
    for k in range(taps):
        g_in = g_in + w_ref[k:k + 1, :] * g_s[taps - 1 - k:taps - 1 - k + L, :]
    gi_ref[...] = g_in.astype(BF16)
    tail_ref[...] = g_in[L - 8:, :]


def conv_back(g_projected, x_proj, gx, conv_in, edge, wb, waits, Q, EB=256):
    T, E = conv_in.shape
    L = T // Q
    row = pl.BlockSpec((L, EB), lambda q, e: (q, e))
    edges = pl.BlockSpec((None, 8, EB), lambda q, e: (q, 0, e))
    rows = wb.shape[0]
    return pl.pallas_call(
        partial(conv_back_kernel, 6 + len(waits)),
        grid=(Q, E // EB),
        in_specs=[
            pl.BlockSpec((L, g_projected.shape[1]), lambda q, e: (q, 0)),
            pl.BlockSpec((EB, x_proj.shape[1]), lambda q, e: (e, 0)),
            row,
            row,
            edges,
            pl.BlockSpec((rows, EB), lambda q, e: (0, e)),
        ] + [pl.BlockSpec(memory_space=pl.ANY)] * len(waits),
        out_specs=[row, edges, edges, pl.BlockSpec((None, rows, EB), lambda q, e: (q, 0, e))],
        out_shape=[
            jax.ShapeDtypeStruct((T, E), BF16),
            jax.ShapeDtypeStruct((Q, 8, E), F32),
            jax.ShapeDtypeStruct((Q, 8, E), F32),
            jax.ShapeDtypeStruct((Q, rows, E), F32),
        ],
        scratch_shapes=[pltpu.VMEM((L + 8, EB), F32)] * 2,
        compiler_params=pltpu.CompilerParams(dimension_semantics=("arbitrary",) * 2),
        name="conv_back",
        cost_estimate=pl.CostEstimate(flops=400 * T * E, bytes_accessed=10 * T * E, transcendentals=T * E),
    )(g_projected, x_proj, gx, conv_in, edge, wb, *waits)


def contract_rows(left, right):
    return lax.dot_general(left, right, (((0,), (0,)), ((), ())), preferred_element_type=F32)


def contract_cols(left, right):
    return lax.dot_general(left, right, (((1,), (1,)), ((), ())), preferred_element_type=F32)


def swap(value, flip):
    return lax.ppermute(value, "rep", [(i, i ^ flip) for i in range(lax.axis_size("rep"))])


def shifted(value, steps):
    count = lax.axis_size("shard")
    first, last = (max(0, -steps), min(count, count - steps))
    return lax.ppermute(value, "shard", [(i, i + steps) for i in range(first, last)])


def rep_gather(value):
    far = swap(value, 2)
    return [value, swap(value, 1), far, swap(far, 1)]


def rep_near(parts):
    low = [part.astype(BF16) for part in parts]
    near = [swap(low[k], 1).astype(F32) for k in (1, 3)]
    return parts[0] + near[0], (parts[2] + near[1]).astype(BF16)


def rep_far(mine, other):
    return mine + swap(other, 2).astype(F32)


def rep_sum(parts):
    near = [swap(parts[k], 1) for k in (1, 3)]
    pair = [parts[0] + near[0], parts[2] + near[1]]
    far = [swap(value, 2) for value in pair]
    full = [pair[0] + far[1], pair[1] + far[0]]
    over = [swap(value, 1) for value in full]
    return [full[0], over[0], full[1], over[1]]


def add_all(value, axis):
    step = 1
    while step < lax.axis_size(axis):
        value = value + lax.ppermute(value, axis, [(i, i ^ step) for i in range(lax.axis_size(axis))])
        step *= 2
    return value


def carry_in(total, state, rates, place, reverse):
    sign = -1 if reverse else 1
    span = lax.axis_size("shard")
    both = shifted(jnp.concatenate([state, total[:, None, :]], axis=1), sign)
    both = both * jnp.where(place >= 1, 1.0, 0.0)
    step = 1
    while step < min(span, 8):
        far = shifted(both, sign * step) * jnp.where(place >= step, 1.0, 0.0)
        total = both[:, -1:]
        state = both[:, :-1] + jnp.exp(rates[None] * total) * far[:, :-1]
        both = jnp.concatenate([state, total + far[:, -1:]], axis=1)
        step *= 2
    return both[:, :-1]


def on_device(
    block_input,
    cotangent,
    seq_lengths,
    slot_order,
    norm_gain,
    in_proj,
    conv_weight,
    conv_bias,
    x_proj,
    dt_proj,
    dt_bias,
    a_log,
    d_skip,
    out_proj,
):
    n_shard, n_rep = (lax.axis_size("shard"), lax.axis_size("rep"))
    shard_at, rep_at = (lax.axis_index("shard"), lax.axis_index("rep"))
    rows, width = block_input.shape
    tokens = n_rep * rows
    taps, wide = conv_weight.shape
    part = wide // n_rep
    chans = part * n_shard
    rank = dt_proj.shape[0]
    states = a_log.shape[0]
    span = max(1, min(n_shard, SPAN_TOKENS // rows))
    in_slot = shard_at % span
    keep_prev = (in_slot != 0).astype(F32)
    keep_next = (in_slot != span - 1).astype(F32)
    places = in_slot * rows + jnp.arange(rows, dtype=jnp.int32)

    def valid_of(flip):
        slot_at = ((rep_at ^ flip) * n_shard + shard_at) // span
        slot_len = jnp.sum(jnp.where(slot_order == slot_at, seq_lengths, 0))
        return (places < slot_len).astype(F32)[:, None]

    valid = [valid_of(k) for k in range(n_rep)]

    def mine(value, axis):
        return lax.dynamic_slice_in_dim(value, rep_at * part, part, axis)

    x_all = rep_gather(block_input)
    small = jnp.concatenate(
        [
            mine(x_proj, 0),
            mine(dt_proj, 1).T,
            mine(a_log, 1).T,
            mine(conv_weight, 1).T,
            mine(conv_bias, 0)[:, None],
            mine(dt_bias, 0)[:, None],
            mine(d_skip, 0)[:, None],
            norm_gain.reshape(part, -1),
        ],
        axis=1,
    )
    if part % LN:
        in_mine = lax.dynamic_index_in_dim(
            in_proj.reshape(in_proj.shape[0], 2, n_shard, n_rep, part), rep_at, 3, keepdims=False
        ).reshape(in_proj.shape[0], 2, chans)
        in_conv, in_gate = (in_mine[:, 0], in_mine[:, 1])
    else:
        in_conv, in_gate = [pick(in_proj, rep_at.reshape(1), n_shard, part, k) for k in range(2)]
    small_all = lax.all_gather(small, "shard", axis=0, tiled=True)
    conv_w = lax.all_gather(in_conv, "shard", axis=0, tiled=True)
    gate_w = lax.all_gather(in_gate, "shard", axis=0, tiled=True)
    out_all = lax.all_gather(mine(out_proj, 0), "shard", axis=0, tiled=True)
    cot_all = rep_gather(cotangent)

    cut = [x_proj.shape[1], rank, states, taps, 1, 1, 1]
    ends = [sum(cut[:i + 1]) for i in range(len(cut))]
    xproj_all = small_all[:, :ends[0]]
    dtproj_all = small_all[:, ends[0]:ends[1]].T
    log_rates = small_all[:, ends[1]:ends[2]].T.astype(F32)
    wb = small_all[:, ends[2]:ends[4]].T.astype(F32)
    dtbias_all = small_all[:, ends[4]].astype(F32)
    skip_all = small_all[:, ends[5]].astype(F32)
    gain_f = small_all[:, ends[6]:].reshape(width).astype(F32)

    def norm(value):
        value = value.astype(F32)
        scale = lax.rsqrt(jnp.mean(value * value, axis=1, keepdims=True) + EPSILON)
        return (value * scale * gain_f[None, :]).astype(BF16)

    normed = jnp.concatenate([norm(value) for value in x_all], axis=0)
    conv_in = jnp.dot(normed, conv_w, preferred_element_type=F32).astype(BF16)
    last = conv_in.reshape(n_rep, rows, chans)[:, rows - (taps - 1):]
    edge = shifted(last, 1).astype(F32) * keep_prev
    edge = jnp.concatenate([jnp.zeros((n_rep, 8 - (taps - 1), chans), F32), edge], axis=1)
    conv_out = conv_pass(conv_in, edge, wb, n_rep)
    proj = lax.dot_general(xproj_all, conv_out, (((0,), (1,)), ((), ())), preferred_element_type=F32)
    proj = jnp.concatenate(
        rep_sum([proj[:, k * rows:(k + 1) * rows] for k in range(n_rep)]), axis=1
    )
    step_low = proj[:rank].astype(BF16)
    b_all = jnp.broadcast_to(proj[rank:rank + states].T[:, :, None], (tokens, states, LN))
    c_all = jnp.broadcast_to(proj[rank + states:].T[:, :, None], (tokens, states, LN))
    step = jax.nn.softplus(contract_rows(step_low, dtproj_all) + dtbias_all[None, :])
    rates = -jnp.exp(log_rates)
    rates2 = rates * LOG2E
    gate_in = jnp.dot(normed, gate_w, preferred_element_type=F32)
    back = jnp.concatenate(
        [(cot_all[k].astype(F32) * valid[k]).astype(BF16) for k in range(n_rep)], axis=0
    )
    g_gated = contract_cols(back, out_all)
    skip = skip_all[None, :]
    local_end = first_pass(step, conv_out, b_all, rates2, n_rep)
    total = jnp.sum(step.reshape(n_rep, rows, chans), axis=1)
    start_state = carry_in(total, local_end, rates, in_slot, False)
    gated, g_gate, g_scanned, kept, local_adj = fwd_pass(
        step, conv_out, gate_in, g_gated, b_all, c_all, rates2, skip, start_state, n_rep
    )
    end_grad = carry_in(total, local_adj, rates, span - 1 - in_slot, True)
    branch = jnp.dot(gated, out_all, preferred_element_type=F32)
    near, other = rep_near([branch[k * rows:(k + 1) * rows] for k in range(n_rep)])
    pieces = width // chans
    held = in_proj.shape[0]
    local = [contract_rows(normed, g_gate).astype(BF16).reshape(n_shard, held, chans)]
    for k in range(pieces):
        piece = contract_rows(gated, back[:, k * chans:(k + 1) * chans])
        local.append(piece.astype(BF16).reshape(n_shard, part, chans))
    local = jnp.concatenate(local, axis=1).reshape(-1, chans)
    branch = rep_far(near, other)
    input_f = block_input.astype(F32)
    activations = (input_f + valid[0] * branch).astype(BF16)

    def scatter(value):
        return lax.psum_scatter(value, "shard", scatter_dimension=0, tiled=True)

    def everyone(value):
        return lax.all_gather(value, "rep", axis=0)

    early = scatter(local)
    back_args = (step, conv_out, g_scanned, b_all, c_all, rates2, skip, kept, end_grad, n_rep)
    prev, groups = ([], chans // 512)
    for k in range(groups):
        prev = bwd_pass(*back_args, k, prev, [local, other] if k == 0 else [activations])
    g_lin, g_scan_in, g_b, g_c, g_a, g_sums = prev
    grad_dt_bias, grad_skip = jnp.sum(g_sums, axis=0)
    grad_dt_proj = contract_rows(g_lin, step_low.T)
    g_low = contract_cols(dtproj_all, g_lin)
    g_b, g_c = [jnp.sum(v, axis=(0, 1)).reshape(tokens, states).T for v in (g_b, g_c)]
    g_proj = jnp.concatenate([g_low, g_b, g_c], axis=0)
    g_proj = jnp.concatenate(
        rep_sum([g_proj[:, k * rows:(k + 1) * rows] for k in range(n_rep)]), axis=1
    )
    g_proj = g_proj.T.astype(BF16)
    grad_x_proj = contract_rows(conv_out, g_proj)
    g_in, head, tail, grad_wb = conv_back(g_proj, xproj_all, g_scan_in, conv_in, edge, wb, [early], n_rep)
    after = shifted(head, -1) * keep_next
    joined = jnp.concatenate([jnp.zeros_like(after), after], axis=1)
    fix = tail
    for k in range(taps - 1):
        at = taps - 1 - k
        fix = fix + wb[k][None, None, :] * joined[:, at:at + 8]
    g_in = g_in.reshape(n_rep, rows, chans).at[:, rows - 8:].set(fix.astype(BF16))
    g_in = g_in.reshape(tokens, chans)
    grad_a_log = rates * jnp.sum(g_a, axis=0)
    small = [grad_x_proj, grad_dt_proj, grad_a_log.T, jnp.sum(grad_wb, axis=0).T, grad_dt_bias[:, None], grad_skip[:, None]]
    small.append(jnp.zeros((chans, -ends[6] % LN), F32))
    small = jnp.concatenate(small, axis=1).astype(BF16).reshape(n_shard, part, -1, LN)
    lanes = small.shape[2]
    small = small.transpose(0, 2, 1, 3).reshape(n_shard, -1, chans)
    late = contract_rows(normed, g_in).astype(BF16).reshape(n_shard, held, chans)
    late = scatter(jnp.concatenate([late, small], axis=1).reshape(-1, chans))
    half = rows // 2
    g_normed = []
    for at in (0, half):
        conv_rows = g_in.reshape(n_rep, rows, chans)[:, at:at + half].reshape(n_rep * half, chans)
        gate_rows = g_gate.reshape(n_rep, rows, chans)[:, at:at + half].reshape(n_rep * half, chans)
        both = contract_cols(conv_rows, conv_w) + contract_cols(gate_rows, gate_w)
        g_normed.append(rep_far(*rep_near([both[k * half:(k + 1) * half] for k in range(n_rep)])))
    g_normed = jnp.concatenate(g_normed, axis=0)
    scale = lax.rsqrt(jnp.mean(input_f * input_f, axis=1, keepdims=True) + EPSILON)
    grad_gain = jnp.sum(g_normed * input_f * scale, axis=0)
    g_hat = g_normed * gain_f[None, :]
    input_grad = (
        cotangent.astype(F32)
        + scale * g_hat
        - input_f * (scale * scale * scale) * jnp.mean(g_hat * input_f, axis=1, keepdims=True)
    )
    grad_gain = add_all(add_all(grad_gain.reshape(-1, LN), "rep"), "shard").reshape(width)
    all_gain = lax.dynamic_slice_in_dim(grad_gain, shard_at * norm_gain.shape[0], norm_gain.shape[0])
    all_early, all_late = (everyone(early), everyone(late))
    all_out = all_early[:, held:].reshape(n_rep, pieces, part, chans).transpose(0, 2, 1, 3)
    all_out = all_out.reshape(wide, width).astype(F32)
    if part % LN:
        all_in = jnp.stack([all_late[:, :held], all_early[:, :held]], axis=0)
        all_in = all_in.reshape(2, n_rep, -1, n_shard, part).transpose(2, 0, 3, 1, 4)
        all_in = all_in.reshape(in_proj.shape).astype(F32)
    else:
        all_in = spread(all_early, *in_proj.shape, part, 1, [])
        all_in = spread(all_late, *in_proj.shape, part, 0, [all_in])
    all_small = all_late[:, held:].reshape(n_rep, lanes, part, LN).transpose(0, 2, 1, 3)
    all_small = all_small.reshape(wide, lanes * LN).astype(F32)
    return (
        activations,
        input_grad,
        all_gain,
        all_in,
        all_small[:, ends[2]:ends[3]].T,
        all_small[:, ends[3]],
        all_small[:, :ends[0]],
        all_small[:, ends[0]:ends[1]].T,
        all_small[:, ends[4]],
        all_small[:, ends[1]:ends[2]].T,
        all_small[:, ends[5]],
        all_out,
    )


def solution(mesh):
    tokens = P(("rep", "shard"), None)
    rows, cols, line, full = (P("shard", None), P(None, "shard"), P("shard"), P())
    return jax.shard_map(
        on_device,
        mesh=mesh,
        in_specs=(tokens, tokens, full, full, line, rows, cols, line, rows, cols, line, cols, line, rows),
        out_specs=(tokens, tokens, line, rows, cols, line, rows, cols, line, cols, line, rows),
        check_vma=False,
    )
```

time: 1150 us -> 1080 us (0.939)
  Pallas kernels: 347 us -> 410 us
  waiting for transfers between devices: 280 us -> 229 us
  other arithmetic: 130 us -> 87.2 us
  local copies, waits for them, and re-layouts: 97.1 us -> 68.5 us
    ppermute x16 -> x27, waiting for transfers between devices: 153 us -> 39 us  [swap(): lax.ppermute(value, 'rep', [(i, i ^ flip) for i in range(lax.axis_size('r...]
    pallas_call x3 -> x8, Pallas kernels: 279 us -> 358 us  [the longest x2 187 us: bwd_pass(): pl.pallas_call(partial(bwd_kernel, U, n_in), grid=(Q, 1, NC), in_specs=[r...]
    ppermute x16 -> x10, waiting for transfers between devices: 28.8 us -> 106 us  [shifted(): lax.ppermute(value, 'shard', [(i, i + steps) for i in range(first, last)])]
    reduce_scatter x3 -> x2, waiting for transfers between devices: 0.01 us -> 41.2 us  [scatter(): return lax.psum_scatter(value, 'shard', scatter_dimension=0, tiled=True)]
    all_gather x3 -> x2, waiting for transfers between devices: 53.6 us -> 18.4 us  [everyone(): return lax.all_gather(value, 'rep', axis=0)]
    convert_element_type x8 -> x6, other arithmetic: 48.7 us -> 17.4 us  [the longest x3 8.74 us: rep_near(): return (parts[0] + near[0], (parts[2] + near[1]).astype(BF16))]
    convert_element_type x3, local copies, waits for them, and re-layouts: 22.8 us -> 3.68 us  [the longest x1 3.24 us: on_device(): all_out = all_out.reshape(wide, width).astype(F32)]
    all_gather x1 -> x2, waiting for transfers between devices: 32.9 us -> 15.9 us  [the longest x1 15.9 us: on_device(): conv_w = lax.all_gather(in_conv, 'shard', axis=0, tiled=True)]
  transfers between devices with their start and end apart: 41 -> 49, of which waited for: 20 -> 24; matrix products, arithmetic and copies ran while one was open for 25% -> 22% of each run, Pallas kernels for 3% -> 23%
where the time goes in v2:
time: 1080 us; the launch traced here: 1070 us
  Pallas kernels  410 us (38%)
  waiting for transfers between devices  229 us (21%)
  matrix products  154 us (14%)
  other arithmetic  87.2 us (8%)
  local copies, waits for them, and re-layouts  68.5 us (6%)
  starting transfers between devices  63 us (6%)
  blocking collectives  38.2 us (4%)
  between operations  15.8 us (1%)
    pallas_call x2, Pallas kernels, bwd_pass(): pl.pallas_call(partial(bwd_kernel, U, n_in), grid=(Q, 1, NC), in_specs=[r...  187 us
    pallas_call x1, Pallas kernels, fwd_pass(): pl.pallas_call(partial(fwd_kernel, U), grid=(Q, NE, NC), in_specs=[row, r...  130 us
    ppermute x10, waiting for transfers between devices, shifted(): lax.ppermute(value, 'shard', [(i, i + steps) for i in range(first, last)])  106 us
    dot_general x7, matrix products, contract_rows(): lax.dot_general(left, right, (((0,), (0,)), ((), ())), preferred_element_...  53.7 us
    dot_general x6, matrix products, contract_cols(): lax.dot_general(left, right, (((1,), (1,)), ((), ())), preferred_element_...  49.8 us
    ppermute x10, starting transfers between devices, shifted(): lax.ppermute(value, 'shard', [(i, i + steps) for i in range(first, last)])  42.1 us
    reduce_scatter x2, waiting for transfers between devices, scatter(): return lax.psum_scatter(value, 'shard', scatter_dimension=0, tiled=True)  41.2 us
    ppermute x27, waiting for transfers between devices, swap(): lax.ppermute(value, 'rep', [(i, i ^ flip) for i in range(lax.axis_size('r...  39 us
  transfers between devices with their start and end apart: 49, of which 24 were waited for; matrix products, arithmetic and copies ran while one was open for 22% of the time, Pallas kernels for 23%

profile of v2, /device:TPU:0, one launch (start us, length us, event | category | flops | bytes accessed | tf_op | source)
XLA Modules:
  0.0 1065.6 jit_solution(394231784536466875)
XLA Ops:
  20.6 38.2 %all_gather.24 = bf16[1024,313]{0,1:T(8,128)(2,1)S(1)} all-gather(bf16[128,313]{0,1:T(8,128)(2,1)S(1)} %concatenate.58), channel_id=1, replica_groups=mesh['rep'=4,'shard'=8] {'shard'}, dimensions={0}, use_global_device_ids=true | all-gather | bytes 721152 | tf_op jit(solution)/shard_map/all_gather | solution.py:502
  80.3 15.9 %all-gather.8.cloned.1.call-done = bf16[2048,1024]{1,0:T(8,128)(2,1)} async-done(((bf16[256,1024]{1,0:T(8,128)(2,1)}), bf16[2048,1024]{1,0:T(8,128)(2,1)}) %all-gather.8.cloned.1.call-update) | async-done | bytes 4194320 | tf_op jit(solution)/shard_map/all_gather | solution.py:503
  96.2 14.8 %convolution_convert_fusion.x_ref.refs_3_ = bf16[2048,1024]{1,0:T(8,128)(2,1)S(1)} fusion(bf16[2048,1024]{1,0:T(8,128)(2,1)} %all-gather.8.cloned.1.call-done, bf16[512,2048]{1,0:T(8,128)(2,1)} %get-tuple-element.107, bf16[512,2048]{1,0:T(8,128)(2,1)} %get-tuple-element.106, bf16[512,2048]{1,0:T(8,128)(2,1)} %get-tuple-element.105, ...), kind=kOutput, calls=%fused_computation.55 | convolution fusion | flops 8625586176 | bytes 16777216 | tf_op jit(solution)/shard_map/dot_general | solution.py:524
  117.7 14.5 %conv_pass.1.x_ref.refs_1_ = bf16[2048,1024]{1,0:T(8,128)(2,1)} custom-call(bf16[2048,1024]{1,0:T(8,128)(2,1)} %copy-done.6, f32[4,8,1024]{2,1,0:T(8,128)} %concatenate.60.edge_ref.refs_4_, f32[5,1024]{1,0:T(8,128)} %convert_bitcast_fusion.1.w_ref.refs_5_), custom_call_target="tpu_custom_call" | custom-call | flops 25165824 | bytes 8388608 | tf_op jit(solution)/shard_map/conv_pass/pallas_call | solution.py:300
  180.7 37.8 %first_pass.1 = f32[4,16,1024]{2,1,0:T(8,128)} custom-call(f32[2048,1024]{1,0:T(8,128)} %get-tuple-element.113.dt_ref.refs_0_, bf16[2048,1024]{1,0:T(8,128)(2,1)} %conv_pass.1.x_ref.refs_1_, f32[2048,16,128]{2,1,0:T(8,128)} %broadcast_in_dim.25.b_ref.refs_3_, f32[16,1024]{1,0:T(8,128)} %broadcast_multiply_fusion.7.a_ref.refs_5_), custom_call_target="tpu_custom_call" | custom-call | flops 167772160 | bytes 20971520 | tf_op jit(solution)/shard_map/first_pass/pallas_call | solution.py:45
  260.9 14.5 %fusion.90.gg_ref = f32[2048,1024]{1,0:T(8,128)} fusion(bf16[2048,2048]{1,0:T(8,128)(2,1)} %pad_maximum_fusion.1, bf16[1024,2048]{1,0:T(8,128)(2,1)} %all-gather.12.cloned.1.call-done), kind=kOutput, calls=%fused_computation.203 | convolution fusion | flops 8589934592 | bytes 20971520 | tf_op jit(solution)/shard_map/dot_general | solution.py:380
  275.5 10.0 collective-permute-start.16
  285.6 16.5 %fusion.75.gate_ref = f32[2048,1024]{1,0:T(8,128)} fusion(bf16[2048,1024]{1,0:T(8,128)(2,1)} %all-gather.10.cloned.1.call-done, bf16[512,2048]{1,0:T(8,128)(2,1)} %get-tuple-element.107, bf16[512,2048]{1,0:T(8,128)(2,1)} %get-tuple-element.106, bf16[512,2048]{1,0:T(8,128)(2,1)} %get-tuple-element.105, bf16[512,2048]{1,0:T(8,128)(2,1)} %get-tuple-element.104), kind=kOutput, calls=%fused_computation.188 | convolution fusion | flops 8623489024 | bytes 20971520 | tf_op jit(solution)/shard_map/dot_general | solution.py:539
  312.1 129.8 %fwd_pass.1 = (bf16[2048,1024]{1,0:T(8,128)(2,1)}, bf16[2048,1024]{1,0:T(8,128)(2,1)}, f32[2048,1024]{1,0:T(8,128)}, f32[32,16,1024]{2,1,0:T(8,128)}, f32[4,16,1024]{2,1,0:T(8,128)}) custom-call(f32[2048,1024]{1,0:T(8,128)} %get-tuple-element.113.dt_ref.refs_0_, bf16[2048,1024]{1,0:T(8,128)(2,1)} %conv_pass.1.x_ref.refs_1_, f32[2048,1024]{1,0:T(8,128)} %fusion.75.gate_ref, ...), custom_call_target="tpu_custom_call" | custom-call | flops 369098752 | bytes 46137344 | tf_op jit(solution)/shard_map/fwd_pass/pallas_call | solution.py:116
  442.0 9.5 fusion.33
  459.7 9.8 convolution_convert_fusion.2
  477.9 15.2 %fusion.87 = (bf16[2048,2048]{1,0:T(8,128)(2,1)S(1)}, f32[2048,2048]{1,0:T(8,128)}) fusion(bf16[2048,1024]{1,0:T(8,128)(2,1)} %get-tuple-element.45, bf16[1024,2048]{1,0:T(8,128)(2,1)} %all-gather.12.cloned.1.call-done), kind=kOutput, calls=%fused_computation.200 | convolution fusion | flops 8594128896 | bytes 33554432 | tf_op jit(solution)/shard_map/dot_general | solution.py:552
  496.1 12.1 %collective-permute-done.20 = f32[4,17,1024]{2,1,0:T(8,128)S(1)} collective-permute-done((f32[4,17,1024]{2,1,0:T(8,128)S(1)}, f32[4,17,1024]{2,1,0:T(8,128)S(1)}, u32[]{:S(2)}, u32[]{:S(2)}) %collective-permute-start.20) | collective-permute-done | bytes 278560 | tf_op jit(solution)/shard_map/ppermute | solution.py:390
  509.7 29.4 %collective-permute-done.21 = f32[4,17,1024]{2,1,0:T(8,128)S(1)} collective-permute-done((f32[4,17,1024]{2,1,0:T(8,128)S(1)}, f32[4,17,1024]{2,1,0:T(8,128)S(1)}, u32[]{:S(2)}, u32[]{:S(2)}) %collective-permute-start.21) | collective-permute-done | bytes 278560 | tf_op jit(solution)/shard_map/ppermute | solution.py:390
  547.2 30.3 %collective-permute-done.22 = f32[4,17,1024]{2,1,0:T(8,128)S(1)} collective-permute-done((f32[4,17,1024]{2,1,0:T(8,128)S(1)}, f32[4,17,1024]{2,1,0:T(8,128)S(1)}, u32[]{:S(2)}, u32[]{:S(2)}) %collective-permute-start.22) | collective-permute-done | bytes 278560 | tf_op jit(solution)/shard_map/ppermute | solution.py:390
  579.0 20.1 %collective-permute-done.23 = f32[4,17,1024]{2,1,0:T(8,128)S(1)} collective-permute-done((f32[4,17,1024]{2,1,0:T(8,128)S(1)}, f32[4,17,1024]{2,1,0:T(8,128)S(1)}, u32[]{:S(2)}, u32[]{:S(2)}) %collective-permute-start.23) | collective-permute-done | bytes 278560 | tf_op jit(solution)/shard_map/ppermute | solution.py:390
  599.9 93.6 %bwd_pass.2 = (bf16[2048,1024]{1,0:T(8,128)(2,1)}, f32[2048,1024]{1,0:T(8,128)}, f32[2,1,32768]{2,1,0:T(1,128)}, f32[2,1,32768]{2,1,0:T(1,128)}, f32[4,16,1024]{2,1,0:T(8,128)}, /*index=5*/f32[4,2,1024]{2,1,0:T(2,128)}) custom-call(f32[2048,1024]{1,0:T(8,128)} %get-tuple-element.113.dt_ref.refs_0_, bf16[2048,1024]{1,0:T(8,128)(2,1)} %conv_pass.1.x_ref.refs_1_, ...), custom_call_target="tpu_custom_call" | custom-call | flops 335544320 | bytes 23068672 | tf_op jit(solution)/shard_map/bwd_pass/pallas_call | solution.py:223
  700.6 93.5 %bwd_pass.3 = (bf16[2048,1024]{1,0:T(8,128)(2,1)}, f32[2048,1024]{1,0:T(8,128)}, f32[2,1,32768]{2,1,0:T(1,128)}, f32[2,1,32768]{2,1,0:T(1,128)}, f32[4,16,1024]{2,1,0:T(8,128)}, /*index=5*/f32[4,2,1024]{2,1,0:T(2,128)}) custom-call(f32[2048,1024]{1,0:T(8,128)} %get-tuple-element.113.dt_r, ...), custom_call_target="tpu_custom_call", output_to_operand_aliasing={{0}: (9, {}), {1}: (10, {}), {2}: (11, {}), {3}: (12, {}), ... | custom-call | flops 335544320 | bytes 23068672 | tf_op jit(solution)/shard_map/bwd_pass/pallas_call | solution.py:223
  810.3 11.1 %collective-permute-done.26 = f32[160,512]{0,1:T(8,128)} collective-permute-done((f32[160,512]{0,1:T(8,128)}, f32[160,512]{0,1:T(8,128)}, u32[]{:S(2)}, u32[]{:S(2)}) %collective-permute-start.26) | collective-permute-done | bytes 327712 | tf_op jit(solution)/shard_map/ppermute | solution.py:384
  839.7 24.2 %conv_back.1 = (bf16[2048,1024]{1,0:T(8,128)(2,1)}, f32[4,8,1024]{2,1,0:T(8,128)}, f32[4,8,1024]{2,1,0:T(8,128)}, f32[4,5,1024]{2,1,0:T(8,128)}) custom-call(bf16[2048,160]{1,0:T(8,128)(2,1)} %fusion.47.refs_0_, bf16[1024,160]{1,0:T(8,128)(2,1)} %copy.45.refs_1_, f32[2048,1024]{1,0:T(8,128)} %get-tuple-element.59.refs_2_, bf16[2048,1024]{1,0:T(8,128)(2,1)} %copy-done.6, ...), custom_call_target="tpu_custom_call" | custom-call | flops 838860800 | bytes 20971520 | tf_op jit(solution)/shard_map/conv_back/pallas_call | solution.py:350
  872.4 12.7 %convolution_convert_fusion.1 = bf16[2048,1024]{1,0:T(8,128)(2,1)S(1)} fusion(bf16[2048,1024]{1,0:T(8,128)(2,1)} %bitcast.156, bf16[512,2048]{1,0:T(8,128)(2,1)} %get-tuple-element.107, bf16[512,2048]{1,0:T(8,128)(2,1)} %get-tuple-element.106, bf16[512,2048]{1,0:T(8,128)(2,1)} %get-tuple-element.105, bf16[512,2048]{1,0:T(8,128)(2,1)} %get-tuple-element.104), kind=kOutput, calls=%fused_computation.56 | convolution fusion | flops 8625586176 | bytes 16777216 | tf_op jit(solution)/shard_map/dot_general | solution.py:376
  923.8 9.8 fusion.89
  944.4 41.1 %reduce-scatter.5.cloned.1.call-done = bf16[304,1024]{1,0:T(8,128)(2,1)} async-done(((bf16[2432,1024]{1,0:T(8,128)(2,1)}), bf16[304,1024]{1,0:T(8,128)(2,1)}) %reduce-scatter.5.cloned.1.call-update) | async-done | bytes 622608 | tf_op jit(solution)/shard_map/reduce_scatter | solution.py:566
  1036.8 10.7 %all-gather.14.cloned.1.call-done = bf16[1216,1024]{1,0:T(8,128)(2,1)} async-done(((bf16[304,1024]{1,0:T(8,128)(2,1)}), bf16[1216,1024]{1,0:T(8,128)(2,1)}) %all-gather.14.cloned.1.call-update) | async-done | bytes 2490384 | tf_op jit(solution)/shard_map/all_gather | solution.py:569
  (341 shorter events, 334.7 us)
Async XLA Ops:
  7.2 89.0 %all-gather.8.cloned.1.call-start = ((), (), s32[]{:S(2)}) async-start(), calls=%async_computation.2 | async-start | bytes 4718592 | tf_op jit(solution)/shard_map/all_gather | solution.py:503
  9.8 251.1 %all-gather.12.cloned.1.call-start = ((), (), s32[]{:S(2)}) async-start(), calls=%async_computation.4 | async-start | bytes 4718592 | tf_op jit(solution)/shard_map/all_gather | solution.py:505
  11.8 273.8 %all-gather.10.cloned.1.call-start = ((), (), s32[]{:S(2)}) async-start(), calls=%async_computation.3 | async-start | bytes 4718592 | tf_op jit(solution)/shard_map/all_gather | solution.py:504
  11.8 49.6 %collective-permute-start.1 = (bf16[512,2048]{1,0:T(8,128)(2,1)S(1)}, bf16[512,2048]{1,0:T(8,128)(2,1)}, u32[]{:S(2)}, u32[]{:S(2)}) collective-permute-start(bf16[512,2048]{1,0:T(8,128)(2,1)S(1)} %copy-done.2), channel_id=1, source_target_pairs={{0,16},{8,24},{16,0},{24,8},{1,17},{9,25},{17,1},{25,9},{2,18},{10... | collective-permute-start | bytes 6291464 | tf_op jit(solution)/shard_map/ppermute | solution.py:384
  14.9 53.1 %collective-permute-start = (bf16[512,2048]{1,0:T(8,128)(2,1)S(1)}, bf16[512,2048]{1,0:T(8,128)(2,1)}, u32[]{:S(2)}, u32[]{:S(2)}) collective-permute-start(bf16[512,2048]{1,0:T(8,128)(2,1)S(1)} %copy-done.2), channel_id=1, source_target_pairs={{0,8},{8,0},{16,24},{24,16},{1,9},{9,1},{17,25},{25,17},{2,10},{10... | collective-permute-start | bytes 6291464 | tf_op jit(solution)/shard_map/ppermute | solution.py:384
  14.9 125.9 %collective-permute-start.11 = (bf16[512,2048]{1,0:T(8,128)(2,1)}, bf16[512,2048]{1,0:T(8,128)(2,1)}, u32[]{:S(2)}, u32[]{:S(2)}) collective-permute-start(bf16[512,2048]{1,0:T(8,128)(2,1)} %param.17), channel_id=1, source_target_pairs={{0,16},{8,24},{16,0},{24,8},{1,17},{9,25},{17,1},{25,9},{2,18},{10... | collective-permute-start | bytes 6291464 | tf_op jit(solution)/shard_map/ppermute | solution.py:384
  15.0 142.4 %collective-permute-start.10 = (bf16[512,2048]{1,0:T(8,128)(2,1)}, bf16[512,2048]{1,0:T(8,128)(2,1)}, u32[]{:S(2)}, u32[]{:S(2)}) collective-permute-start(bf16[512,2048]{1,0:T(8,128)(2,1)} %param.17), channel_id=1, source_target_pairs={{0,8},{8,0},{16,24},{24,16},{1,9},{9,1},{17,25},{25,17},{2,10},{10... | collective-permute-start | bytes 6291464 | tf_op jit(solution)/shard_map/ppermute | solution.py:384
  17.7 822.0 %reduce-scatter.3.cloned.1.call-start = ((), (), s32[]{:S(2)}) async-start(), calls=%async_computation.5 | async-start | bytes 9437184 | tf_op jit(solution)/shard_map/reduce_scatter | solution.py:566
  140.8 83.7 %collective-permute-start.12 = (bf16[512,2048]{1,0:T(8,128)(2,1)}, bf16[512,2048]{1,0:T(8,128)(2,1)}, u32[]{:S(2)}, u32[]{:S(2)}) collective-permute-start(bf16[512,2048]{1,0:T(8,128)(2,1)} %collective-permute-done.11), channel_id=1, source_target_pairs={{0,8},{8,0},{16,24},{24,16},{1,9},{9,1},{17,25},{25,17},{2,10},{10... | collective-permute-start | bytes 6291464 | tf_op jit(solution)/shard_map/ppermute | solution.py:384
  252.4 23.0 %collective-permute-start.15 = (f32[4,17,1024]{2,1,0:T(8,128)S(1)}, f32[4,17,1024]{2,1,0:T(8,128)S(1)}, u32[]{:S(2)}, u32[]{:S(2)}) collective-permute-start(f32[4,17,1024]{2,1,0:T(8,128)S(1)} %pad_maximum_fusion.10), channel_id=1, source_target_pairs={{0,2},{1,3},{2,4},{3,5},{4,6},{5,7},{8,10},{9,11},{10,12},{11,13},... | collective-permute-start | bytes 835592 | tf_op jit(solution)/shard_map/ppermute | solution.py:390
  275.5 26.9 %collective-permute-start.16 = (f32[4,17,1024]{2,1,0:T(8,128)S(1)}, f32[4,17,1024]{2,1,0:T(8,128)S(1)}, u32[]{:S(2)}, u32[]{:S(2)}) collective-permute-start(f32[4,17,1024]{2,1,0:T(8,128)S(1)} %pad_maximum_fusion.11), channel_id=1, source_target_pairs={{0,4},{1,5},{2,6},{3,7},{8,12},{9,13},{10,14},{11,15},{16,20},{17,... | collective-permute-start | bytes 835592 | tf_op jit(solution)/shard_map/ppermute | solution.py:390
  477.9 507.6 %reduce-scatter.5.cloned.1.call-start = ((), (), s32[]{:S(2)}) async-start(), calls=%async_computation.6 | async-start | bytes 5603328 | tf_op jit(solution)/shard_map/reduce_scatter | solution.py:566
  494.8 44.3 %collective-permute-start.18 = (bf16[512,2048]{1,0:T(8,128)(2,1)S(1)}, bf16[512,2048]{1,0:T(8,128)(2,1)}, u32[]{:S(2)}, u32[]{:S(2)}) collective-permute-start(bf16[512,2048]{1,0:T(8,128)(2,1)S(1)} %get-tuple-element.77), channel_id=1, source_target_pairs={{0,8},{8,0},{16,24},{24,16},{1,9},{9,1},{17,25},{25,17},{2,10},{10... | collective-permute-start | bytes 6291464 | tf_op jit(solution)/shard_map/ppermute | solution.py:384
  508.3 30.8 %collective-permute-start.21 = (f32[4,17,1024]{2,1,0:T(8,128)S(1)}, f32[4,17,1024]{2,1,0:T(8,128)S(1)}, u32[]{:S(2)}, u32[]{:S(2)}) collective-permute-start(f32[4,17,1024]{2,1,0:T(8,128)S(1)} %broadcast_multiply_fusion.2), channel_id=1, source_target_pairs={{1,0},{2,1},{3,2},{4,3},{5,4},{6,5},{7,6},{9,8},{10,9},{11,10},{12... | collective-permute-start | bytes 835592 | tf_op jit(solution)/shard_map/ppermute | solution.py:390
  509.6 183.9 %collective-permute-start.17 = (bf16[512,2048]{1,0:T(8,128)(2,1)}, bf16[512,2048]{1,0:T(8,128)(2,1)}, u32[]{:S(2)}, u32[]{:S(2)}) collective-permute-start(bf16[512,2048]{1,0:T(8,128)(2,1)} %get-tuple-element.76), channel_id=1, source_target_pairs={{0,8},{8,0},{16,24},{24,16},{1,9},{9,1},{17,25},{25,17},{2,10},{10... | collective-permute-start | bytes 6291464 | tf_op jit(solution)/shard_map/ppermute | solution.py:384
  544.0 149.4 %collective-permute-start.19 = (bf16[512,2048]{1,0:T(8,128)(2,1)}, bf16[512,2048]{1,0:T(8,128)(2,1)}, u32[]{:S(2)}, u32[]{:S(2)}) collective-permute-start(bf16[512,2048]{1,0:T(8,128)(2,1)} %fusion.23.refs_10_), channel_id=1, source_target_pairs={{0,16},{8,24},{16,0},{24,8},{1,17},{9,25},{17,1},{25,9},{2,18},{10... | collective-permute-start | bytes 6291464 | tf_op jit(solution)/shard_map/ppermute | solution.py:384
  545.7 31.8 %collective-permute-start.22 = (f32[4,17,1024]{2,1,0:T(8,128)S(1)}, f32[4,17,1024]{2,1,0:T(8,128)S(1)}, u32[]{:S(2)}, u32[]{:S(2)}) collective-permute-start(f32[4,17,1024]{2,1,0:T(8,128)S(1)} %pad_maximum_fusion.12), channel_id=1, source_target_pairs={{2,0},{3,1},{4,2},{5,3},{6,4},{7,5},{10,8},{11,9},{12,10},{13,11},... | collective-permute-start | bytes 835592 | tf_op jit(solution)/shard_map/ppermute | solution.py:390
  888.1 133.2 %all-gather.16.cloned.1.call-start = ((), (), s32[]{:S(2)}) async-start(), calls=%async_computation.8 | async-start | bytes 5242880 | tf_op jit(solution)/shard_map/all_gather | solution.py:569
  892.3 155.2 %all-gather.14.cloned.1.call-start = ((), (), s32[]{:S(2)}) async-start(), calls=%async_computation.7 | async-start | bytes 3112960 | tf_op jit(solution)/shard_map/all_gather | solution.py:569
  912.6 25.9 %collective-permute-start.35 = (bf16[256,2048]{1,0:T(8,128)(2,1)}, bf16[256,2048]{1,0:T(8,128)(2,1)}, u32[]{:S(2)}, u32[]{:S(2)}) collective-permute-start(bf16[256,2048]{1,0:T(8,128)(2,1)} %get-tuple-element.85), channel_id=1, source_target_pairs={{0,8},{8,0},{16,24},{24,16},{1,9},{9,1},{17,25},{25,17},{2,10},{10... | collective-permute-start | bytes 3145736 | tf_op jit(solution)/shard_map/ppermute | solution.py:384
  938.0 47.5 %collective-permute-start.34 = (bf16[256,2048]{1,0:T(8,128)(2,1)S(1)}, bf16[256,2048]{1,0:T(8,128)(2,1)S(1)}, u32[]{:S(2)}, u32[]{:S(2)}) collective-permute-start(bf16[256,2048]{1,0:T(8,128)(2,1)S(1)} %get-tuple-element.84), channel_id=1, source_target_pairs={{0,8},{8,0},{16,24},{24,16},{1,9},{9,1},{17,25},{25,17},{2,10},{10... | collective-permute-start | bytes 3145736 | tf_op jit(solution)/shard_map/ppermute | solution.py:384
  941.0 44.5 %collective-permute-start.36 = (bf16[256,2048]{1,0:T(8,128)(2,1)}, bf16[256,2048]{1,0:T(8,128)(2,1)S(1)}, u32[]{:S(2)}, u32[]{:S(2)}) collective-permute-start(bf16[256,2048]{1,0:T(8,128)(2,1)} %fusion.26), channel_id=1, source_target_pairs={{0,16},{8,24},{16,0},{24,8},{1,17},{9,25},{17,1},{25,9},{2,18},{10... | collective-permute-start | bytes 3145736 | tf_op jit(solution)/shard_map/ppermute | solution.py:384
  942.3 45.4 %collective-permute-start.31 = (bf16[256,2048]{1,0:T(8,128)(2,1)}, bf16[256,2048]{1,0:T(8,128)(2,1)}, u32[]{:S(2)}, u32[]{:S(2)}) collective-permute-start(bf16[256,2048]{1,0:T(8,128)(2,1)} %get-tuple-element.78), channel_id=1, source_target_pairs={{0,8},{8,0},{16,24},{24,16},{1,9},{9,1},{17,25},{25,17},{2,10},{10... | collective-permute-start | bytes 3145736 | tf_op jit(solution)/shard_map/ppermute | solution.py:384
  943.5 45.4 %collective-permute-start.33 = (bf16[256,2048]{1,0:T(8,128)(2,1)}, bf16[256,2048]{1,0:T(8,128)(2,1)}, u32[]{:S(2)}, u32[]{:S(2)}) collective-permute-start(bf16[256,2048]{1,0:T(8,128)(2,1)} %fusion.28), channel_id=1, source_target_pairs={{0,16},{8,24},{16,0},{24,8},{1,17},{9,25},{17,1},{25,9},{2,18},{10... | collective-permute-start | bytes 3145736 | tf_op jit(solution)/shard_map/ppermute | solution.py:384
  (73 other events, 934.6 us)
Sparse Core Ops, SparseCore 0:
  10.7 85.4 all-gather.7
  98.3 72.0 all-gather.11
  172.5 71.2 all-gather.9
  478.0 168.3 reduce-scatter.2
  888.2 97.2 reduce-scatter.4
  986.9 34.2 all-gather.15
  1022.8 24.6 all-gather.13

commit v3 on v2

--- a/solution.py
+++ b/solution.py
@@ -57,7 +57,7 @@
 def sums(tb):
     return (lax.broadcasted_iota(jnp.int32,(tb,tb*8),1)//8 == lax.broadcasted_iota(jnp.int32,(tb,tb*8),0)).astype(BF16)
 
-def fwd_kernel(U, dt_ref, x_ref, gate_ref, gg_ref, b_ref, c_ref, a_ref, skip_ref, h0_ref,
+def fwd_kernel(U, TB, dt_ref, x_ref, gate_ref, gg_ref, b_ref, c_ref, a_ref, skip_ref, h0_ref,
                out_ref, gz_ref, g_ref, ck_ref, adj_ref, h_s, p_s, r_s, q_s, y_s, dtx_s):
     TC, EG = dt_ref.shape
     NT = EG//LN
@@ -65,19 +65,14 @@
     @pl.when(c == 0)
     def _():
         h_s[...] = h0_ref[...]; p_s[...] = jnp.ones_like(p_s); r_s[...] = jnp.zeros_like(r_s)
-        q_s[...] = jnp.zeros_like(q_s)
     ck_ref[...] = h_s[...]
     dtx_s[...] = dt_ref[...]*x_ref[...].astype(F32)
     gate = gate_ref[...]
     g_ref[...] = gg_ref[...]*(gate*jax.nn.sigmoid(gate))
     sl = [slice(j*LN,(j+1)*LN) for j in range(NT)]
     A = [a_ref[:, s] for s in sl]
-    S = sums(U)
     G = TC//U
-    def reduce(i):
-        y_s[pl.ds(pl.multiple_of(i*U,U),U),:] = jnp.dot(S, q_s[...], preferred_element_type=F32)
     def body(i, carry):
-        reduce(jnp.maximum(i-1,0))
         h, p, r = [list(v) for v in carry]
         rows = pl.ds(pl.multiple_of(i*U,U),U)
         dv, xv, gv = dt_ref.at[rows], dtx_s.at[rows], g_ref.at[rows]
@@ -93,11 +88,13 @@
                 q = h[j]*ct
                 q = q[:8]+q[8:]
                 if k % 2 == 0: low[j] = q
-                else: q_s[k*8-8:k*8+8, sl[j]] = jnp.concatenate([low[j],q],axis=0).astype(BF16)
+                else: q_s[pl.ds(pl.multiple_of(i*(U*8)+k*8-8,16),16), sl[j]] = jnp.concatenate([low[j],q],axis=0).astype(BF16)
         return tuple(h), tuple(p), tuple(r)
     init = tuple(tuple(s_[:, s] for s in sl) for s_ in (h_s, p_s, r_s))
     h, p, r = lax.fori_loop(0, G, body, init)
-    reduce(G-1)
+    S = sums(TB)
+    for m in range(0, TC, TB):
+        y_s[m:m+TB,:] = jnp.dot(S, q_s[m*8:(m+TB)*8,:], preferred_element_type=F32)
     for j in range(NT):
         h_s[:, sl[j]] = h[j]; p_s[:, sl[j]] = p[j]; r_s[:, sl[j]] = r[j]
     gate = gate_ref[...]
@@ -108,22 +105,22 @@
     @pl.when(c == pl.num_programs(2)-1)
     def _(): adj_ref[...] = r_s[...]
 
-def fwd_pass(dt, x, gate, gg, bx, cx, a2, skip, h0, Q, TC=64, EG=512, U=8):
+def fwd_pass(dt, x, gate, gg, bx, cx, a2, skip, h0, Q, TC=128, EG=512, U=8, TB=32):
     T,E = dt.shape; N = a2.shape[0]; L=T//Q; NC=L//TC; NE=E//EG
     row = pl.BlockSpec((TC,EG), lambda q,e,c:(q*NC+c, e))
     sp = pl.BlockSpec((TC,N,LN), lambda q,e,c:(q*NC+c,0,0))
     st = pl.BlockSpec((None,N,EG), lambda q,e,c:(q,0,e))
-    return pl.pallas_call(partial(fwd_kernel,U), grid=(Q,NE,NC),
+    return pl.pallas_call(partial(fwd_kernel,U,TB), grid=(Q,NE,NC),
         in_specs=[row,row,row,row,sp,sp,pl.BlockSpec((N,EG), lambda q,e,c:(0,e)), pl.BlockSpec((1,EG), lambda q,e,c:(0,e)), st],
         out_specs=[row, row, row, pl.BlockSpec((None,N,EG), lambda q,e,c:(q*NC+c,0,e)), st],
         out_shape=[jax.ShapeDtypeStruct((T,E),BF16)]*2 + [jax.ShapeDtypeStruct((T,E),F32),
             jax.ShapeDtypeStruct((Q*NC,N,E),F32), jax.ShapeDtypeStruct((Q,N,E),F32)],
-        scratch_shapes=[pltpu.VMEM((N,EG),F32)]*3 + [pltpu.VMEM((U*8,EG),BF16)] + [pltpu.VMEM((TC,EG),F32)]*2,
+        scratch_shapes=[pltpu.VMEM((N,EG),F32)]*3 + [pltpu.VMEM((TC*8,EG),BF16)] + [pltpu.VMEM((TC,EG),F32)]*2,
         compiler_params=pltpu.CompilerParams(dimension_semantics=("arbitrary",)*3, vmem_limit_bytes=60<<20),
         name="fwd_pass",
         cost_estimate=pl.CostEstimate(flops=11*T*E*N, bytes_accessed=22*T*E, transcendentals=T*E*N))(dt,x,gate,gg,bx,cx,a2,skip,h0)
 
-def bwd_kernel(U, n_in, *refs):
+def bwd_kernel(U, TB, n_in, *refs):
     dt_ref, x_ref, g_ref, b_ref, c_ref, a_ref, skip_ref, ck_ref, mu0_ref = refs[:9]
     (gl_ref, gx_ref, gb_ref, gc_ref, ga_ref, su_ref,
      mu_s, ga_s, su_s, qa_s, qb_s, zb_s, zc_s, sa_s, sb_s, dtx_s, a_s, h_s) = refs[n_in:]
@@ -134,7 +131,7 @@
     @pl.when(c == 0)
     def _():
         mu_s[...] = mu0_ref[...]
-        for v in (ga_s, su_s, qa_s, qb_s, zb_s, zc_s): v[...] = jnp.zeros_like(v)
+        for v in (ga_s, su_s): v[...] = jnp.zeros_like(v)
     dtx_s[...] = dt_ref[...]*x_ref[...].astype(F32)
     sl = [slice(j*LN,(j+1)*LN) for j in range(NT)]
     A = [a_ref[:, s] for s in sl]
@@ -154,19 +151,8 @@
                 h_s[t+1, :, sl[j]] = h[j]
         return tuple(h)
     h = lax.fori_loop(0, G, up, tuple(ck_ref[:, s] for s in sl))
-    S = sums(U)
-    ones = jnp.ones((8,LN),BF16)
-    nt = (((1,),(1,)),((),()))
-    def reduce(i):
-        rows = pl.ds(pl.multiple_of(i*U,U),U)
-        sa_s[rows,:] = jnp.dot(S, qa_s[...], preferred_element_type=F32)
-        sb_s[rows,:] = jnp.dot(S, qb_s[...], preferred_element_type=F32)
-        cols = pl.ds(pl.multiple_of(i*(U*N),U*N),U*N)
-        gb_ref[:,cols] = lax.dot_general(ones, zb_s[...], nt, preferred_element_type=F32)[:1]
-        gc_ref[:,cols] = lax.dot_general(ones, zc_s[...], nt, preferred_element_type=F32)[:1]
     def down(ii, carry):
         i = G-1-ii
-        reduce(jnp.minimum(i+1,G-1))
         mu, ga, h = [list(v) for v in carry]
         rows = pl.ds(pl.multiple_of(i*U,U),U)
         dv, gv, xv = dt_ref.at[rows], g_ref.at[rows], dtx_s.at[rows]
@@ -192,14 +178,23 @@
                 qb = qb[:8]+qb[8:]
                 if k % 2: la[j], lb[j] = qa, qb
                 else:
-                    qa_s[k*8:k*8+16, sl[j]] = jnp.concatenate([qa,la[j]],axis=0).astype(BF16)
-                    qb_s[k*8:k*8+16, sl[j]] = jnp.concatenate([qb,lb[j]],axis=0).astype(BF16)
-            zb_s[k*N:k*N+N,:] = zb.astype(BF16)
-            zc_s[k*N:k*N+N,:] = zc.astype(BF16)
+                    r16 = pl.ds(pl.multiple_of(i*(U*8)+k*8,16),16)
+                    qa_s[r16, sl[j]] = jnp.concatenate([qa,la[j]],axis=0).astype(BF16)
+                    qb_s[r16, sl[j]] = jnp.concatenate([qb,lb[j]],axis=0).astype(BF16)
+            rn = pl.ds(pl.multiple_of(t*N,N),N)
+            zb_s[rn,:] = zb.astype(BF16)
+            zc_s[rn,:] = zc.astype(BF16)
         return tuple(mu), tuple(ga), tuple(h)
     init = tuple(tuple(s_[:, s] for s in sl) for s_ in (mu_s, ga_s)) + (h,)
     mu, ga, h = lax.fori_loop(0, G, down, init)
-    reduce(0)
+    S = sums(TB)
+    for m in range(0, TC, TB):
+        sa_s[m:m+TB,:] = jnp.dot(S, qa_s[m*8:(m+TB)*8,:], preferred_element_type=F32)
+        sb_s[m:m+TB,:] = jnp.dot(S, qb_s[m*8:(m+TB)*8,:], preferred_element_type=F32)
+    ones = jnp.ones((8,LN),BF16)
+    nt = (((1,),(1,)),((),()))
+    gb_ref[...] = lax.dot_general(ones, zb_s[...], nt, preferred_element_type=F32)[:1]
+    gc_ref[...] = lax.dot_general(ones, zc_s[...], nt, preferred_element_type=F32)[:1]
     for j in range(NT): ga_s[:, sl[j]] = ga[j]; mu_s[:, sl[j]] = mu[j]
     d = dt_ref[...]; x = x_ref[...].astype(F32); g = g_ref[...]
     sb = sb_s[...]
@@ -212,7 +207,7 @@
     def _():
         ga_ref[...] = ga_s[...]; su_ref[...] = su_s[...]
 
-def bwd_pass(dt, x, g, bx, cx, a2, skip, ck, mu0, Q, at, prev, waits, TC=64, EG=512, U=8):
+def bwd_pass(dt, x, g, bx, cx, a2, skip, ck, mu0, Q, at, prev, waits, TC=128, EG=512, U=8, TB=32):
     T,E = dt.shape; N = a2.shape[0]; L=T//Q; NC=L//TC; NE=E//EG
     row = pl.BlockSpec((TC,EG), lambda q,e,c:(q*NC+NC-1-c, at))
     sp = pl.BlockSpec((TC,N,LN), lambda q,e,c:(q*NC+NC-1-c,0,0))
@@ -220,14 +215,14 @@
     nb = pl.BlockSpec((None,1,TC*N), lambda q,e,c:(at,0,q*NC+NC-1-c))
     args = (dt,x,g,bx,cx,a2,skip,ck,mu0)
     n_in = len(args)+len(prev)+len(waits)
-    return pl.pallas_call(partial(bwd_kernel,U,n_in), grid=(Q,1,NC),
+    return pl.pallas_call(partial(bwd_kernel,U,TB,n_in), grid=(Q,1,NC),
         in_specs=[row,row,row,sp,sp,pl.BlockSpec((N,EG), lambda q,e,c:(0,at)), pl.BlockSpec((1,EG), lambda q,e,c:(0,at)),
             pl.BlockSpec((None,N,EG), lambda q,e,c:(q*NC+NC-1-c,0,at)), st]+[pl.BlockSpec(memory_space=pl.ANY)]*(len(prev)+len(waits)),
         out_specs=[row,row,nb,nb,st,pl.BlockSpec((None,2,EG), lambda q,e,c:(q,0,at))],
         out_shape=[jax.ShapeDtypeStruct((T,E),BF16), jax.ShapeDtypeStruct((T,E),F32)]+[jax.ShapeDtypeStruct((NE,1,T*N),F32)]*2
             +[jax.ShapeDtypeStruct((Q,N,E),F32), jax.ShapeDtypeStruct((Q,2,E),F32)],
         input_output_aliases={len(args)+i: i for i in range(len(prev))},
-        scratch_shapes=[pltpu.VMEM((N,EG),F32)]*2+[pltpu.VMEM((2,EG),F32)]+[pltpu.VMEM((U*8,EG),BF16)]*2+[pltpu.VMEM((U*N,LN),BF16)]*2
+        scratch_shapes=[pltpu.VMEM((N,EG),F32)]*2+[pltpu.VMEM((2,EG),F32)]+[pltpu.VMEM((TC*8,EG),BF16)]*2+[pltpu.VMEM((TC*N,LN),BF16)]*2
             +[pltpu.VMEM((TC,EG),F32)]*3+[pltpu.VMEM((TC,N,EG),F32), pltpu.VMEM((TC+1,N,EG),F32)],
         compiler_params=pltpu.CompilerParams(dimension_semantics=("arbitrary",)*3, vmem_limit_bytes=62<<20),
         name="bwd_pass",
@@ -422,19 +417,41 @@
     return value
 
 
-def carry_in(total, state, rates, place, reverse):
-    sign = -1 if reverse else 1
-    span = lax.axis_size("shard")
-    both = shifted(jnp.concatenate([state, total[:, None, :]], axis=1), sign)
-    both = both * jnp.where(place >= 1, 1.0, 0.0)
-    step = 1
-    while step < min(span, 8):
-        far = shifted(both, sign * step) * jnp.where(place >= step, 1.0, 0.0)
-        total = both[:, -1:]
-        state = both[:, :-1] + jnp.exp(rates[None] * total) * far[:, :-1]
-        both = jnp.concatenate([state, total + far[:, -1:]], axis=1)
-        step *= 2
-    return both[:, :-1]
+def carry_in(total, state, rates, place, span, reverse):
+    if span == 1:
+        return jnp.zeros_like(state)
+    n_rep, states, chans = state.shape
+    count = lax.axis_size("shard")
+    group = 2 if span % 2 == 0 else 1
+
+    def moved(total, state, target):
+        sent = jnp.concatenate([state.reshape(n_rep * states, chans), total], axis=0).astype(BF16)
+        pairs = [(i, target(i)) for i in range(count)]
+        pairs = [(i, j) for i, j in pairs if 0 <= j < count and i // span == j // span]
+        got = lax.ppermute(sent, "shard", pairs).astype(F32)
+        return got[n_rep * states:], got[:n_rep * states].reshape(state.shape)
+
+    def decay(amount):
+        return jnp.exp(rates[None] * amount[:, None, :])
+
+    second = place % group == 1
+    if group == 2:
+        other_total, other_state = moved(total, state, lambda i: i ^ 1)
+        first_state, last_state = jnp.where(second, other_state, state), jnp.where(second, state, other_state)
+        last_total = jnp.where(second, total, other_total)
+        block_state = decay(last_total) * first_state + last_state
+        block_total = total + other_total
+    else:
+        block_total, block_state = (total, state)
+    step = -group if reverse else group
+    got = [moved(block_total, block_state, lambda i, k=k: i + k * step) for k in range(1, span // group)]
+    start, gone = (jnp.zeros_like(state), jnp.zeros_like(total))
+    for far_total, far_state in got:
+        start = start + decay(gone) * far_state
+        gone = gone + far_total
+    if group == 2:
+        start = jnp.where(second, decay(other_total) * start + other_state, start)
+    return start
 
 
 def on_device(
@@ -544,11 +561,11 @@
     skip = skip_all[None, :]
     local_end = first_pass(step, conv_out, b_all, rates2, n_rep)
     total = jnp.sum(step.reshape(n_rep, rows, chans), axis=1)
-    start_state = carry_in(total, local_end, rates, in_slot, False)
+    start_state = carry_in(total, local_end, rates, in_slot, span, False)
     gated, g_gate, g_scanned, kept, local_adj = fwd_pass(
         step, conv_out, gate_in, g_gated, b_all, c_all, rates2, skip, start_state, n_rep
     )
-    end_grad = carry_in(total, local_adj, rates, span - 1 - in_slot, True)
+    end_grad = carry_in(total, local_adj, rates, span - 1 - in_slot, span, True)
     branch = jnp.dot(gated, out_all, preferred_element_type=F32)
     near, other = rep_near([branch[k * rows:(k + 1) * rows] for k in range(n_rep)])
     pieces = width // chans
@@ -558,6 +575,7 @@
         piece = contract_rows(gated, back[:, k * chans:(k + 1) * chans])
         local.append(piece.astype(BF16).reshape(n_shard, part, chans))
     local = jnp.concatenate(local, axis=1).reshape(-1, chans)
+    local, other, end_grad = lax.optimization_barrier((local, other, end_grad))
     branch = rep_far(near, other)
     input_f = block_input.astype(F32)
     activations = (input_f + valid[0] * branch).astype(BF16)
@@ -583,8 +601,10 @@
         rep_sum([g_proj[:, k * rows:(k + 1) * rows] for k in range(n_rep)]), axis=1
     )
     g_proj = g_proj.T.astype(BF16)
+    early, g_proj = lax.optimization_barrier((early, g_proj))
+    all_early = everyone(early)
     grad_x_proj = contract_rows(conv_out, g_proj)
-    g_in, head, tail, grad_wb = conv_back(g_proj, xproj_all, g_scan_in, conv_in, edge, wb, [early], n_rep)
+    g_in, head, tail, grad_wb = conv_back(g_proj, xproj_all, g_scan_in, conv_in, edge, wb, [], n_rep)
     after = shifted(head, -1) * keep_next
     joined = jnp.concatenate([jnp.zeros_like(after), after], axis=1)
     fix = tail
@@ -600,7 +620,9 @@
     lanes = small.shape[2]
     small = small.transpose(0, 2, 1, 3).reshape(n_shard, -1, chans)
     late = contract_rows(normed, g_in).astype(BF16).reshape(n_shard, held, chans)
-    late = scatter(jnp.concatenate([late, small], axis=1).reshape(-1, chans))
+    late = jnp.concatenate([late, small], axis=1).reshape(-1, chans)
+    late, all_early = lax.optimization_barrier((late, all_early))
+    late = scatter(late)
     half = rows // 2
     g_normed = []
     for at in (0, half):
@@ -619,7 +641,7 @@
     )
     grad_gain = add_all(add_all(grad_gain.reshape(-1, LN), "rep"), "shard").reshape(width)
     all_gain = lax.dynamic_slice_in_dim(grad_gain, shard_at * norm_gain.shape[0], norm_gain.shape[0])
-    all_early, all_late = (everyone(early), everyone(late))
+    all_late = everyone(late)
     all_out = all_early[:, held:].reshape(n_rep, pieces, part, chans).transpose(0, 2, 1, 3)
     all_out = all_out.reshape(wide, width).astype(F32)
     if part % LN:

time: 1080 us -> 837 us (0.78)
  Pallas kernels: 410 us -> 302 us
  waiting for transfers between devices: 229 us -> 123 us
    pallas_call x3, Pallas kernels: 317 us -> 208 us  [the longest x2 133 us: bwd_pass(): pl.pallas_call(partial(bwd_kernel, U, TB, n_in), grid=(Q, 1, NC), in_spec...]
    ppermute x10 -> x2, waiting for transfers between devices: 106 us -> 1.71 us  [shifted(): lax.ppermute(value, 'shard', [(i, i + steps) for i in range(first, last)])]
    ppermute x10 -> x2, starting transfers between devices: 42.1 us -> 4.14 us  [shifted(): lax.ppermute(value, 'shard', [(i, i + steps) for i in range(first, last)])]
    ppermute x0 -> x8, starting transfers between devices: none -> 28.9 us  [moved(): got = lax.ppermute(sent, 'shard', pairs).astype(F32)]
    all_gather x2, waiting for transfers between devices: 18.4 us -> 0.01 us  [everyone(): return lax.all_gather(value, 'rep', axis=0)]
    ppermute x0 -> x8, waiting for transfers between devices: none -> 11 us  [moved(): got = lax.ppermute(sent, 'shard', pairs).astype(F32)]
  transfers between devices with their start and end apart: 49 -> 49, of which waited for: 24 -> 18; matrix products, arithmetic and copies ran while one was open for 22% -> 27% of each run, Pallas kernels for 23% -> 26%
where the time goes in v3:
time: 837 us; the launch traced here: 827 us
  Pallas kernels  302 us (36%)
  matrix products  153 us (18%)
  waiting for transfers between devices  123 us (15%)
  other arithmetic  77.5 us (9%)
  local copies, waits for them, and re-layouts  64.3 us (8%)
  starting transfers between devices  53.4 us (6%)
  blocking collectives  37.8 us (5%)
  between operations  16.1 us (2%)
    pallas_call x2, Pallas kernels, bwd_pass(): pl.pallas_call(partial(bwd_kernel, U, TB, n_in), grid=(Q, 1, NC), in_spec...  133 us
    pallas_call x1, Pallas kernels, fwd_pass(): pl.pallas_call(partial(fwd_kernel, U, TB), grid=(Q, NE, NC), in_specs=[ro...  75.1 us
    dot_general x7, matrix products, contract_rows(): lax.dot_general(left, right, (((0,), (0,)), ((), ())), preferred_element_...  51.8 us
    dot_general x6, matrix products, contract_cols(): lax.dot_general(left, right, (((1,), (1,)), ((), ())), preferred_element_...  49.8 us
    reduce_scatter x2, waiting for transfers between devices, scatter(): return lax.psum_scatter(value, 'shard', scatter_dimension=0, tiled=True)  47 us
    ppermute x27, waiting for transfers between devices, swap(): lax.ppermute(value, 'rep', [(i, i ^ flip) for i in range(lax.axis_size('r...  40.6 us
    pallas_call x1, Pallas kernels, first_pass(): pl.pallas_call(partial(first_kernel, U), grid=(Q, NE, NC), in_specs=[row,...  37.9 us
    all_gather x1, blocking collectives, on_device(): small_all = lax.all_gather(small, 'shard', axis=0, tiled=True)  37.8 us
  transfers between devices with their start and end apart: 49, of which 18 were waited for; matrix products, arithmetic and copies ran while one was open for 27% of the time, Pallas kernels for 26%

profile of v3, /device:TPU:0, one launch (start us, length us, event | category | flops | bytes accessed | tf_op | source)
XLA Modules:
  0.0 827.4 jit_solution(6304597335962523243)
XLA Ops:
  21.5 37.8 %all_gather.24 = bf16[1024,313]{0,1:T(8,128)(2,1)S(1)} all-gather(bf16[128,313]{0,1:T(8,128)(2,1)S(1)} %concatenate.60), channel_id=1, replica_groups=mesh['rep'=4,'shard'=8] {'shard'}, dimensions={0}, use_global_device_ids=true | all-gather | bytes 721152 | tf_op jit(solution)/shard_map/all_gather | solution.py:519
  80.3 15.0 %all-gather.8.cloned.1.call-done = bf16[2048,1024]{1,0:T(8,128)(2,1)} async-done(((bf16[256,1024]{1,0:T(8,128)(2,1)}), bf16[2048,1024]{1,0:T(8,128)(2,1)}) %all-gather.8.cloned.1.call-update) | async-done | bytes 4194320 | tf_op jit(solution)/shard_map/all_gather | solution.py:520
  95.3 14.5 %convolution_convert_fusion.x_ref.refs_3_ = bf16[2048,1024]{1,0:T(8,128)(2,1)S(1)} fusion(bf16[2048,1024]{1,0:T(8,128)(2,1)} %all-gather.8.cloned.1.call-done, bf16[512,2048]{1,0:T(8,128)(2,1)} %get-tuple-element.123, bf16[512,2048]{1,0:T(8,128)(2,1)} %get-tuple-element.122, bf16[512,2048]{1,0:T(8,128)(2,1)} %get-tuple-element.121, ...), kind=kOutput, calls=%fused_computation.55 | convolution fusion | flops 8625586176 | bytes 16777216 | tf_op jit(solution)/shard_map/dot_general | solution.py:541
  116.6 14.5 %conv_pass.1.x_ref.refs_1_ = bf16[2048,1024]{1,0:T(8,128)(2,1)} custom-call(bf16[2048,1024]{1,0:T(8,128)(2,1)} %copy-done.6, f32[4,8,1024]{2,1,0:T(8,128)} %concatenate.62.edge_ref.refs_4_, f32[5,1024]{1,0:T(8,128)} %convert_bitcast_fusion.1.w_ref.refs_5_), custom_call_target="tpu_custom_call" | custom-call | flops 25165824 | bytes 8388608 | tf_op jit(solution)/shard_map/conv_pass/pallas_call | solution.py:295
  168.5 9.0 %broadcast_in_dim.23.b_ref.refs_3_ = f32[2048,16,128]{2,1,0:T(8,128)} broadcast(f32[2048,16]{1,0:T(8,128)S(1)} %copy.42), dimensions={0,1} | broadcast | bytes 16908288 | tf_op jit(solution)/shard_map/broadcast_in_dim | solution.py:551
  177.6 37.9 %first_pass.1 = f32[4,16,1024]{2,1,0:T(8,128)} custom-call(f32[2048,1024]{1,0:T(8,128)} %get-tuple-element.129.dt_ref.refs_0_, bf16[2048,1024]{1,0:T(8,128)(2,1)} %conv_pass.1.x_ref.refs_1_, f32[2048,16,128]{2,1,0:T(8,128)} %broadcast_in_dim.23.b_ref.refs_3_, f32[16,1024]{1,0:T(8,128)} %get-tuple-element.110.a_ref.refs_5_), custom_call_target="tpu_custom_call" | custom-call | flops 167772160 | bytes 20971520 | tf_op jit(solution)/shard_map/first_pass/pallas_call | solution.py:45
  219.3 14.5 %fusion.82.gg_ref = f32[2048,1024]{1,0:T(8,128)} fusion(bf16[2048,2048]{1,0:T(8,128)(2,1)} %pad_maximum_fusion.1, bf16[1024,2048]{1,0:T(8,128)(2,1)} %all-gather.12.cloned.1.call-done), kind=kOutput, calls=%fused_computation.184 | convolution fusion | flops 8589934592 | bytes 20971520 | tf_op jit(solution)/shard_map/dot_general | solution.py:375
  234.0 15.6 %collective-permute-start.15 = (bf16[68,1024]{1,0:T(8,128)(2,1)S(1)}, bf16[68,1024]{1,0:T(8,128)(2,1)S(1)}, u32[]{:S(2)}, u32[]{:S(2)}) collective-permute-start(bf16[68,1024]{1,0:T(8,128)(2,1)S(1)} %pad_maximum_fusion.9), channel_id=1, source_target_pairs={{0,4},{1,5},{2,6},{3,7},{8,12},{9,13},{10,14},{11,15},{16,20},{17,... | collective-permute-start | bytes 417800 | tf_op jit(solution)/shard_map/ppermute | solution.py:431
  252.3 16.5 %fusion.67.gate_ref = f32[2048,1024]{1,0:T(8,128)} fusion(bf16[2048,1024]{1,0:T(8,128)(2,1)} %all-gather.10.cloned.1.call-done, bf16[512,2048]{1,0:T(8,128)(2,1)} %get-tuple-element.123, bf16[512,2048]{1,0:T(8,128)(2,1)} %get-tuple-element.122, bf16[512,2048]{1,0:T(8,128)(2,1)} %get-tuple-element.121, bf16[512,2048]{1,0:T(8,128)(2,1)} %get-tuple-element.120), kind=kOutput, calls=%fused_computation.169 | convolution fusion | flops 8623489024 | bytes 20971520 | tf_op jit(solution)/shard_map/dot_general | solution.py:556
  275.8 9.0 %broadcast_in_dim.24.c_ref.refs_4_ = f32[2048,16,128]{2,1,0:T(8,128)} broadcast(f32[2048,16]{1,0:T(8,128)S(1)} %copy.43), dimensions={0,1} | broadcast | bytes 16908288 | tf_op jit(solution)/shard_map/broadcast_in_dim | solution.py:552
  284.8 75.1 %fwd_pass.1 = (bf16[2048,1024]{1,0:T(8,128)(2,1)}, bf16[2048,1024]{1,0:T(8,128)(2,1)}, f32[2048,1024]{1,0:T(8,128)}, f32[16,16,1024]{2,1,0:T(8,128)}, f32[4,16,1024]{2,1,0:T(8,128)}) custom-call(f32[2048,1024]{1,0:T(8,128)} %get-tuple-element.129.dt_ref.refs_0_, bf16[2048,1024]{1,0:T(8,128)(2,1)} %conv_pass.1.x_ref.refs_1_, f32[2048,1024]{1,0:T(8,128)} %fusion.67.gate_ref, ...), custom_call_target="tpu_custom_call" | custom-call | flops 369098752 | bytes 46137344 | tf_op jit(solution)/shard_map/fwd_pass/pallas_call | solution.py:113
  359.9 9.5 %fusion.33 = bf16[1024,1024]{1,0:T(8,128)(2,1)} fusion(bf16[2048,1024]{1,0:T(8,128)(2,1)} %get-tuple-element.52, bf16[2048,2048]{1,0:T(8,128)(2,1)} %pad_maximum_fusion.1), kind=kOutput, calls=%fused_computation.68 | convolution fusion | flops 4296015872 | bytes 10485760 | tf_op jit(solution)/shard_map/dot_general | solution.py:371
  369.4 11.4 %convolution_convert_fusion.2 = bf16[2048,1024]{1,0:T(8,128)(2,1)S(1)} fusion(bf16[2048,1024]{1,0:T(8,128)(2,1)S(1)} %copy-done.11, bf16[512,2048]{1,0:T(8,128)(2,1)} %get-tuple-element.123, bf16[512,2048]{1,0:T(8,128)(2,1)} %get-tuple-element.122, bf16[512,2048]{1,0:T(8,128)(2,1)} %get-tuple-element.121, bf16[512,2048]{1,0:T(8,128)(2,1)S(1)} %copy-done.15), kind=kOutput, calls=%fused_computation.57 | convolution fusion | flops 8625586176 | bytes 16777216 | tf_op jit(solution)/shard_map/dot_general | solution.py:371
  380.8 17.0 %fusion.79 = (bf16[2048,2048]{1,0:T(8,128)(2,1)}, f32[2048,2048]{1,0:T(8,128)}) fusion(bf16[2048,1024]{1,0:T(8,128)(2,1)} %get-tuple-element.52, bf16[1024,2048]{1,0:T(8,128)(2,1)} %all-gather.12.cloned.1.call-done), kind=kOutput, calls=%fused_computation.181 | convolution fusion | flops 8594128896 | bytes 33554432 | tf_op jit(solution)/shard_map/dot_general | solution.py:569
  416.4 7.7 collective-permute-done.21
  431.1 66.8 %bwd_pass.2 = (bf16[2048,1024]{1,0:T(8,128)(2,1)}, f32[2048,1024]{1,0:T(8,128)}, f32[2,1,32768]{2,1,0:T(1,128)}, f32[2,1,32768]{2,1,0:T(1,128)}, f32[4,16,1024]{2,1,0:T(8,128)}, /*index=5*/f32[4,2,1024]{2,1,0:T(2,128)}) custom-call(f32[2048,1024]{1,0:T(8,128)} %get-tuple-element.129.dt_ref.refs_0_, bf16[2048,1024]{1,0:T(8,128)(2,1)} %conv_pass.1.x_ref.refs_1_, ...), custom_call_target="tpu_custom_call" | custom-call | flops 335544320 | bytes 23068672 | tf_op jit(solution)/shard_map/bwd_pass/pallas_call | solution.py:218
  505.4 66.3 %bwd_pass.3 = (bf16[2048,1024]{1,0:T(8,128)(2,1)}, f32[2048,1024]{1,0:T(8,128)}, f32[2,1,32768]{2,1,0:T(1,128)}, f32[2,1,32768]{2,1,0:T(1,128)}, f32[4,16,1024]{2,1,0:T(8,128)}, /*index=5*/f32[4,2,1024]{2,1,0:T(2,128)}) custom-call(f32[2048,1024]{1,0:T(8,128)} %get-tuple-element.129.dt_r, ...), custom_call_target="tpu_custom_call", output_to_operand_aliasing={{0}: (9, {}), {1}: (10, {}), {2}: (11, {}), {3}: (12, {}), ... | custom-call | flops 335544320 | bytes 23068672 | tf_op jit(solution)/shard_map/bwd_pass/pallas_call | solution.py:218
  581.7 13.4 %collective-permute-done.26 = f32[160,512]{0,1:T(8,128)S(1)} collective-permute-done((f32[160,512]{0,1:T(8,128)S(1)}, f32[160,512]{0,1:T(8,128)S(1)}, u32[]{:S(2)}, u32[]{:S(2)}) %collective-permute-start.26) | collective-permute-done | bytes 327712 | tf_op jit(solution)/shard_map/ppermute | solution.py:379
  595.8 12.5 %collective-permute-done.28 = f32[160,512]{0,1:T(8,128)S(1)} collective-permute-done((f32[160,512]{0,1:T(8,128)S(1)}, f32[160,512]{0,1:T(8,128)S(1)}, u32[]{:S(2)}, u32[]{:S(2)}) %collective-permute-start.28) | collective-permute-done | bytes 327712 | tf_op jit(solution)/shard_map/ppermute | solution.py:379
  616.2 24.4 %conv_back.1 = (bf16[2048,1024]{1,0:T(8,128)(2,1)}, f32[4,8,1024]{2,1,0:T(8,128)}, f32[4,8,1024]{2,1,0:T(8,128)}, f32[4,5,1024]{2,1,0:T(8,128)}) custom-call(bf16[2048,160]{1,0:T(8,128)(2,1)} %maximum_bitcast_fusion.refs_0_, bf16[1024,160]{1,0:T(8,128)(2,1)} %copy.45.refs_1_, f32[2048,1024]{1,0:T(8,128)} %get-tuple-element.70.refs_2_, ...), custom_call_target="tpu_custom_call" | custom-call | flops 838860800 | bytes 20971520 | tf_op jit(solution)/shard_map/conv_back/pallas_call | solution.py:345
  649.1 12.7 %convolution_convert_fusion.1 = bf16[2048,1024]{1,0:T(8,128)(2,1)S(1)} fusion(bf16[2048,1024]{1,0:T(8,128)(2,1)} %bitcast.157, bf16[512,2048]{1,0:T(8,128)(2,1)} %get-tuple-element.123, bf16[512,2048]{1,0:T(8,128)(2,1)} %get-tuple-element.122, bf16[512,2048]{1,0:T(8,128)(2,1)} %get-tuple-element.121, bf16[512,2048]{1,0:T(8,128)(2,1)} %get-tuple-element.120), kind=kOutput, calls=%fused_computation.56 | convolution fusion | flops 8625586176 | bytes 16777216 | tf_op jit(solution)/shard_map/dot_general | solution.py:371
  677.4 8.3 fusion.80
  697.8 9.8 %fusion.81 = (bf16[1024,2048]{1,0:T(8,128)(2,1)}, f32[1024,2048]{1,0:T(8,128)S(1)}) fusion(f32[1024,2048]{1,0:T(8,128)} %fusion.83, bf16[1024,1024]{1,0:T(8,128)(2,1)S(1)} %bitcast.176, bf16[2048,1024]{1,0:T(8,128)(2,1)} %all-gather.10.cloned.1.call-done), kind=kOutput, calls=%fused_computation.183 | convolution fusion | flops 4299161600 | bytes 27262976 | tf_op jit(solution)/shard_map/dot_general | solution.py:375
  718.3 47.0 %reduce-scatter.5.cloned.1.call-done = bf16[304,1024]{1,0:T(8,128)(2,1)} async-done(((bf16[2432,1024]{1,0:T(8,128)(2,1)}), bf16[304,1024]{1,0:T(8,128)(2,1)}) %reduce-scatter.5.cloned.1.call-update) | async-done | bytes 622608 | tf_op jit(solution)/shard_map/reduce_scatter | solution.py:584
  (338 shorter events, 245.3 us)
Async XLA Ops:
  7.2 88.1 %all-gather.8.cloned.1.call-start = ((), (), s32[]{:S(2)}) async-start(), calls=%async_computation.2 | async-start | bytes 4718592 | tf_op jit(solution)/shard_map/all_gather | solution.py:520
  9.8 209.5 %all-gather.12.cloned.1.call-start = ((), (), s32[]{:S(2)}) async-start(), calls=%async_computation.4 | async-start | bytes 4718592 | tf_op jit(solution)/shard_map/all_gather | solution.py:522
  11.8 240.5 %all-gather.10.cloned.1.call-start = ((), (), s32[]{:S(2)}) async-start(), calls=%async_computation.3 | async-start | bytes 4718592 | tf_op jit(solution)/shard_map/all_gather | solution.py:521
  11.8 56.2 %collective-permute-start = (bf16[512,2048]{1,0:T(8,128)(2,1)S(1)}, bf16[512,2048]{1,0:T(8,128)(2,1)}, u32[]{:S(2)}, u32[]{:S(2)}) collective-permute-start(bf16[512,2048]{1,0:T(8,128)(2,1)S(1)} %copy-done.2), channel_id=1, source_target_pairs={{0,8},{8,0},{16,24},{24,16},{1,9},{9,1},{17,25},{25,17},{2,10},{10... | collective-permute-start | bytes 6291464 | tf_op jit(solution)/shard_map/ppermute | solution.py:379
  12.4 49.1 %collective-permute-start.1 = (bf16[512,2048]{1,0:T(8,128)(2,1)S(1)}, bf16[512,2048]{1,0:T(8,128)(2,1)}, u32[]{:S(2)}, u32[]{:S(2)}) collective-permute-start(bf16[512,2048]{1,0:T(8,128)(2,1)S(1)} %copy-done.2), channel_id=1, source_target_pairs={{0,16},{8,24},{16,0},{24,8},{1,17},{9,25},{17,1},{25,9},{2,18},{10... | collective-permute-start | bytes 6291464 | tf_op jit(solution)/shard_map/ppermute | solution.py:379
  14.9 100.3 %collective-permute-start.11 = (bf16[512,2048]{1,0:T(8,128)(2,1)}, bf16[512,2048]{1,0:T(8,128)(2,1)}, u32[]{:S(2)}, u32[]{:S(2)}) collective-permute-start(bf16[512,2048]{1,0:T(8,128)(2,1)} %param.17), channel_id=1, source_target_pairs={{0,16},{8,24},{16,0},{24,8},{1,17},{9,25},{17,1},{25,9},{2,18},{10... | collective-permute-start | bytes 6291464 | tf_op jit(solution)/shard_map/ppermute | solution.py:379
  15.0 124.2 %collective-permute-start.10 = (bf16[512,2048]{1,0:T(8,128)(2,1)}, bf16[512,2048]{1,0:T(8,128)(2,1)}, u32[]{:S(2)}, u32[]{:S(2)}) collective-permute-start(bf16[512,2048]{1,0:T(8,128)(2,1)} %param.17), channel_id=1, source_target_pairs={{0,8},{8,0},{16,24},{24,16},{1,9},{9,1},{17,25},{25,17},{2,10},{10... | collective-permute-start | bytes 6291464 | tf_op jit(solution)/shard_map/ppermute | solution.py:379
  17.5 593.7 %reduce-scatter.3.cloned.1.call-start = ((), (), s32[]{:S(2)}) async-start(), calls=%async_computation.5 | async-start | bytes 9437184 | tf_op jit(solution)/shard_map/reduce_scatter | solution.py:584
  115.3 33.7 %collective-permute-start.12 = (bf16[512,2048]{1,0:T(8,128)(2,1)}, bf16[512,2048]{1,0:T(8,128)(2,1)}, u32[]{:S(2)}, u32[]{:S(2)}) collective-permute-start(bf16[512,2048]{1,0:T(8,128)(2,1)} %collective-permute-done.11), channel_id=1, source_target_pairs={{0,8},{8,0},{16,24},{24,16},{1,9},{9,1},{17,25},{25,17},{2,10},{10... | collective-permute-start | bytes 6291464 | tf_op jit(solution)/shard_map/ppermute | solution.py:379
  216.4 17.4 %collective-permute-start.13 = (bf16[68,1024]{1,0:T(8,128)(2,1)S(1)}, bf16[68,1024]{1,0:T(8,128)(2,1)S(1)}, u32[]{:S(2)}, u32[]{:S(2)}) collective-permute-start(bf16[68,1024]{1,0:T(8,128)(2,1)S(1)} %pad_maximum_fusion.8), channel_id=1, source_target_pairs={{0,1},{1,0},{2,3},{3,2},{4,5},{5,4},{6,7},{7,6},{8,9},{9,8},{10,11... | collective-permute-start | bytes 417800 | tf_op jit(solution)/shard_map/ppermute | solution.py:431
  234.0 38.3 %collective-permute-start.15 = (bf16[68,1024]{1,0:T(8,128)(2,1)S(1)}, bf16[68,1024]{1,0:T(8,128)(2,1)S(1)}, u32[]{:S(2)}, u32[]{:S(2)}) collective-permute-start(bf16[68,1024]{1,0:T(8,128)(2,1)S(1)} %pad_maximum_fusion.9), channel_id=1, source_target_pairs={{0,4},{1,5},{2,6},{3,7},{8,12},{9,13},{10,14},{11,15},{16,20},{17,... | collective-permute-start | bytes 417800 | tf_op jit(solution)/shard_map/ppermute | solution.py:431
  249.6 22.8 %collective-permute-start.14 = (bf16[68,1024]{1,0:T(8,128)(2,1)S(1)}, bf16[68,1024]{1,0:T(8,128)(2,1)S(1)}, u32[]{:S(2)}, u32[]{:S(2)}) collective-permute-start(bf16[68,1024]{1,0:T(8,128)(2,1)S(1)} %pad_maximum_fusion.9), channel_id=1, source_target_pairs={{0,2},{1,3},{2,4},{3,5},{4,6},{5,7},{8,10},{9,11},{10,12},{11,13},... | collective-permute-start | bytes 417800 | tf_op jit(solution)/shard_map/ppermute | solution.py:431
  401.9 23.2 %collective-permute-start.18 = (bf16[512,2048]{1,0:T(8,128)(2,1)S(1)}, bf16[512,2048]{1,0:T(8,128)(2,1)S(1)}, u32[]{:S(2)}, u32[]{:S(2)}) collective-permute-start(bf16[512,2048]{1,0:T(8,128)(2,1)S(1)} %get-tuple-element.91), channel_id=1, source_target_pairs={{0,8},{8,0},{16,24},{24,16},{1,9},{9,1},{17,25},{25,17},{2,10},{10... | collective-permute-start | bytes 6291464 | tf_op jit(solution)/shard_map/ppermute | solution.py:379
  408.5 15.8 %collective-permute-start.22 = (bf16[68,1024]{1,0:T(8,128)(2,1)S(1)}, bf16[68,1024]{1,0:T(8,128)(2,1)S(1)}, u32[]{:S(2)}, u32[]{:S(2)}) collective-permute-start(bf16[68,1024]{1,0:T(8,128)(2,1)S(1)} %pad_maximum_fusion.10), channel_id=1, source_target_pairs={{6,0},{7,1},{14,8},{15,9},{22,16},{23,17},{30,24},{31,25}} | collective-permute-start | bytes 417800 | tf_op jit(solution)/shard_map/ppermute | solution.py:431
  429.5 235.2 %all-gather.14.cloned.1.call-start = ((), (), s32[]{:S(2)}) async-start(), calls=%async_computation.7 | async-start | bytes 5242880 | tf_op jit(solution)/shard_map/all_gather | solution.py:587
  429.5 68.4 %collective-permute-start.17 = (bf16[512,2048]{1,0:T(8,128)(2,1)}, bf16[512,2048]{1,0:T(8,128)(2,1)}, u32[]{:S(2)}, u32[]{:S(2)}) collective-permute-start(bf16[512,2048]{1,0:T(8,128)(2,1)} %get-tuple-element.90), channel_id=1, source_target_pairs={{0,8},{8,0},{16,24},{24,16},{1,9},{9,1},{17,25},{25,17},{2,10},{10... | collective-permute-start | bytes 6291464 | tf_op jit(solution)/shard_map/ppermute | solution.py:379
  429.6 68.4 %collective-permute-start.23 = (bf16[512,2048]{1,0:T(8,128)(2,1)}, bf16[512,2048]{1,0:T(8,128)(2,1)}, u32[]{:S(2)}, u32[]{:S(2)}) collective-permute-start(bf16[512,2048]{1,0:T(8,128)(2,1)} %fusion.19.refs_10_), channel_id=1, source_target_pairs={{0,16},{8,24},{16,0},{24,8},{1,17},{9,25},{17,1},{25,9},{2,18},{10... | collective-permute-start | bytes 6291464 | tf_op jit(solution)/shard_map/ppermute | solution.py:379
  611.2 154.1 %reduce-scatter.5.cloned.1.call-start = ((), (), s32[]{:S(2)}) async-start(), calls=%async_computation.6 | async-start | bytes 5603328 | tf_op jit(solution)/shard_map/reduce_scatter | solution.py:584
  664.7 144.4 %all-gather.16.cloned.1.call-start = ((), (), s32[]{:S(2)}) async-start(), calls=%async_computation.8 | async-start | bytes 3112960 | tf_op jit(solution)/shard_map/all_gather | solution.py:587
  686.8 25.6 %collective-permute-start.35 = (bf16[256,2048]{1,0:T(8,128)(2,1)}, bf16[256,2048]{1,0:T(8,128)(2,1)}, u32[]{:S(2)}, u32[]{:S(2)}) collective-permute-start(bf16[256,2048]{1,0:T(8,128)(2,1)} %get-tuple-element.99), channel_id=1, source_target_pairs={{0,8},{8,0},{16,24},{24,16},{1,9},{9,1},{17,25},{25,17},{2,10},{10... | collective-permute-start | bytes 3145736 | tf_op jit(solution)/shard_map/ppermute | solution.py:379
  712.0 53.4 %collective-permute-start.34 = (bf16[256,2048]{1,0:T(8,128)(2,1)S(1)}, bf16[256,2048]{1,0:T(8,128)(2,1)S(1)}, u32[]{:S(2)}, u32[]{:S(2)}) collective-permute-start(bf16[256,2048]{1,0:T(8,128)(2,1)S(1)} %get-tuple-element.98), channel_id=1, source_target_pairs={{0,8},{8,0},{16,24},{24,16},{1,9},{9,1},{17,25},{25,17},{2,10},{10... | collective-permute-start | bytes 3145736 | tf_op jit(solution)/shard_map/ppermute | solution.py:379
  715.0 50.3 %collective-permute-start.36 = (bf16[256,2048]{1,0:T(8,128)(2,1)}, bf16[256,2048]{1,0:T(8,128)(2,1)}, u32[]{:S(2)}, u32[]{:S(2)}) collective-permute-start(bf16[256,2048]{1,0:T(8,128)(2,1)} %fusion.26), channel_id=1, source_target_pairs={{0,16},{8,24},{16,0},{24,8},{1,17},{9,25},{17,1},{25,9},{2,18},{10... | collective-permute-start | bytes 3145736 | tf_op jit(solution)/shard_map/ppermute | solution.py:379
  715.8 51.9 %collective-permute-start.31 = (bf16[256,2048]{1,0:T(8,128)(2,1)}, bf16[256,2048]{1,0:T(8,128)(2,1)}, u32[]{:S(2)}, u32[]{:S(2)}) collective-permute-start(bf16[256,2048]{1,0:T(8,128)(2,1)} %get-tuple-element.92), channel_id=1, source_target_pairs={{0,8},{8,0},{16,24},{24,16},{1,9},{9,1},{17,25},{25,17},{2,10},{10... | collective-permute-start | bytes 3145736 | tf_op jit(solution)/shard_map/ppermute | solution.py:379
  717.0 50.7 %collective-permute-start.33 = (bf16[256,2048]{1,0:T(8,128)(2,1)}, bf16[256,2048]{1,0:T(8,128)(2,1)}, u32[]{:S(2)}, u32[]{:S(2)}) collective-permute-start(bf16[256,2048]{1,0:T(8,128)(2,1)} %fusion.28), channel_id=1, source_target_pairs={{0,16},{8,24},{16,0},{24,8},{1,17},{9,25},{17,1},{25,9},{2,18},{10... | collective-permute-start | bytes 3145736 | tf_op jit(solution)/shard_map/ppermute | solution.py:379
  (69 other events, 901.4 us)
Sparse Core Ops, SparseCore 0:
  10.7 84.5 all-gather.7
  97.4 72.2 all-gather.11
  171.8 74.7 all-gather.9
  429.6 148.3 reduce-scatter.2
  611.3 34.5 all-gather.13
  664.8 100.4 reduce-scatter.4
  766.9 24.6 all-gather.15

commit v4 on v3

--- a/solution.py
+++ b/solution.py
@@ -9,6 +9,7 @@
 
 EPSILON = 1e-05
 SPAN_TOKENS = 4096
+GROUP = 512
 F32=jnp.float32; BF16=jnp.bfloat16
 LN=128
 def first_kernel(U, dt_ref, x_ref, b_ref, a_ref, hend_ref, h_s, dtx_s):
@@ -37,7 +38,7 @@
     def _():
         hend_ref[...] = h_s[...]
 
-def first_pass(dt, x, bx, a2, Q, TC=128, EG=512, U=8):
+def first_pass(dt, x, bx, a2, Q, TC=256, EG=GROUP, U=8):
     T,E = dt.shape; N = a2.shape[0]; L=T//Q; NC=L//TC; NE=E//EG
     row = pl.BlockSpec((TC,EG), lambda q,e,c:(q*NC+c, e))
     sp = pl.BlockSpec((TC,N,LN), lambda q,e,c:(q*NC+c,0,0))
@@ -105,7 +106,7 @@
     @pl.when(c == pl.num_programs(2)-1)
     def _(): adj_ref[...] = r_s[...]
 
-def fwd_pass(dt, x, gate, gg, bx, cx, a2, skip, h0, Q, TC=128, EG=512, U=8, TB=32):
+def fwd_pass(dt, x, gate, gg, bx, cx, a2, skip, h0, Q, TC=256, EG=GROUP, U=8, TB=32):
     T,E = dt.shape; N = a2.shape[0]; L=T//Q; NC=L//TC; NE=E//EG
     row = pl.BlockSpec((TC,EG), lambda q,e,c:(q*NC+c, e))
     sp = pl.BlockSpec((TC,N,LN), lambda q,e,c:(q*NC+c,0,0))
@@ -207,7 +208,7 @@
     def _():
         ga_ref[...] = ga_s[...]; su_ref[...] = su_s[...]
 
-def bwd_pass(dt, x, g, bx, cx, a2, skip, ck, mu0, Q, at, prev, waits, TC=128, EG=512, U=8, TB=32):
+def bwd_pass(dt, x, g, bx, cx, a2, skip, ck, mu0, Q, at, prev, waits, TC=256, EG=GROUP, U=8, TB=32):
     T,E = dt.shape; N = a2.shape[0]; L=T//Q; NC=L//TC; NE=E//EG
     row = pl.BlockSpec((TC,EG), lambda q,e,c:(q*NC+NC-1-c, at))
     sp = pl.BlockSpec((TC,N,LN), lambda q,e,c:(q*NC+NC-1-c,0,0))
@@ -229,23 +230,31 @@
         cost_estimate=pl.CostEstimate(flops=20*T*EG*N, bytes_accessed=22*T*EG, transcendentals=T*EG*N))(*args,*prev,*waits)
 
 
-def spread_kernel(in_ref, *refs):
-    refs[-1][...] = jnp.concatenate([in_ref[r].astype(F32) for r in range(in_ref.shape[0])], axis=1)
-
-
-def spread(pieces, rows, cols, part, half, prev):
-    n_rep, n_shard = (pieces.shape[0], pieces.shape[2] // part)
+def spread_kernel(count, at_ref, *refs):
+    out_ref = refs[-1]
+    part = out_ref.shape[1] // count
+    for k in range(count):
+        at = pl.multiple_of((at_ref[0] ^ k) * part, part)
+        out_ref[:, pl.ds(at, part)] = refs[k][...].astype(F32)
+
+
+def spread(pieces, at, rows, cols, part, start, prev):
+    count = len(pieces)
+    piece = pl.BlockSpec((rows, part), lambda s, a: (0, s))
     return pl.pallas_call(
-        spread_kernel,
-        grid=(n_shard,),
-        in_specs=[pl.BlockSpec((n_rep, rows, part), lambda s: (0, 0, s))] + [pl.BlockSpec(memory_space=pl.ANY)] * len(prev),
-        out_specs=pl.BlockSpec((rows, n_rep * part), lambda s: (0, half * n_shard + s)),
+        partial(spread_kernel, count),
+        grid_spec=pltpu.PrefetchScalarGridSpec(
+            num_scalar_prefetch=1,
+            grid=(pieces[0].shape[1] // part,),
+            in_specs=[piece] * count + [pl.BlockSpec(memory_space=pl.ANY)] * len(prev),
+            out_specs=pl.BlockSpec((rows, count * part), lambda s, a: (0, start + s)),
+        ),
         out_shape=jax.ShapeDtypeStruct((rows, cols), F32),
-        input_output_aliases={1 + i: i for i in range(len(prev))},
+        input_output_aliases={1 + count + i: i for i in range(len(prev))},
         compiler_params=pltpu.CompilerParams(dimension_semantics=("arbitrary",)),
         name="spread",
         cost_estimate=pl.CostEstimate(flops=0, bytes_accessed=3 * rows * cols, transcendentals=0),
-    )(pieces, *prev)
+    )(at, *pieces, *prev)
 
 
 def pick_kernel(count, at_ref, in_ref, out_ref):
@@ -256,11 +265,11 @@
         out_ref[:, k * part:(k + 1) * part] = in_ref[:, pl.ds(pl.multiple_of(k * wide + at, part), part)]
 
 
-def pick(value, at, n_shard, part, half):
+def pick(value, at, n_rep, n_shard, part, half):
     rows, cols = value.shape
     count = 4 if n_shard % 4 == 0 else n_shard
     steps = n_shard // count
-    wide = cols // (2 * steps)
+    wide = n_rep * part * count
     return pl.pallas_call(
         partial(pick_kernel, count),
         grid_spec=pltpu.PrefetchScalarGridSpec(
@@ -276,7 +285,8 @@
     )(at, value)
 
 
-def conv_kernel(x_ref, edge_ref, w_ref, o_ref, x_s):
+def conv_kernel(x_ref, edge_ref, w_ref, *refs):
+    o_ref, x_s = refs[-2:]
     L = x_ref.shape[0]
     taps = w_ref.shape[0] - 1
     x_s[0:8, :] = edge_ref[...]
@@ -288,9 +298,10 @@
     o_ref[...] = (pre * jax.nn.sigmoid(pre)).astype(BF16)
 
 
-def conv_pass(conv_in, edge, wb, Q, EB=256):
+def conv_pass(conv_in, edge, wb, Q, at, prev, EB=256):
     T, E = conv_in.shape
     L = T // Q
+    at = at * (E // EB)
     row = pl.BlockSpec((L, EB), lambda q, e: (q, e))
     return pl.pallas_call(
         conv_kernel,
@@ -298,20 +309,19 @@
         in_specs=[
             row,
             pl.BlockSpec((None, 8, EB), lambda q, e: (q, 0, e)),
-            pl.BlockSpec((wb.shape[0], EB), lambda q, e: (0, e)),
-        ],
-        out_specs=row,
-        out_shape=jax.ShapeDtypeStruct((T, E), BF16),
+            pl.BlockSpec((wb.shape[0], EB), lambda q, e: (0, at + e)),
+        ] + [pl.BlockSpec(memory_space=pl.ANY)] * len(prev),
+        out_specs=pl.BlockSpec((L, EB), lambda q, e: (q, at + e)),
+        out_shape=jax.ShapeDtypeStruct((T, wb.shape[1]), BF16),
+        input_output_aliases={3 + i: i for i in range(len(prev))},
         scratch_shapes=[pltpu.VMEM((L + 8, EB), F32)],
         compiler_params=pltpu.CompilerParams(dimension_semantics=("arbitrary",) * 2),
         name="conv_pass",
         cost_estimate=pl.CostEstimate(flops=12 * T * E, bytes_accessed=4 * T * E, transcendentals=T * E),
-    )(conv_in, edge, wb)
-
-
-def conv_back_kernel(n_in, *refs):
-    gp_ref, xp_ref, gx_ref, x_ref, edge_ref, w_ref = refs[:6]
-    gi_ref, head_ref, tail_ref, gw_ref, x_s, g_s = refs[n_in:]
+    )(conv_in, edge, wb, *prev)
+
+
+def conv_back_kernel(gp_ref, xp_ref, gx_ref, x_ref, edge_ref, w_ref, gi_ref, head_ref, tail_ref, gw_ref, x_s, g_s):
     L = x_ref.shape[0]
     taps = w_ref.shape[0] - 1
     x_s[0:8, :] = edge_ref[...]
@@ -336,23 +346,24 @@
     tail_ref[...] = g_in[L - 8:, :]
 
 
-def conv_back(g_projected, x_proj, gx, conv_in, edge, wb, waits, Q, EB=256):
+def conv_back(g_projected, x_proj, gx, conv_in, edge, wb, Q, at, EB=256):
     T, E = conv_in.shape
     L = T // Q
+    at = at * (E // EB)
     row = pl.BlockSpec((L, EB), lambda q, e: (q, e))
     edges = pl.BlockSpec((None, 8, EB), lambda q, e: (q, 0, e))
     rows = wb.shape[0]
     return pl.pallas_call(
-        partial(conv_back_kernel, 6 + len(waits)),
+        conv_back_kernel,
         grid=(Q, E // EB),
         in_specs=[
             pl.BlockSpec((L, g_projected.shape[1]), lambda q, e: (q, 0)),
-            pl.BlockSpec((EB, x_proj.shape[1]), lambda q, e: (e, 0)),
-            row,
+            pl.BlockSpec((EB, x_proj.shape[1]), lambda q, e: (at + e, 0)),
+            pl.BlockSpec((L, EB), lambda q, e: (q, at + e)),
             row,
             edges,
-            pl.BlockSpec((rows, EB), lambda q, e: (0, e)),
-        ] + [pl.BlockSpec(memory_space=pl.ANY)] * len(waits),
+            pl.BlockSpec((rows, EB), lambda q, e: (0, at + e)),
+        ],
         out_specs=[row, edges, edges, pl.BlockSpec((None, rows, EB), lambda q, e: (q, 0, e))],
         out_shape=[
             jax.ShapeDtypeStruct((T, E), BF16),
@@ -364,7 +375,7 @@
         compiler_params=pltpu.CompilerParams(dimension_semantics=("arbitrary",) * 2),
         name="conv_back",
         cost_estimate=pl.CostEstimate(flops=400 * T * E, bytes_accessed=10 * T * E, transcendentals=T * E),
-    )(g_projected, x_proj, gx, conv_in, edge, wb, *waits)
+    )(g_projected, x_proj, gx, conv_in, edge, wb)
 
 
 def contract_rows(left, right):
@@ -400,21 +411,52 @@
     return mine + swap(other, 2).astype(F32)
 
 
-def rep_sum(parts):
-    near = [swap(parts[k], 1) for k in (1, 3)]
-    pair = [parts[0] + near[0], parts[2] + near[1]]
-    far = [swap(value, 2) for value in pair]
-    full = [pair[0] + far[1], pair[1] + far[0]]
-    over = [swap(value, 1) for value in full]
-    return [full[0], over[0], full[1], over[1]]
+def rep_sum(value):
+    wide = value.shape[1] // lax.axis_size("rep")
+    parts = [value[:, k * wide:(k + 1) * wide] for k in range(lax.axis_size("rep"))]
+    near = [swap(parts[k].astype(BF16), 1).astype(F32) for k in (1, 3)]
+    pair = [(parts[0] + near[0]).astype(BF16), (parts[2] + near[1]).astype(BF16)]
+    far = [swap(value, 2).astype(F32) for value in pair]
+    full = [pair[0].astype(F32) + far[1], pair[1].astype(F32) + far[0]]
+    over = [swap(value.astype(BF16), 1).astype(F32) for value in full]
+    return jnp.concatenate([full[0], over[0], full[1], over[1]], axis=1)
+
+
+def in_order(pieces, at):
+    def piece(k):
+        flip = at ^ k
+        odd, far = (flip % 2 == 1, flip // 2 == 1)
+        return jnp.where(far, jnp.where(odd, pieces[3], pieces[2]), jnp.where(odd, pieces[1], pieces[0]))
+
+    return [piece(k) for k in range(len(pieces))]
+
+
+def other(value, axis, flip):
+    return lax.ppermute(value, axis, [(i, i ^ flip) for i in range(lax.axis_size(axis))])
 
 
 def add_all(value, axis):
     step = 1
     while step < lax.axis_size(axis):
-        value = value + lax.ppermute(value, axis, [(i, i ^ step) for i in range(lax.axis_size(axis))])
+        pair = value + other(value, axis, step)
+        if step * 4 <= lax.axis_size(axis):
+            far = [other(value, axis, step * k) for k in (2, 3)]
+            pair = pair + (far[0] + far[1])
+            step *= 2
+        value = pair
         step *= 2
     return value
+
+
+def halve(value):
+    step = lax.axis_size("shard") // 2
+    while step:
+        own = lax.axis_index("shard") // step % 2
+        keep = lax.dynamic_slice_in_dim(value, own * step, step, 0)
+        send = lax.dynamic_slice_in_dim(value, (1 - own) * step, step, 0)
+        value = keep + other(send.astype(BF16), "shard", step).astype(F32)
+        step //= 2
+    return value[0]
 
 
 def carry_in(total, state, rates, place, span, reverse):
@@ -495,7 +537,7 @@
     def mine(value, axis):
         return lax.dynamic_slice_in_dim(value, rep_at * part, part, axis)
 
-    x_all = rep_gather(block_input)
+    x_far = swap(block_input, 2)
     small = jnp.concatenate(
         [
             mine(x_proj, 0),
@@ -509,18 +551,22 @@
         ],
         axis=1,
     )
+    groups = chans // GROUP
     if part % LN:
         in_mine = lax.dynamic_index_in_dim(
             in_proj.reshape(in_proj.shape[0], 2, n_shard, n_rep, part), rep_at, 3, keepdims=False
         ).reshape(in_proj.shape[0], 2, chans)
         in_conv, in_gate = (in_mine[:, 0], in_mine[:, 1])
+        in_conv = [in_conv]
     else:
-        in_conv, in_gate = [pick(in_proj, rep_at.reshape(1), n_shard, part, k) for k in range(2)]
+        in_conv = [pick(in_proj, rep_at.reshape(1), n_rep, n_shard, part, 0)]
+        in_gate = pick(in_proj, rep_at.reshape(1), n_rep, n_shard, part, 1)
     small_all = lax.all_gather(small, "shard", axis=0, tiled=True)
-    conv_w = lax.all_gather(in_conv, "shard", axis=0, tiled=True)
+    x_far, small_all = lax.optimization_barrier((x_far, small_all))
+    x_all = [block_input, swap(block_input, 1), x_far, swap(x_far, 1)]
+    conv_w = [lax.all_gather(value, "shard", axis=0, tiled=True) for value in in_conv]
     gate_w = lax.all_gather(in_gate, "shard", axis=0, tiled=True)
     out_all = lax.all_gather(mine(out_proj, 0), "shard", axis=0, tiled=True)
-    cot_all = rep_gather(cotangent)
 
     cut = [x_proj.shape[1], rank, states, taps, 1, 1, 1]
     ends = [sum(cut[:i + 1]) for i in range(len(cut))]
@@ -538,15 +584,19 @@
         return (value * scale * gain_f[None, :]).astype(BF16)
 
     normed = jnp.concatenate([norm(value) for value in x_all], axis=0)
-    conv_in = jnp.dot(normed, conv_w, preferred_element_type=F32).astype(BF16)
-    last = conv_in.reshape(n_rep, rows, chans)[:, rows - (taps - 1):]
-    edge = shifted(last, 1).astype(F32) * keep_prev
-    edge = jnp.concatenate([jnp.zeros((n_rep, 8 - (taps - 1), chans), F32), edge], axis=1)
-    conv_out = conv_pass(conv_in, edge, wb, n_rep)
-    proj = lax.dot_general(xproj_all, conv_out, (((0,), (1,)), ((), ())), preferred_element_type=F32)
-    proj = jnp.concatenate(
-        rep_sum([proj[:, k * rows:(k + 1) * rows] for k in range(n_rep)]), axis=1
-    )
+    cot, normed = lax.optimization_barrier((cotangent, normed))
+    cot_all = rep_gather(cot)
+    conv_in, edge, conv_out = ([], [], [])
+    for k in range(1):
+        if k:
+            normed, conv_out[0] = lax.optimization_barrier((normed, conv_out[0]))
+        conv_in.append(jnp.dot(normed, conv_w[k], preferred_element_type=F32).astype(BF16))
+        last = conv_in[k].reshape(n_rep, rows, chans)[:, rows - (taps - 1):]
+        before = shifted(last, 1).astype(F32) * keep_prev
+        edge.append(jnp.concatenate([jnp.zeros((n_rep, 8 - (taps - 1), chans), F32), before], axis=1))
+        conv_out = [conv_pass(conv_in[k], edge[k], wb, n_rep, k, conv_out)]
+    conv_out = conv_out[0]
+    proj = rep_sum(lax.dot_general(xproj_all, conv_out, (((0,), (1,)), ((), ())), preferred_element_type=F32))
     step_low = proj[:rank].astype(BF16)
     b_all = jnp.broadcast_to(proj[rank:rank + states].T[:, :, None], (tokens, states, LN))
     c_all = jnp.broadcast_to(proj[rank + states:].T[:, :, None], (tokens, states, LN))
@@ -583,12 +633,9 @@
     def scatter(value):
         return lax.psum_scatter(value, "shard", scatter_dimension=0, tiled=True)
 
-    def everyone(value):
-        return lax.all_gather(value, "rep", axis=0)
-
     early = scatter(local)
     back_args = (step, conv_out, g_scanned, b_all, c_all, rates2, skip, kept, end_grad, n_rep)
-    prev, groups = ([], chans // 512)
+    prev = []
     for k in range(groups):
         prev = bwd_pass(*back_args, k, prev, [local, other] if k == 0 else [activations])
     g_lin, g_scan_in, g_b, g_c, g_a, g_sums = prev
@@ -597,39 +644,52 @@
     g_low = contract_cols(dtproj_all, g_lin)
     g_b, g_c = [jnp.sum(v, axis=(0, 1)).reshape(tokens, states).T for v in (g_b, g_c)]
     g_proj = jnp.concatenate([g_low, g_b, g_c], axis=0)
-    g_proj = jnp.concatenate(
-        rep_sum([g_proj[:, k * rows:(k + 1) * rows] for k in range(n_rep)]), axis=1
-    )
-    g_proj = g_proj.T.astype(BF16)
+    g_proj = rep_sum(g_proj).T.astype(BF16)
+    half = rows // 2
+
+    def rows_of(value, at):
+        value = value.reshape(n_rep, rows, -1)[:, at:at + half]
+        return value.reshape(n_rep * half, -1)
+
     early, g_proj = lax.optimization_barrier((early, g_proj))
-    all_early = everyone(early)
+    early = rep_gather(early)
     grad_x_proj = contract_rows(conv_out, g_proj)
-    g_in, head, tail, grad_wb = conv_back(g_proj, xproj_all, g_scan_in, conv_in, edge, wb, [], n_rep)
-    after = shifted(head, -1) * keep_next
-    joined = jnp.concatenate([jnp.zeros_like(after), after], axis=1)
-    fix = tail
-    for k in range(taps - 1):
-        at = taps - 1 - k
-        fix = fix + wb[k][None, None, :] * joined[:, at:at + 8]
-    g_in = g_in.reshape(n_rep, rows, chans).at[:, rows - 8:].set(fix.astype(BF16))
-    g_in = g_in.reshape(tokens, chans)
     grad_a_log = rates * jnp.sum(g_a, axis=0)
-    small = [grad_x_proj, grad_dt_proj, grad_a_log.T, jnp.sum(grad_wb, axis=0).T, grad_dt_bias[:, None], grad_skip[:, None]]
-    small.append(jnp.zeros((chans, -ends[6] % LN), F32))
-    small = jnp.concatenate(small, axis=1).astype(BF16).reshape(n_shard, part, -1, LN)
-    lanes = small.shape[2]
-    small = small.transpose(0, 2, 1, 3).reshape(n_shard, -1, chans)
-    late = contract_rows(normed, g_in).astype(BF16).reshape(n_shard, held, chans)
-    late = jnp.concatenate([late, small], axis=1).reshape(-1, chans)
-    late, all_early = lax.optimization_barrier((late, all_early))
-    late = scatter(late)
-    half = rows // 2
-    g_normed = []
+    g_in, late, grad_wb = ([], [], [])
+    for k in range(1):
+        taps_k = wb[:, k * chans:(k + 1) * chans]
+        out, head, tail, grad_taps = conv_back(g_proj, xproj_all, g_scan_in, conv_in[k], edge[k], wb, n_rep, k)
+        grad_wb.append(jnp.sum(grad_taps, axis=0))
+        after = shifted(head, -1) * keep_next
+        joined = jnp.concatenate([jnp.zeros_like(after), after], axis=1)
+        fix = tail
+        for i in range(taps - 1):
+            at = taps - 1 - i
+            fix = fix + taps_k[i][None, None, :] * joined[:, at:at + 8]
+        out = out.reshape(n_rep, rows, chans).at[:, rows - 8:].set(fix.astype(BF16)).reshape(tokens, chans)
+        grad = contract_rows(normed, out).astype(BF16).reshape(n_shard, held, chans)
+        small = [grad_x_proj, grad_dt_proj, grad_a_log.T, grad_wb[0].T, grad_dt_bias[:, None], grad_skip[:, None]]
+        small.append(jnp.zeros((chans, -ends[6] % LN), F32))
+        small = halve(jnp.concatenate(small, axis=1).reshape(n_shard, part, -1)).astype(BF16)
+        small = rep_gather(small)
+        grad = grad.reshape(-1, chans)
+        g_in.append(out)
+        late.append(scatter(grad))
+    pairs = []
     for at in (0, half):
-        conv_rows = g_in.reshape(n_rep, rows, chans)[:, at:at + half].reshape(n_rep * half, chans)
-        gate_rows = g_gate.reshape(n_rep, rows, chans)[:, at:at + half].reshape(n_rep * half, chans)
-        both = contract_cols(conv_rows, conv_w) + contract_cols(gate_rows, gate_w)
-        g_normed.append(rep_far(*rep_near([both[k * half:(k + 1) * half] for k in range(n_rep)])))
+        both = contract_cols(rows_of(g_in[0], at), conv_w[0]) + contract_cols(rows_of(g_gate, at), gate_w)
+        pairs.append(rep_near([both[k * half:(k + 1) * half] for k in range(n_rep)]))
+    all_out = [value[held:].reshape(pieces, part, chans).transpose(1, 0, 2).reshape(part, width) for value in early]
+    all_out = jnp.concatenate(in_order(all_out, rep_at), axis=0).astype(F32)
+    early = [value[:held] for value in early]
+    at = rep_at.reshape(1)
+    direct = part % LN == 0
+    if direct:
+        all_in = spread(early, at, *in_proj.shape, part, n_shard, [])
+        tied = [late[0], all_in, all_out, pairs[-1][0]]
+        late[0], all_in, all_out, mine_last = lax.optimization_barrier(tied)
+        pairs[-1] = (mine_last, pairs[-1][1])
+    g_normed = [rep_far(*pair) for pair in pairs]
     g_normed = jnp.concatenate(g_normed, axis=0)
     scale = lax.rsqrt(jnp.mean(input_f * input_f, axis=1, keepdims=True) + EPSILON)
     grad_gain = jnp.sum(g_normed * input_f * scale, axis=0)
@@ -641,18 +701,15 @@
     )
     grad_gain = add_all(add_all(grad_gain.reshape(-1, LN), "rep"), "shard").reshape(width)
     all_gain = lax.dynamic_slice_in_dim(grad_gain, shard_at * norm_gain.shape[0], norm_gain.shape[0])
-    all_late = everyone(late)
-    all_out = all_early[:, held:].reshape(n_rep, pieces, part, chans).transpose(0, 2, 1, 3)
-    all_out = all_out.reshape(wide, width).astype(F32)
-    if part % LN:
-        all_in = jnp.stack([all_late[:, :held], all_early[:, :held]], axis=0)
+    late = [rep_gather(value) for value in late]
+    all_small = jnp.concatenate(in_order(small, rep_at), axis=0).astype(F32)
+    if direct:
+        all_in = spread(late[0], at, *in_proj.shape, part, 0, [all_in])
+    else:
+        late = [jnp.concatenate([values[k] for values in late], axis=1) for k in range(n_rep)]
+        all_in = jnp.stack([jnp.stack(in_order(value, rep_at), axis=0) for value in (late, early)], axis=0)
         all_in = all_in.reshape(2, n_rep, -1, n_shard, part).transpose(2, 0, 3, 1, 4)
         all_in = all_in.reshape(in_proj.shape).astype(F32)
-    else:
-        all_in = spread(all_early, *in_proj.shape, part, 1, [])
-        all_in = spread(all_late, *in_proj.shape, part, 0, [all_in])
-    all_small = all_late[:, held:].reshape(n_rep, lanes, part, LN).transpose(0, 2, 1, 3)
-    all_small = all_small.reshape(wide, lanes * LN).astype(F32)
     return (
         activations,
         input_grad,

time: 837 us -> 811 us (0.969)
  waiting for transfers between devices: 123 us -> 104 us
  other arithmetic: 77.5 us -> 89.5 us
  Pallas kernels: 302 us -> 292 us
    reduce_scatter x2, waiting for transfers between devices: 47 us -> 0.59 us  [scatter(): return lax.psum_scatter(value, 'shard', scatter_dimension=0, tiled=True)]
    ppermute x27 -> x36, waiting for transfers between devices: 40.6 us -> 53.2 us  [swap(): lax.ppermute(value, 'rep', [(i, i ^ flip) for i in range(lax.axis_size('r...]
    ppermute x5 -> x10, waiting for transfers between devices: 7.56 us -> 17.5 us  [other(): lax.ppermute(value, axis, [(i, i ^ flip) for i in range(lax.axis_size(axi...]
    ppermute x8, starting transfers between devices: 28.9 us -> 19.3 us  [moved(): got = lax.ppermute(sent, 'shard', pairs).astype(F32)]
    ppermute x27 -> x36, starting transfers between devices: 13.4 us -> 18.4 us  [swap(): lax.ppermute(value, 'rep', [(i, i ^ flip) for i in range(lax.axis_size('r...]
  transfers between devices with their start and end apart: 49 -> 61, of which waited for: 18 -> 21; matrix products, arithmetic and copies ran while one was open for 27% -> 27% of each run, Pallas kernels for 26% -> 26%
where the time goes in v4:
time: 811 us; the launch traced here: 802 us
  Pallas kernels  292 us (36%)
  matrix products  151 us (19%)
  waiting for transfers between devices  104 us (13%)
  other arithmetic  89.5 us (11%)
  local copies, waits for them, and re-layouts  57.3 us (7%)
  starting transfers between devices  55.6 us (7%)
  blocking collectives  36.9 us (5%)
  between operations  15.6 us (2%)
    pallas_call x2, Pallas kernels, bwd_pass(): pl.pallas_call(partial(bwd_kernel, U, TB, n_in), grid=(Q, 1, NC), in_spec...  132 us
    pallas_call x1, Pallas kernels, fwd_pass(): pl.pallas_call(partial(fwd_kernel, U, TB), grid=(Q, NE, NC), in_specs=[ro...  73 us
    dot_general x6, matrix products, contract_cols(): lax.dot_general(left, right, (((1,), (1,)), ((), ())), preferred_element_...  53.8 us
    ppermute x36, waiting for transfers between devices, swap(): lax.ppermute(value, 'rep', [(i, i ^ flip) for i in range(lax.axis_size('r...  53.2 us
    dot_general x7, matrix products, contract_rows(): lax.dot_general(left, right, (((0,), (0,)), ((), ())), preferred_element_...  49.3 us
    all_gather x1, blocking collectives, on_device(): small_all = lax.all_gather(small, 'shard', axis=0, tiled=True)  36.9 us
    pallas_call x1, Pallas kernels, first_pass(): pl.pallas_call(partial(first_kernel, U), grid=(Q, NE, NC), in_specs=[row,...  30.5 us
    pallas_call x1, Pallas kernels, conv_back(): pl.pallas_call(conv_back_kernel, grid=(Q, E // EB), in_specs=[pl.BlockSpe...  24.3 us
  transfers between devices with their start and end apart: 61, of which 21 were waited for; matrix products, arithmetic and copies ran while one was open for 27% of the time, Pallas kernels for 26%

profile of v4, /device:TPU:0, one launch (start us, length us, event | category | flops | bytes accessed | tf_op | source)
XLA Modules:
  0.0 801.6 jit_solution(6685195246123439312)
XLA Ops:
  22.8 36.9 %all_gather.12 = bf16[1024,313]{0,1:T(8,128)(2,1)S(1)} all-gather(bf16[128,313]{0,1:T(8,128)(2,1)S(1)} %concatenate.75), channel_id=1, replica_groups=mesh['rep'=4,'shard'=8] {'shard'}, dimensions={0}, use_global_device_ids=true | all-gather | bytes 721152 | tf_op jit(solution)/shard_map/all_gather | solution.py:564
  80.0 15.3 %all-gather.4.cloned.1.call-done = bf16[2048,1024]{1,0:T(8,128)(2,1)} async-done(((bf16[256,1024]{1,0:T(8,128)(2,1)}), bf16[2048,1024]{1,0:T(8,128)(2,1)}) %all-gather.4.cloned.1.call-update) | async-done | bytes 4194320 | tf_op jit(solution)/shard_map/all_gather | solution.py:567
  95.2 12.5 %convolution_convert_fusion.x_ref = bf16[2048,1024]{1,0:T(8,128)(2,1)S(1)} fusion(bf16[2048,2048]{1,0:T(8,128)(2,1)} %pad_maximum_fusion, bf16[2048,1024]{1,0:T(8,128)(2,1)} %all-gather.4.cloned.1.call-done), kind=kOutput, calls=%fused_computation.51 | convolution fusion | flops 8592031744 | bytes 16777216 | tf_op jit(solution)/shard_map/dot_general | solution.py:593
  114.5 14.5 %conv_pass.1.x_ref.refs_1_ = bf16[2048,1024]{1,0:T(8,128)(2,1)} custom-call(bf16[2048,1024]{1,0:T(8,128)(2,1)} %copy-done.6, f32[4,8,1024]{2,1,0:T(8,128)} %concatenate.77.edge_ref, f32[5,1024]{1,0:T(8,128)} %convert_bitcast_fusion.1.w_ref), custom_call_target="tpu_custom_call" | custom-call | flops 25165824 | bytes 8388608 | tf_op jit(solution)/shard_map/conv_pass/pallas_call | solution.py:306
  161.2 9.0 %broadcast_in_dim.23.b_ref.refs_3_ = f32[2048,16,128]{2,1,0:T(8,128)} broadcast(f32[2048,16]{1,0:T(8,128)S(1)} %copy-done.15), dimensions={0,1} | broadcast | bytes 16908288 | tf_op jit(solution)/shard_map/broadcast_in_dim | solution.py:601
  170.3 30.5 %first_pass.1 = f32[4,16,1024]{2,1,0:T(8,128)} custom-call(f32[2048,1024]{1,0:T(8,128)} %get-tuple-element.161.dt_ref.refs_0_, bf16[2048,1024]{1,0:T(8,128)(2,1)} %conv_pass.1.x_ref.refs_1_, f32[2048,16,128]{2,1,0:T(8,128)} %broadcast_in_dim.23.b_ref.refs_3_, f32[16,1024]{1,0:T(8,128)} %get-tuple-element.129.a_ref.refs_5_), custom_call_target="tpu_custom_call" | custom-call | flops 167772160 | bytes 20971520 | tf_op jit(solution)/shard_map/first_pass/pallas_call | solution.py:46
  226.3 14.5 %fusion.87.gate_ref = f32[2048,1024]{1,0:T(8,128)} fusion(bf16[2048,2048]{1,0:T(8,128)(2,1)} %pad_maximum_fusion, bf16[2048,1024]{1,0:T(8,128)(2,1)} %all-gather.6.cloned.1.call-done), kind=kOutput, calls=%fused_computation.207 | convolution fusion | flops 8589934592 | bytes 20971520 | tf_op jit(solution)/shard_map/dot_general | solution.py:606
  255.8 14.5 %fusion.88.gg_ref = f32[2048,1024]{1,0:T(8,128)} fusion(bf16[2048,2048]{1,0:T(8,128)(2,1)} %pad_maximum_fusion.1, bf16[1024,2048]{1,0:T(8,128)(2,1)} %all-gather.8.cloned.1.call-done), kind=kOutput, calls=%fused_computation.208 | convolution fusion | flops 8589934592 | bytes 20971520 | tf_op jit(solution)/shard_map/dot_general | solution.py:386
  270.4 9.0 %broadcast_in_dim.24.c_ref.refs_4_ = f32[2048,16,128]{2,1,0:T(8,128)} broadcast(f32[2048,16]{1,0:T(8,128)S(1)} %copy.47), dimensions={0,1} | broadcast | bytes 16908288 | tf_op jit(solution)/shard_map/broadcast_in_dim | solution.py:602
  279.3 73.0 %fwd_pass.1 = (bf16[2048,1024]{1,0:T(8,128)(2,1)}, bf16[2048,1024]{1,0:T(8,128)(2,1)}, f32[2048,1024]{1,0:T(8,128)}, f32[8,16,1024]{2,1,0:T(8,128)}, f32[4,16,1024]{2,1,0:T(8,128)}) custom-call(f32[2048,1024]{1,0:T(8,128)} %get-tuple-element.161.dt_ref.refs_0_, bf16[2048,1024]{1,0:T(8,128)(2,1)} %conv_pass.1.x_ref.refs_1_, f32[2048,1024]{1,0:T(8,128)} %fusion.87.gate_ref, ...), custom_call_target="tpu_custom_call" | custom-call | flops 369098752 | bytes 46137344 | tf_op jit(solution)/shard_map/fwd_pass/pallas_call | solution.py:114
  352.3 8.2 %fusion.31 = bf16[1024,1024]{1,0:T(8,128)(2,1)S(1)} fusion(bf16[2048,1024]{1,0:T(8,128)(2,1)} %get-tuple-element.62, bf16[2048,2048]{1,0:T(8,128)(2,1)} %pad_maximum_fusion.1), kind=kOutput, calls=%fused_computation.65 | convolution fusion | flops 4296015872 | bytes 10485760 | tf_op jit(solution)/shard_map/dot_general | solution.py:382
  360.5 11.7 %convolution_convert_fusion.2 = bf16[2048,1024]{1,0:T(8,128)(2,1)S(1)} fusion(bf16[2048,2048]{1,0:T(8,128)(2,1)} %pad_maximum_fusion, bf16[2048,1024]{1,0:T(8,128)(2,1)S(1)} %copy-done.16), kind=kOutput, calls=%fused_computation.53 | convolution fusion | flops 8592031744 | bytes 16777216 | tf_op jit(solution)/shard_map/dot_general | solution.py:382
  372.2 16.4 %fusion.84 = (bf16[2048,2048]{1,0:T(8,128)(2,1)}, f32[2048,2048]{1,0:T(8,128)}) fusion(bf16[2048,1024]{1,0:T(8,128)(2,1)} %get-tuple-element.62, bf16[1024,2048]{1,0:T(8,128)(2,1)S(1)} %copy-done.52), kind=kOutput, calls=%fused_computation.204 | convolution fusion | flops 8594128896 | bytes 33554432 | tf_op jit(solution)/shard_map/dot_general | solution.py:619
  407.3 9.6 %collective-permute-done.21 = bf16[68,1024]{1,0:T(8,128)(2,1)S(1)} collective-permute-done((bf16[68,1024]{1,0:T(8,128)(2,1)S(1)}, bf16[68,1024]{1,0:T(8,128)(2,1)S(1)}, u32[]{:S(2)}, u32[]{:S(2)}) %collective-permute-start.21) | collective-permute-done | bytes 139296 | tf_op jit(solution)/shard_map/ppermute | solution.py:473
  425.7 66.3 %bwd_pass.2 = (bf16[2048,1024]{1,0:T(8,128)(2,1)}, f32[2048,1024]{1,0:T(8,128)}, f32[2,1,32768]{2,1,0:T(1,128)}, f32[2,1,32768]{2,1,0:T(1,128)}, f32[4,16,1024]{2,1,0:T(8,128)}, /*index=5*/f32[4,2,1024]{2,1,0:T(2,128)}) custom-call(f32[2048,1024]{1,0:T(8,128)} %get-tuple-element.161.dt_ref.refs_0_, bf16[2048,1024]{1,0:T(8,128)(2,1)} %conv_pass.1.x_ref.refs_1_, ...), custom_call_target="tpu_custom_call" | custom-call | flops 335544320 | bytes 23068672 | tf_op jit(solution)/shard_map/bwd_pass/pallas_call | solution.py:219
  499.3 66.0 %bwd_pass.3 = (bf16[2048,1024]{1,0:T(8,128)(2,1)}, f32[2048,1024]{1,0:T(8,128)}, f32[2,1,32768]{2,1,0:T(1,128)}, f32[2,1,32768]{2,1,0:T(1,128)}, f32[4,16,1024]{2,1,0:T(8,128)}, /*index=5*/f32[4,2,1024]{2,1,0:T(2,128)}) custom-call(f32[2048,1024]{1,0:T(8,128)} %get-tuple-element.161.dt_r, ...), custom_call_target="tpu_custom_call", output_to_operand_aliasing={{0}: (9, {}), {1}: (10, {}), {2}: (11, {}), {3}: (12, {}), ... | custom-call | flops 335544320 | bytes 23068672 | tf_op jit(solution)/shard_map/bwd_pass/pallas_call | solution.py:219
  599.5 24.3 %conv_back.1 = (bf16[2048,1024]{1,0:T(8,128)(2,1)}, f32[4,8,1024]{2,1,0:T(8,128)}, f32[4,8,1024]{2,1,0:T(8,128)}, f32[4,5,1024]{2,1,0:T(8,128)}) custom-call(bf16[2048,160]{1,0:T(8,128)(2,1)} %maximum_bitcast_fusion.gp_ref, bf16[1024,160]{1,0:T(8,128)(2,1)} %copy.49.xp_ref, f32[2048,1024]{1,0:T(8,128)} %get-tuple-element.80.gx_ref, ...), custom_call_target="tpu_custom_call" | custom-call | flops 838860800 | bytes 20971520 | tf_op jit(solution)/shard_map/conv_back/pallas_call | solution.py:356
  640.8 12.8 %convolution_convert_fusion.1 = bf16[2048,1024]{1,0:T(8,128)(2,1)} fusion(bf16[2048,2048]{1,0:T(8,128)(2,1)} %pad_maximum_fusion, bf16[2048,1024]{1,0:T(8,128)(2,1)S(1)} %bitcast.156), kind=kOutput, calls=%fused_computation.52 | convolution fusion | flops 8592031744 | bytes 16777216 | tf_op jit(solution)/shard_map/dot_general | solution.py:382
  653.6 10.9 %fusion.89 = f32[1024,2048]{1,0:T(8,128)} fusion(bf16[1024,1024]{1,0:T(8,128)(2,1)} %bitcast.176, bf16[2048,1024]{1,0:T(8,128)(2,1)} %all-gather.4.cloned.1.call-done), kind=kOutput, calls=%fused_computation.209 | convolution fusion | flops 4294967296 | bytes 14680064 | tf_op jit(solution)/shard_map/dot_general | solution.py:386
  664.6 8.3 %fusion.86 = (bf16[1024,2048]{1,0:T(8,128)(2,1)S(1)}, f32[1024,2048]{1,0:T(8,128)S(1)}) fusion(f32[1024,2048]{1,0:T(8,128)} %fusion.89, bf16[1024,1024]{1,0:T(8,128)(2,1)S(1)} %bitcast.174, bf16[2048,1024]{1,0:T(8,128)(2,1)} %all-gather.6.cloned.1.call-done), kind=kOutput, calls=%fused_computation.206 | convolution fusion | flops 4299161600 | bytes 27262976 | tf_op jit(solution)/shard_map/dot_general | solution.py:386
  674.6 13.9 %collective-permute-done.51 = bf16[2,128,384]{1,2,0:T(8,128)(2,1)S(1)} collective-permute-done((bf16[2,128,384]{1,2,0:T(8,128)(2,1)S(1)}, bf16[2,128,384]{1,2,0:T(8,128)(2,1)S(1)}, u32[]{:S(2)}, u32[]{:S(2)}) %collective-permute-start.51) | collective-permute-done | bytes 196640 | tf_op jit(solution)/shard_map/ppermute | solution.py:435
  697.1 9.7 %fusion.85 = (bf16[1024,2048]{1,0:T(8,128)(2,1)}, f32[1024,2048]{1,0:T(8,128)S(1)}) fusion(f32[1024,2048]{1,0:T(8,128)} %fusion.90, bf16[1024,1024]{1,0:T(8,128)(2,1)S(1)} %bitcast.173, bf16[2048,1024]{1,0:T(8,128)(2,1)} %all-gather.6.cloned.1.call-done), kind=kOutput, calls=%fused_computation.205 | convolution fusion | flops 4299161600 | bytes 27262976 | tf_op jit(solution)/shard_map/dot_general | solution.py:386
  733.1 8.0 collective-permute-done.33
  745.7 16.9 %collective-permute-done.39 = bf16[256,2048]{1,0:T(8,128)(2,1)} collective-permute-done((bf16[256,2048]{1,0:T(8,128)(2,1)}, bf16[256,2048]{1,0:T(8,128)(2,1)}, u32[]{:S(2)}, u32[]{:S(2)}) %collective-permute-start.39) | collective-permute-done | bytes 1048608 | tf_op jit(solution)/shard_map/ppermute | solution.py:390
  (395 shorter events, 273.3 us)
Async XLA Ops:
  7.2 88.1 %all-gather.4.cloned.1.call-start = ((), (), s32[]{:S(2)}) async-start(), calls=%async_computation.2 | async-start | bytes 4718592 | tf_op jit(solution)/shard_map/all_gather | solution.py:567
  9.8 216.5 %all-gather.6.cloned.1.call-start = ((), (), s32[]{:S(2)}) async-start(), calls=%async_computation.3 | async-start | bytes 4718592 | tf_op jit(solution)/shard_map/all_gather | solution.py:568
  12.2 243.6 %all-gather.8.cloned.1.call-start = ((), (), s32[]{:S(2)}) async-start(), calls=%async_computation.4 | async-start | bytes 4718592 | tf_op jit(solution)/shard_map/all_gather | solution.py:569
  12.3 48.8 %collective-permute-start = (bf16[512,2048]{1,0:T(8,128)(2,1)S(1)}, bf16[512,2048]{1,0:T(8,128)(2,1)}, u32[]{:S(2)}, u32[]{:S(2)}) collective-permute-start(bf16[512,2048]{1,0:T(8,128)(2,1)S(1)} %copy-done.2), channel_id=1, source_target_pairs={{0,16},{8,24},{16,0},{24,8},{1,17},{9,25},{17,1},{25,9},{2,18},{10... | collective-permute-start | bytes 6291464 | tf_op jit(solution)/shard_map/ppermute | solution.py:390
  15.3 48.1 %collective-permute-start.1 = (bf16[512,2048]{1,0:T(8,128)(2,1)S(1)}, bf16[512,2048]{1,0:T(8,128)(2,1)}, u32[]{:S(2)}, u32[]{:S(2)}) collective-permute-start(bf16[512,2048]{1,0:T(8,128)(2,1)S(1)} %copy-done.2), channel_id=1, source_target_pairs={{0,8},{8,0},{16,24},{24,16},{1,9},{9,1},{17,25},{25,17},{2,10},{10... | collective-permute-start | bytes 6291464 | tf_op jit(solution)/shard_map/ppermute | solution.py:390
  17.2 581.3 %reduce-scatter.3.cloned.1.call-start = ((), (), s32[]{:S(2)}) async-start(), calls=%async_computation.5 | async-start | bytes 9437184 | tf_op jit(solution)/shard_map/reduce_scatter | solution.py:634
  78.3 59.5 %collective-permute-start.11 = (bf16[512,2048]{1,0:T(8,128)(2,1)S(1)}, bf16[512,2048]{1,0:T(8,128)(2,1)}, u32[]{:S(2)}, u32[]{:S(2)}) collective-permute-start(bf16[512,2048]{1,0:T(8,128)(2,1)S(1)} %copy-done.7), channel_id=1, source_target_pairs={{0,16},{8,24},{16,0},{24,8},{1,17},{9,25},{17,1},{25,9},{2,18},{10... | collective-permute-start | bytes 6291464 | tf_op jit(solution)/shard_map/ppermute | solution.py:390
  133.9 70.8 %collective-permute-start.10 = (bf16[512,2048]{1,0:T(8,128)(2,1)S(1)}, bf16[512,2048]{1,0:T(8,128)(2,1)}, u32[]{:S(2)}, u32[]{:S(2)}) collective-permute-start(bf16[512,2048]{1,0:T(8,128)(2,1)S(1)} %copy-done.7), channel_id=1, source_target_pairs={{0,8},{8,0},{16,24},{24,16},{1,9},{9,1},{17,25},{25,17},{2,10},{10... | collective-permute-start | bytes 6291464 | tf_op jit(solution)/shard_map/ppermute | solution.py:390
  137.7 111.9 %collective-permute-start.12 = (bf16[512,2048]{1,0:T(8,128)(2,1)}, bf16[512,2048]{1,0:T(8,128)(2,1)}, u32[]{:S(2)}, u32[]{:S(2)}) collective-permute-start(bf16[512,2048]{1,0:T(8,128)(2,1)} %collective-permute-done.11), channel_id=1, source_target_pairs={{0,8},{8,0},{16,24},{24,16},{1,9},{9,1},{17,25},{25,17},{2,10},{10... | collective-permute-start | bytes 6291464 | tf_op jit(solution)/shard_map/ppermute | solution.py:390
  213.8 33.1 %collective-permute-start.16 = (bf16[68,1024]{1,0:T(8,128)(2,1)}, bf16[68,1024]{1,0:T(8,128)(2,1)}, u32[]{:S(2)}, u32[]{:S(2)}) collective-permute-start(bf16[68,1024]{1,0:T(8,128)(2,1)} %pad_maximum_fusion.8), channel_id=1, source_target_pairs={{0,6},{1,7},{8,14},{9,15},{16,22},{17,23},{24,30},{25,31}} | collective-permute-start | bytes 417800 | tf_op jit(solution)/shard_map/ppermute | solution.py:473
  221.6 20.5 %collective-permute-start.15 = (bf16[68,1024]{1,0:T(8,128)(2,1)}, bf16[68,1024]{1,0:T(8,128)(2,1)}, u32[]{:S(2)}, u32[]{:S(2)}) collective-permute-start(bf16[68,1024]{1,0:T(8,128)(2,1)} %pad_maximum_fusion.8), channel_id=1, source_target_pairs={{0,4},{1,5},{2,6},{3,7},{8,12},{9,13},{10,14},{11,15},{16,20},{17,... | collective-permute-start | bytes 417800 | tf_op jit(solution)/shard_map/ppermute | solution.py:473
  223.5 20.8 %collective-permute-start.14 = (bf16[68,1024]{1,0:T(8,128)(2,1)}, bf16[68,1024]{1,0:T(8,128)(2,1)}, u32[]{:S(2)}, u32[]{:S(2)}) collective-permute-start(bf16[68,1024]{1,0:T(8,128)(2,1)} %pad_maximum_fusion.8), channel_id=1, source_target_pairs={{0,2},{1,3},{2,4},{3,5},{4,6},{5,7},{8,10},{9,11},{10,12},{11,13},... | collective-permute-start | bytes 417800 | tf_op jit(solution)/shard_map/ppermute | solution.py:473
  392.9 25.0 %collective-permute-start.18 = (bf16[512,2048]{1,0:T(8,128)(2,1)S(1)}, bf16[512,2048]{1,0:T(8,128)(2,1)S(1)}, u32[]{:S(2)}, u32[]{:S(2)}) collective-permute-start(bf16[512,2048]{1,0:T(8,128)(2,1)S(1)} %get-tuple-element.107), channel_id=1, source_target_pairs={{0,8},{8,0},{16,24},{24,16},{1,9},{9,1},{17,25},{25,17},{2,10},{10... | collective-permute-start | bytes 6291464 | tf_op jit(solution)/shard_map/ppermute | solution.py:390
  422.2 323.5 %reduce-scatter.5.cloned.1.call-start = ((), (), s32[]{:S(2)}) async-start(), calls=%async_computation.6 | async-start | bytes 4718592 | tf_op jit(solution)/shard_map/reduce_scatter | solution.py:634
  422.2 69.7 %collective-permute-start.17 = (bf16[512,2048]{1,0:T(8,128)(2,1)}, bf16[512,2048]{1,0:T(8,128)(2,1)}, u32[]{:S(2)}, u32[]{:S(2)}) collective-permute-start(bf16[512,2048]{1,0:T(8,128)(2,1)} %get-tuple-element.106), channel_id=1, source_target_pairs={{0,8},{8,0},{16,24},{24,16},{1,9},{9,1},{17,25},{25,17},{2,10},{10... | collective-permute-start | bytes 6291464 | tf_op jit(solution)/shard_map/ppermute | solution.py:390
  422.3 69.7 %collective-permute-start.23 = (bf16[512,2048]{1,0:T(8,128)(2,1)}, bf16[512,2048]{1,0:T(8,128)(2,1)}, u32[]{:S(2)}, u32[]{:S(2)}) collective-permute-start(bf16[512,2048]{1,0:T(8,128)(2,1)} %fusion.18.refs_10_), channel_id=1, source_target_pairs={{0,16},{8,24},{16,0},{24,8},{1,17},{9,25},{17,1},{25,9},{2,18},{10... | collective-permute-start | bytes 6291464 | tf_op jit(solution)/shard_map/ppermute | solution.py:390
  598.5 120.5 %collective-permute-start.34 = (bf16[512,1024]{1,0:T(8,128)(2,1)}, bf16[512,1024]{1,0:T(8,128)(2,1)}, u32[]{:S(2)}, u32[]{:S(2)}) collective-permute-start(bf16[512,1024]{1,0:T(8,128)(2,1)} %reduce-scatter.3.cloned.1.call-done), channel_id=1, source_target_pairs={{0,8},{8,0},{16,24},{24,16},{1,9},{9,1},{17,25},{25,17},{2,10},{10... | collective-permute-start | bytes 3145736 | tf_op jit(solution)/shard_map/ppermute | solution.py:390
  598.7 113.0 %collective-permute-start.35 = (bf16[512,1024]{1,0:T(8,128)(2,1)}, bf16[512,1024]{1,0:T(8,128)(2,1)}, u32[]{:S(2)}, u32[]{:S(2)}) collective-permute-start(bf16[512,1024]{1,0:T(8,128)(2,1)} %reduce-scatter.3.cloned.1.call-done), channel_id=1, source_target_pairs={{0,16},{8,24},{16,0},{24,8},{1,17},{9,25},{17,1},{25,9},{2,18},{10... | collective-permute-start | bytes 3145736 | tf_op jit(solution)/shard_map/ppermute | solution.py:390
  629.8 43.0 %collective-permute-start.50 = (bf16[4,128,384]{1,2,0:T(8,128)(2,1)S(1)}, bf16[4,128,384]{1,2,0:T(8,128)(2,1)S(1)}, u32[]{:S(2)}, u32[]{:S(2)}) collective-permute-start(bf16[4,128,384]{1,2,0:T(8,128)(2,1)S(1)} %dynamic-slice_convert_fusion), channel_id=1, source_target_pairs={{0,4},{1,5},{2,6},{3,7},{4,0},{5,1},{6,2},{7,3},{8,12},{9,13},{10,... | collective-permute-start | bytes 1179656 | tf_op jit(solution)/shard_map/ppermute | solution.py:435
  674.5 37.2 %collective-permute-start.32 = (bf16[256,2048]{1,0:T(8,128)(2,1)}, bf16[256,2048]{1,0:T(8,128)(2,1)}, u32[]{:S(2)}, u32[]{:S(2)}) collective-permute-start(bf16[256,2048]{1,0:T(8,128)(2,1)} %get-tuple-element.109), channel_id=1, source_target_pairs={{0,8},{8,0},{16,24},{24,16},{1,9},{9,1},{17,25},{25,17},{2,10},{10... | collective-permute-start | bytes 3145736 | tf_op jit(solution)/shard_map/ppermute | solution.py:390
  711.7 21.4 %collective-permute-start.31 = (bf16[256,2048]{1,0:T(8,128)(2,1)}, bf16[256,2048]{1,0:T(8,128)(2,1)}, u32[]{:S(2)}, u32[]{:S(2)}) collective-permute-start(bf16[256,2048]{1,0:T(8,128)(2,1)} %get-tuple-element.108), channel_id=1, source_target_pairs={{0,8},{8,0},{16,24},{24,16},{1,9},{9,1},{17,25},{25,17},{2,10},{10... | collective-permute-start | bytes 3145736 | tf_op jit(solution)/shard_map/ppermute | solution.py:390
  714.7 26.3 %collective-permute-start.33 = (bf16[256,2048]{1,0:T(8,128)(2,1)}, bf16[256,2048]{1,0:T(8,128)(2,1)}, u32[]{:S(2)}, u32[]{:S(2)}) collective-permute-start(bf16[256,2048]{1,0:T(8,128)(2,1)} %fusion.26), channel_id=1, source_target_pairs={{0,16},{8,24},{16,0},{24,8},{1,17},{9,25},{17,1},{25,9},{2,18},{10... | collective-permute-start | bytes 3145736 | tf_op jit(solution)/shard_map/ppermute | solution.py:390
  717.7 45.0 %collective-permute-start.39 = (bf16[256,2048]{1,0:T(8,128)(2,1)}, bf16[256,2048]{1,0:T(8,128)(2,1)}, u32[]{:S(2)}, u32[]{:S(2)}) collective-permute-start(bf16[256,2048]{1,0:T(8,128)(2,1)} %get-tuple-element.104), channel_id=1, source_target_pairs={{0,16},{8,24},{16,0},{24,8},{1,17},{9,25},{17,1},{25,9},{2,18},{10... | collective-permute-start | bytes 3145736 | tf_op jit(solution)/shard_map/ppermute | solution.py:390
  769.6 18.2 %collective-permute-start.47 = (bf16[256,1024]{1,0:T(8,128)(2,1)S(1)}, bf16[256,1024]{1,0:T(8,128)(2,1)S(1)}, u32[]{:S(2)}, u32[]{:S(2)}) collective-permute-start(bf16[256,1024]{1,0:T(8,128)(2,1)S(1)} %copy-done.33), channel_id=1, source_target_pairs={{0,8},{8,0},{16,24},{24,16},{1,9},{9,1},{17,25},{25,17},{2,10},{10... | collective-permute-start | bytes 1572872 | tf_op jit(solution)/shard_map/ppermute | solution.py:390
  (95 other events, 1093.8 us)
Sparse Core Ops, SparseCore 0:
  10.7 84.5 all-gather.3
  97.4 72.1 all-gather.5
  171.7 75.8 all-gather.7
  422.3 147.3 reduce-scatter.2
  653.8 91.9 reduce-scatter.4

commit v5 on v4

--- a/solution.py
+++ b/solution.py
@@ -12,7 +12,8 @@
 GROUP = 512
 F32=jnp.float32; BF16=jnp.bfloat16
 LN=128
-def first_kernel(U, dt_ref, x_ref, b_ref, a_ref, hend_ref, h_s, dtx_s):
+def first_kernel(U, dt_ref, x_ref, b_ref, a_ref, *refs):
+    hend_ref, h_s, dtx_s = refs[-3:]
     TC, EG = dt_ref.shape
     NT = EG//LN
     c = pl.program_id(2)
@@ -38,19 +39,19 @@
     def _():
         hend_ref[...] = h_s[...]
 
-def first_pass(dt, x, bx, a2, Q, TC=256, EG=GROUP, U=8):
+def first_pass(dt, x, bx, a2, waits, Q, TC=256, EG=GROUP, U=8):
     T,E = dt.shape; N = a2.shape[0]; L=T//Q; NC=L//TC; NE=E//EG
     row = pl.BlockSpec((TC,EG), lambda q,e,c:(q*NC+c, e))
     sp = pl.BlockSpec((TC,N,LN), lambda q,e,c:(q*NC+c,0,0))
     st = pl.BlockSpec((None,N,EG), lambda q,e,c:(q,0,e))
     return pl.pallas_call(partial(first_kernel,U), grid=(Q,NE,NC),
-        in_specs=[row,row,sp,pl.BlockSpec((N,EG), lambda q,e,c:(0,e))],
+        in_specs=[row,row,sp,pl.BlockSpec((N,EG), lambda q,e,c:(0,e))]+[pl.BlockSpec(memory_space=pl.ANY)]*len(waits),
         out_specs=st,
         out_shape=jax.ShapeDtypeStruct((Q,N,E),F32),
         scratch_shapes=[pltpu.VMEM((N,EG),F32),pltpu.VMEM((TC,EG),F32)],
         compiler_params=pltpu.CompilerParams(dimension_semantics=("arbitrary",)*3, vmem_limit_bytes=60<<20),
         name="first_pass",
-        cost_estimate=pl.CostEstimate(flops=5*T*E*N, bytes_accessed=10*T*E, transcendentals=T*E*N))(dt,x,bx,a2)
+        cost_estimate=pl.CostEstimate(flops=5*T*E*N, bytes_accessed=10*T*E, transcendentals=T*E*N))(dt,x,bx,a2,*waits)
 
 LOG2E = 1.4426950408889634
 
@@ -449,14 +450,11 @@
 
 
 def halve(value):
-    step = lax.axis_size("shard") // 2
-    while step:
-        own = lax.axis_index("shard") // step % 2
-        keep = lax.dynamic_slice_in_dim(value, own * step, step, 0)
-        send = lax.dynamic_slice_in_dim(value, (1 - own) * step, step, 0)
-        value = keep + other(send.astype(BF16), "shard", step).astype(F32)
-        step //= 2
-    return value[0]
+    step = value.shape[0] // 2
+    own = lax.axis_index("shard") // step % 2
+    keep = lax.dynamic_slice_in_dim(value, own * step, step, 0)
+    send = lax.dynamic_slice_in_dim(value, (1 - own) * step, step, 0)
+    return keep + other(send.astype(BF16), "shard", step).astype(F32)
 
 
 def carry_in(total, state, rates, place, span, reverse):
@@ -609,7 +607,7 @@
     )
     g_gated = contract_cols(back, out_all)
     skip = skip_all[None, :]
-    local_end = first_pass(step, conv_out, b_all, rates2, n_rep)
+    local_end = first_pass(step, conv_out, b_all, rates2, [c_all, back], n_rep)
     total = jnp.sum(step.reshape(n_rep, rows, chans), axis=1)
     start_state = carry_in(total, local_end, rates, in_slot, span, False)
     gated, g_gate, g_scanned, kept, local_adj = fwd_pass(
@@ -670,15 +668,17 @@
         grad = contract_rows(normed, out).astype(BF16).reshape(n_shard, held, chans)
         small = [grad_x_proj, grad_dt_proj, grad_a_log.T, grad_wb[0].T, grad_dt_bias[:, None], grad_skip[:, None]]
         small.append(jnp.zeros((chans, -ends[6] % LN), F32))
-        small = halve(jnp.concatenate(small, axis=1).reshape(n_shard, part, -1)).astype(BF16)
-        small = rep_gather(small)
+        small = halve(jnp.concatenate(small, axis=1).reshape(n_shard, part, -1))
         grad = grad.reshape(-1, chans)
+        grad, *early = lax.optimization_barrier((grad, *early))
         g_in.append(out)
         late.append(scatter(grad))
     pairs = []
     for at in (0, half):
-        both = contract_cols(rows_of(g_in[0], at), conv_w[0]) + contract_cols(rows_of(g_gate, at), gate_w)
-        pairs.append(rep_near([both[k * half:(k + 1) * half] for k in range(n_rep)]))
+        conv_rows, gate_rows = (rows_of(g_in[0], at), rows_of(g_gate, at))
+        both = contract_cols(conv_rows, conv_w[0]) + contract_cols(gate_rows, gate_w)
+        both = [both[k * half:(k + 1) * half] for k in range(n_rep)]
+        pairs.append(rep_near(both))
     all_out = [value[held:].reshape(pieces, part, chans).transpose(1, 0, 2).reshape(part, width) for value in early]
     all_out = jnp.concatenate(in_order(all_out, rep_at), axis=0).astype(F32)
     early = [value[:held] for value in early]
@@ -690,6 +690,10 @@
         late[0], all_in, all_out, mine_last = lax.optimization_barrier(tied)
         pairs[-1] = (mine_last, pairs[-1][1])
     g_normed = [rep_far(*pair) for pair in pairs]
+    g_normed[0], small = lax.optimization_barrier((g_normed[0], small))
+    while small.shape[0] > 1:
+        small = halve(small)
+    small = rep_gather(small[0].astype(BF16))
     g_normed = jnp.concatenate(g_normed, axis=0)
     scale = lax.rsqrt(jnp.mean(input_f * input_f, axis=1, keepdims=True) + EPSILON)
     grad_gain = jnp.sum(g_normed * input_f * scale, axis=0)

time: 811 us -> 808 us (level)
  waiting for transfers between devices: 104 us -> 94.4 us
    ppermute x36, waiting for transfers between devices: 53.2 us -> 38.1 us  [swap(): lax.ppermute(value, 'rep', [(i, i ^ flip) for i in range(lax.axis_size('r...]
  transfers between devices with their start and end apart: 61 -> 61, of which waited for: 21 -> 22; matrix products, arithmetic and copies ran while one was open for 27% -> 31% of each run, Pallas kernels for 26% -> 26%
where the time goes in v5:
time: 808 us; the launch traced here: 798 us
  Pallas kernels  292 us (36%)
  matrix products  153 us (19%)
  waiting for transfers between devices  94.4 us (12%)
  other arithmetic  89 us (11%)
  starting transfers between devices  61.5 us (8%)
  local copies, waits for them, and re-layouts  56.3 us (7%)
  blocking collectives  36.7 us (5%)
  between operations  15.5 us (2%)
    pallas_call x2, Pallas kernels, bwd_pass(): pl.pallas_call(partial(bwd_kernel, U, TB, n_in), grid=(Q, 1, NC), in_spec...  132 us
    pallas_call x1, Pallas kernels, fwd_pass(): pl.pallas_call(partial(fwd_kernel, U, TB), grid=(Q, NE, NC), in_specs=[ro...  73 us
    dot_general x6, matrix products, contract_cols(): lax.dot_general(left, right, (((1,), (1,)), ((), ())), preferred_element_...  54 us
    dot_general x7, matrix products, contract_rows(): lax.dot_general(left, right, (((0,), (0,)), ((), ())), preferred_element_...  51.3 us
    ppermute x36, waiting for transfers between devices, swap(): lax.ppermute(value, 'rep', [(i, i ^ flip) for i in range(lax.axis_size('r...  38.1 us
    all_gather x1, blocking collectives, on_device(): small_all = lax.all_gather(small, 'shard', axis=0, tiled=True)  36.7 us
    pallas_call x1, Pallas kernels, first_pass(): pl.pallas_call(partial(first_kernel, U), grid=(Q, NE, NC), in_specs=[row,...  30.8 us
    pallas_call x1, Pallas kernels, conv_back(): pl.pallas_call(conv_back_kernel, grid=(Q, E // EB), in_specs=[pl.BlockSpe...  24.3 us
  transfers between devices with their start and end apart: 61, of which 22 were waited for; matrix products, arithmetic and copies ran while one was open for 31% of the time, Pallas kernels for 26%

profile of v5, /device:TPU:0, one launch (start us, length us, event | category | flops | bytes accessed | tf_op | source)
XLA Modules:
  0.0 798.4 jit_solution(174420707834998055)
XLA Ops:
  23.3 36.7 %all_gather.12 = bf16[1024,313]{0,1:T(8,128)(2,1)S(1)} all-gather(bf16[128,313]{0,1:T(8,128)(2,1)S(1)} %concatenate.75), channel_id=1, replica_groups=mesh['rep'=4,'shard'=8] {'shard'}, dimensions={0}, use_global_device_ids=true | all-gather | bytes 721152 | tf_op jit(solution)/shard_map/all_gather | solution.py:562
  80.1 15.2 %all-gather.4.cloned.1.call-done = bf16[2048,1024]{1,0:T(8,128)(2,1)} async-done(((bf16[256,1024]{1,0:T(8,128)(2,1)}), bf16[2048,1024]{1,0:T(8,128)(2,1)}) %all-gather.4.cloned.1.call-update) | async-done | bytes 4194320 | tf_op jit(solution)/shard_map/all_gather | solution.py:565
  95.3 12.5 %convolution_convert_fusion.x_ref = bf16[2048,1024]{1,0:T(8,128)(2,1)S(1)} fusion(bf16[2048,2048]{1,0:T(8,128)(2,1)} %pad_maximum_fusion, bf16[2048,1024]{1,0:T(8,128)(2,1)} %all-gather.4.cloned.1.call-done), kind=kOutput, calls=%fused_computation.51 | convolution fusion | flops 8592031744 | bytes 16777216 | tf_op jit(solution)/shard_map/dot_general | solution.py:591
  114.5 14.5 %conv_pass.1.x_ref.refs_1_ = bf16[2048,1024]{1,0:T(8,128)(2,1)} custom-call(bf16[2048,1024]{1,0:T(8,128)(2,1)} %copy-done.6, f32[4,8,1024]{2,1,0:T(8,128)} %concatenate.77.edge_ref, f32[5,1024]{1,0:T(8,128)} %convert_bitcast_fusion.1.w_ref), custom_call_target="tpu_custom_call" | custom-call | flops 25165824 | bytes 8388608 | tf_op jit(solution)/shard_map/conv_pass/pallas_call | solution.py:307
  169.4 9.0 %broadcast_in_dim.23.b_ref.refs_3_ = f32[2048,16,128]{2,1,0:T(8,128)} broadcast(f32[2048,16]{1,0:T(8,128)S(1)} %copy-done.12), dimensions={0,1} | broadcast | bytes 16908288 | tf_op jit(solution)/shard_map/broadcast_in_dim | solution.py:599
  178.4 8.9 %broadcast_in_dim.24.refs_0_.c_ref.refs_4_ = f32[2048,16,128]{2,1,0:T(8,128)} broadcast(f32[2048,16]{1,0:T(8,128)S(1)} %copy-done.13), dimensions={0,1} | broadcast | bytes 16908288 | tf_op jit(solution)/shard_map/broadcast_in_dim | solution.py:600
  187.4 30.8 %first_pass.1 = f32[4,16,1024]{2,1,0:T(8,128)} custom-call(f32[2048,1024]{1,0:T(8,128)} %get-tuple-element.175.dt_ref.refs_0_, bf16[2048,1024]{1,0:T(8,128)(2,1)} %conv_pass.1.x_ref.refs_1_, f32[2048,16,128]{2,1,0:T(8,128)} %broadcast_in_dim.23.b_ref.refs_3_, f32[16,1024]{1,0:T(8,128)} %get-tuple-element.143.a_ref.refs_5_, ...), custom_call_target="tpu_custom_call" | custom-call | flops 167772160 | bytes 20971520 | tf_op jit(solution)/shard_map/first_pass/pallas_call | solution.py:47
  221.8 14.7 %fusion.87.gate_ref = f32[2048,1024]{1,0:T(8,128)} fusion(bf16[2048,2048]{1,0:T(8,128)(2,1)} %pad_maximum_fusion, bf16[2048,1024]{1,0:T(8,128)(2,1)} %all-gather.6.cloned.1.call-done), kind=kOutput, calls=%fused_computation.207 | convolution fusion | flops 8589934592 | bytes 20971520 | tf_op jit(solution)/shard_map/dot_general | solution.py:604
  245.8 14.5 %fusion.88.gg_ref = f32[2048,1024]{1,0:T(8,128)} fusion(bf16[2048,2048]{1,0:T(8,128)(2,1)} %pad_maximum_fusion.1.refs_1_, bf16[1024,2048]{1,0:T(8,128)(2,1)} %all-gather.8.cloned.1.call-done), kind=kOutput, calls=%fused_computation.208 | convolution fusion | flops 8589934592 | bytes 20971520 | tf_op jit(solution)/shard_map/dot_general | solution.py:387
  260.3 8.8 %collective-permute-start.16 = (bf16[68,1024]{1,0:T(8,128)(2,1)S(1)}, bf16[68,1024]{1,0:T(8,128)(2,1)S(1)}, u32[]{:S(2)}, u32[]{:S(2)}) collective-permute-start(bf16[68,1024]{1,0:T(8,128)(2,1)S(1)} %pad_maximum_fusion.8), channel_id=1, source_target_pairs={{0,6},{1,7},{8,14},{9,15},{16,22},{17,23},{24,30},{25,31}} | collective-permute-start | bytes 417800 | tf_op jit(solution)/shard_map/ppermute | solution.py:471
  272.6 73.0 %fwd_pass.1 = (bf16[2048,1024]{1,0:T(8,128)(2,1)}, bf16[2048,1024]{1,0:T(8,128)(2,1)}, f32[2048,1024]{1,0:T(8,128)}, f32[8,16,1024]{2,1,0:T(8,128)}, f32[4,16,1024]{2,1,0:T(8,128)}) custom-call(f32[2048,1024]{1,0:T(8,128)} %get-tuple-element.175.dt_ref.refs_0_, bf16[2048,1024]{1,0:T(8,128)(2,1)} %conv_pass.1.x_ref.refs_1_, f32[2048,1024]{1,0:T(8,128)} %fusion.87.gate_ref, ...), custom_call_target="tpu_custom_call" | custom-call | flops 369098752 | bytes 46137344 | tf_op jit(solution)/shard_map/fwd_pass/pallas_call | solution.py:115
  345.6 8.2 %fusion.31 = bf16[1024,1024]{1,0:T(8,128)(2,1)S(1)} fusion(bf16[2048,1024]{1,0:T(8,128)(2,1)} %get-tuple-element.69, bf16[2048,2048]{1,0:T(8,128)(2,1)} %pad_maximum_fusion.1.refs_1_), kind=kOutput, calls=%fused_computation.65 | convolution fusion | flops 4296015872 | bytes 10485760 | tf_op jit(solution)/shard_map/dot_general | solution.py:383
  353.8 11.7 %convolution_convert_fusion.2 = bf16[2048,1024]{1,0:T(8,128)(2,1)S(1)} fusion(bf16[2048,2048]{1,0:T(8,128)(2,1)} %pad_maximum_fusion, bf16[2048,1024]{1,0:T(8,128)(2,1)S(1)} %copy-done.14), kind=kOutput, calls=%fused_computation.53 | convolution fusion | flops 8592031744 | bytes 16777216 | tf_op jit(solution)/shard_map/dot_general | solution.py:383
  365.6 16.4 %fusion.84 = (bf16[2048,2048]{1,0:T(8,128)(2,1)}, f32[2048,2048]{1,0:T(8,128)}) fusion(bf16[2048,1024]{1,0:T(8,128)(2,1)} %get-tuple-element.69, bf16[1024,2048]{1,0:T(8,128)(2,1)S(1)} %copy-done.48), kind=kOutput, calls=%fused_computation.204 | convolution fusion | flops 8594128896 | bytes 33554432 | tf_op jit(solution)/shard_map/dot_general | solution.py:617
  400.3 7.9 collective-permute-done.21
  417.0 66.1 %bwd_pass.2 = (bf16[2048,1024]{1,0:T(8,128)(2,1)}, f32[2048,1024]{1,0:T(8,128)}, f32[2,1,32768]{2,1,0:T(1,128)}, f32[2,1,32768]{2,1,0:T(1,128)}, f32[4,16,1024]{2,1,0:T(8,128)}, /*index=5*/f32[4,2,1024]{2,1,0:T(2,128)}) custom-call(f32[2048,1024]{1,0:T(8,128)} %get-tuple-element.175.dt_ref.refs_0_, bf16[2048,1024]{1,0:T(8,128)(2,1)} %conv_pass.1.x_ref.refs_1_, ...), custom_call_target="tpu_custom_call" | custom-call | flops 335544320 | bytes 23068672 | tf_op jit(solution)/shard_map/bwd_pass/pallas_call | solution.py:220
  490.5 66.0 %bwd_pass.3 = (bf16[2048,1024]{1,0:T(8,128)(2,1)}, f32[2048,1024]{1,0:T(8,128)}, f32[2,1,32768]{2,1,0:T(1,128)}, f32[2,1,32768]{2,1,0:T(1,128)}, f32[4,16,1024]{2,1,0:T(8,128)}, /*index=5*/f32[4,2,1024]{2,1,0:T(2,128)}) custom-call(f32[2048,1024]{1,0:T(8,128)} %get-tuple-element.175.dt_r, ...), custom_call_target="tpu_custom_call", output_to_operand_aliasing={{0}: (9, {}), {1}: (10, {}), {2}: (11, {}), {3}: (12, {}), ... | custom-call | flops 335544320 | bytes 23068672 | tf_op jit(solution)/shard_map/bwd_pass/pallas_call | solution.py:220
  593.6 24.3 %conv_back.1 = (bf16[2048,1024]{1,0:T(8,128)(2,1)}, f32[4,8,1024]{2,1,0:T(8,128)}, f32[4,8,1024]{2,1,0:T(8,128)}, f32[4,5,1024]{2,1,0:T(8,128)}) custom-call(bf16[2048,160]{1,0:T(8,128)(2,1)} %maximum_bitcast_fusion.gp_ref, bf16[1024,160]{1,0:T(8,128)(2,1)} %copy.49.xp_ref, f32[2048,1024]{1,0:T(8,128)} %get-tuple-element.87.gx_ref, ...), custom_call_target="tpu_custom_call" | custom-call | flops 838860800 | bytes 20971520 | tf_op jit(solution)/shard_map/conv_back/pallas_call | solution.py:357
  627.3 14.0 %convolution_convert_fusion.1 = bf16[2048,1024]{1,0:T(8,128)(2,1)} fusion(bf16[2048,2048]{1,0:T(8,128)(2,1)} %pad_maximum_fusion, bf16[2048,1024]{1,0:T(8,128)(2,1)} %bitcast.156), kind=kOutput, calls=%fused_computation.52 | convolution fusion | flops 8592031744 | bytes 16777216 | tf_op jit(solution)/shard_map/dot_general | solution.py:383
  652.2 9.8 %fusion.86 = (bf16[1024,2048]{1,0:T(8,128)(2,1)S(1)}, f32[1024,2048]{1,0:T(8,128)S(1)}) fusion(f32[1024,2048]{1,0:T(8,128)} %fusion.89, bf16[1024,1024]{1,0:T(8,128)(2,1)} %bitcast.174, bf16[2048,1024]{1,0:T(8,128)(2,1)} %all-gather.6.cloned.1.call-done), kind=kOutput, calls=%fused_computation.206 | convolution fusion | flops 4299161600 | bytes 27262976 | tf_op jit(solution)/shard_map/dot_general | solution.py:387
  669.3 9.1 %fusion.90 = f32[1024,2048]{1,0:T(8,128)} fusion(bf16[1024,1024]{1,0:T(8,128)(2,1)S(1)} %bitcast.175, bf16[2048,1024]{1,0:T(8,128)(2,1)} %all-gather.4.cloned.1.call-done), kind=kOutput, calls=%fused_computation.210 | convolution fusion | flops 4294967296 | bytes 14680064 | tf_op jit(solution)/shard_map/dot_general | solution.py:387
  681.5 10.2 %fusion.85 = (bf16[1024,2048]{1,0:T(8,128)(2,1)S(1)}, f32[1024,2048]{1,0:T(8,128)}) fusion(f32[1024,2048]{1,0:T(8,128)} %fusion.90, bf16[1024,1024]{1,0:T(8,128)(2,1)S(1)} %bitcast.173, bf16[2048,1024]{1,0:T(8,128)(2,1)} %all-gather.6.cloned.1.call-done), kind=kOutput, calls=%fused_computation.205 | convolution fusion | flops 4299161600 | bytes 27262976 | tf_op jit(solution)/shard_map/dot_general | solution.py:387
  693.7 12.9 %collective-permute-done.34 = bf16[4,128,384]{1,2,0:T(8,128)(2,1)S(1)} collective-permute-done((bf16[4,128,384]{1,2,0:T(8,128)(2,1)}, bf16[4,128,384]{1,2,0:T(8,128)(2,1)S(1)}, u32[]{:S(2)}, u32[]{:S(2)}) %collective-permute-start.34) | collective-permute-done | bytes 393248 | tf_op jit(solution)/shard_map/ppermute | solution.py:436
  728.5 13.8 %collective-permute-done.53 = bf16[128,384]{0,1:T(8,128)(2,1)S(1)} collective-permute-done((bf16[128,384]{0,1:T(8,128)(2,1)S(1)}, bf16[128,384]{0,1:T(8,128)(2,1)S(1)}, u32[]{:S(2)}, u32[]{:S(2)}) %collective-permute-start.53) | collective-permute-done | bytes 98336 | tf_op jit(solution)/shard_map/ppermute | solution.py:391
  (386 shorter events, 273.9 us)
Async XLA Ops:
  7.2 88.1 %all-gather.4.cloned.1.call-start = ((), (), s32[]{:S(2)}) async-start(), calls=%async_computation.2 | async-start | bytes 4718592 | tf_op jit(solution)/shard_map/all_gather | solution.py:565
  9.8 212.0 %all-gather.6.cloned.1.call-start = ((), (), s32[]{:S(2)}) async-start(), calls=%async_computation.3 | async-start | bytes 4718592 | tf_op jit(solution)/shard_map/all_gather | solution.py:566
  12.2 233.6 %all-gather.8.cloned.1.call-start = ((), (), s32[]{:S(2)}) async-start(), calls=%async_computation.4 | async-start | bytes 4718592 | tf_op jit(solution)/shard_map/all_gather | solution.py:567
  12.3 48.8 %collective-permute-start = (bf16[512,2048]{1,0:T(8,128)(2,1)S(1)}, bf16[512,2048]{1,0:T(8,128)(2,1)}, u32[]{:S(2)}, u32[]{:S(2)}) collective-permute-start(bf16[512,2048]{1,0:T(8,128)(2,1)S(1)} %copy-done.2), channel_id=1, source_target_pairs={{0,16},{8,24},{16,0},{24,8},{1,17},{9,25},{17,1},{25,9},{2,18},{10... | collective-permute-start | bytes 6291464 | tf_op jit(solution)/shard_map/ppermute | solution.py:391
  15.3 47.6 %collective-permute-start.1 = (bf16[512,2048]{1,0:T(8,128)(2,1)S(1)}, bf16[512,2048]{1,0:T(8,128)(2,1)}, u32[]{:S(2)}, u32[]{:S(2)}) collective-permute-start(bf16[512,2048]{1,0:T(8,128)(2,1)S(1)} %copy-done.2), channel_id=1, source_target_pairs={{0,8},{8,0},{16,24},{24,16},{1,9},{9,1},{17,25},{25,17},{2,10},{10... | collective-permute-start | bytes 6291464 | tf_op jit(solution)/shard_map/ppermute | solution.py:391
  17.2 575.5 %reduce-scatter.3.cloned.1.call-start = ((), (), s32[]{:S(2)}) async-start(), calls=%async_computation.5 | async-start | bytes 9437184 | tf_op jit(solution)/shard_map/reduce_scatter | solution.py:632
  78.4 56.6 %collective-permute-start.11 = (bf16[512,2048]{1,0:T(8,128)(2,1)S(1)}, bf16[512,2048]{1,0:T(8,128)(2,1)}, u32[]{:S(2)}, u32[]{:S(2)}) collective-permute-start(bf16[512,2048]{1,0:T(8,128)(2,1)S(1)} %copy-done.7), channel_id=1, source_target_pairs={{0,16},{8,24},{16,0},{24,8},{1,17},{9,25},{17,1},{25,9},{2,18},{10... | collective-permute-start | bytes 6291464 | tf_op jit(solution)/shard_map/ppermute | solution.py:391
  113.1 35.3 %collective-permute-start.10 = (bf16[512,2048]{1,0:T(8,128)(2,1)S(1)}, bf16[512,2048]{1,0:T(8,128)(2,1)}, u32[]{:S(2)}, u32[]{:S(2)}) collective-permute-start(bf16[512,2048]{1,0:T(8,128)(2,1)S(1)} %copy-done.7), channel_id=1, source_target_pairs={{0,8},{8,0},{16,24},{24,16},{1,9},{9,1},{17,25},{25,17},{2,10},{10... | collective-permute-start | bytes 6291464 | tf_op jit(solution)/shard_map/ppermute | solution.py:391
  135.0 27.6 %collective-permute-start.12 = (bf16[512,2048]{1,0:T(8,128)(2,1)}, bf16[512,2048]{1,0:T(8,128)(2,1)}, u32[]{:S(2)}, u32[]{:S(2)}) collective-permute-start(bf16[512,2048]{1,0:T(8,128)(2,1)} %collective-permute-done.11), channel_id=1, source_target_pairs={{0,8},{8,0},{16,24},{24,16},{1,9},{9,1},{17,25},{25,17},{2,10},{10... | collective-permute-start | bytes 6291464 | tf_op jit(solution)/shard_map/ppermute | solution.py:391
  236.7 32.5 %collective-permute-start.15 = (bf16[68,1024]{1,0:T(8,128)(2,1)S(1)}, bf16[68,1024]{1,0:T(8,128)(2,1)S(1)}, u32[]{:S(2)}, u32[]{:S(2)}) collective-permute-start(bf16[68,1024]{1,0:T(8,128)(2,1)S(1)} %pad_maximum_fusion.8), channel_id=1, source_target_pairs={{0,4},{1,5},{2,6},{3,7},{8,12},{9,13},{10,14},{11,15},{16,20},{17,... | collective-permute-start | bytes 417800 | tf_op jit(solution)/shard_map/ppermute | solution.py:471
  241.4 27.8 %collective-permute-start.14 = (bf16[68,1024]{1,0:T(8,128)(2,1)S(1)}, bf16[68,1024]{1,0:T(8,128)(2,1)S(1)}, u32[]{:S(2)}, u32[]{:S(2)}) collective-permute-start(bf16[68,1024]{1,0:T(8,128)(2,1)S(1)} %pad_maximum_fusion.8), channel_id=1, source_target_pairs={{0,2},{1,3},{2,4},{3,5},{4,6},{5,7},{8,10},{9,11},{10,12},{11,13},... | collective-permute-start | bytes 417800 | tf_op jit(solution)/shard_map/ppermute | solution.py:471
  386.1 23.2 %collective-permute-start.18 = (bf16[512,2048]{1,0:T(8,128)(2,1)S(1)}, bf16[512,2048]{1,0:T(8,128)(2,1)S(1)}, u32[]{:S(2)}, u32[]{:S(2)}) collective-permute-start(bf16[512,2048]{1,0:T(8,128)(2,1)S(1)} %get-tuple-element.121), channel_id=1, source_target_pairs={{0,8},{8,0},{16,24},{24,16},{1,9},{9,1},{17,25},{25,17},{2,10},{10... | collective-permute-start | bytes 6291464 | tf_op jit(solution)/shard_map/ppermute | solution.py:391
  413.6 345.5 %reduce-scatter.5.cloned.1.call-start = ((), (), s32[]{:S(2)}) async-start(), calls=%async_computation.6 | async-start | bytes 4718592 | tf_op jit(solution)/shard_map/reduce_scatter | solution.py:632
  413.6 69.6 %collective-permute-start.17 = (bf16[512,2048]{1,0:T(8,128)(2,1)}, bf16[512,2048]{1,0:T(8,128)(2,1)}, u32[]{:S(2)}, u32[]{:S(2)}) collective-permute-start(bf16[512,2048]{1,0:T(8,128)(2,1)} %get-tuple-element.120), channel_id=1, source_target_pairs={{0,8},{8,0},{16,24},{24,16},{1,9},{9,1},{17,25},{25,17},{2,10},{10... | collective-permute-start | bytes 6291464 | tf_op jit(solution)/shard_map/ppermute | solution.py:391
  413.7 69.5 %collective-permute-start.23 = (bf16[512,2048]{1,0:T(8,128)(2,1)}, bf16[512,2048]{1,0:T(8,128)(2,1)}, u32[]{:S(2)}, u32[]{:S(2)}) collective-permute-start(bf16[512,2048]{1,0:T(8,128)(2,1)} %fusion.18.refs_10_), channel_id=1, source_target_pairs={{0,16},{8,24},{16,0},{24,8},{1,17},{9,25},{17,1},{25,9},{2,18},{10... | collective-permute-start | bytes 6291464 | tf_op jit(solution)/shard_map/ppermute | solution.py:391
  592.8 59.4 %collective-permute-start.35 = (bf16[512,1024]{1,0:T(8,128)(2,1)}, bf16[512,1024]{1,0:T(8,128)(2,1)}, u32[]{:S(2)}, u32[]{:S(2)}) collective-permute-start(bf16[512,1024]{1,0:T(8,128)(2,1)} %reduce-scatter.3.cloned.1.call-done), channel_id=1, source_target_pairs={{0,8},{8,0},{16,24},{24,16},{1,9},{9,1},{17,25},{25,17},{2,10},{10... | collective-permute-start | bytes 3145736 | tf_op jit(solution)/shard_map/ppermute | solution.py:391
  592.9 48.4 %collective-permute-start.36 = (bf16[512,1024]{1,0:T(8,128)(2,1)}, bf16[512,1024]{1,0:T(8,128)(2,1)}, u32[]{:S(2)}, u32[]{:S(2)}) collective-permute-start(bf16[512,1024]{1,0:T(8,128)(2,1)} %reduce-scatter.3.cloned.1.call-done), channel_id=1, source_target_pairs={{0,16},{8,24},{16,0},{24,8},{1,17},{9,25},{17,1},{25,9},{2,18},{10... | collective-permute-start | bytes 3145736 | tf_op jit(solution)/shard_map/ppermute | solution.py:391
  664.4 42.2 %collective-permute-start.34 = (bf16[4,128,384]{1,2,0:T(8,128)(2,1)}, bf16[4,128,384]{1,2,0:T(8,128)(2,1)S(1)}, u32[]{:S(2)}, u32[]{:S(2)}) collective-permute-start(bf16[4,128,384]{1,2,0:T(8,128)(2,1)} %dynamic-slice_convert_fusion), channel_id=1, source_target_pairs={{0,4},{1,5},{2,6},{3,7},{4,0},{5,1},{6,2},{7,3},{8,12},{9,13},{10,... | collective-permute-start | bytes 1179656 | tf_op jit(solution)/shard_map/ppermute | solution.py:436
  669.3 37.3 %collective-permute-start.31 = (bf16[256,2048]{1,0:T(8,128)(2,1)}, bf16[256,2048]{1,0:T(8,128)(2,1)}, u32[]{:S(2)}, u32[]{:S(2)}) collective-permute-start(bf16[256,2048]{1,0:T(8,128)(2,1)} %get-tuple-element.122), channel_id=1, source_target_pairs={{0,8},{8,0},{16,24},{24,16},{1,9},{9,1},{17,25},{25,17},{2,10},{10... | collective-permute-start | bytes 3145736 | tf_op jit(solution)/shard_map/ppermute | solution.py:391
  679.8 26.9 %collective-permute-start.33 = (bf16[256,2048]{1,0:T(8,128)(2,1)}, bf16[256,2048]{1,0:T(8,128)(2,1)}, u32[]{:S(2)}, u32[]{:S(2)}) collective-permute-start(bf16[256,2048]{1,0:T(8,128)(2,1)} %fusion.26), channel_id=1, source_target_pairs={{0,16},{8,24},{16,0},{24,8},{1,17},{9,25},{17,1},{25,9},{2,18},{10... | collective-permute-start | bytes 3145736 | tf_op jit(solution)/shard_map/ppermute | solution.py:391
  715.0 44.1 %collective-permute-start.40 = (bf16[256,2048]{1,0:T(8,128)(2,1)}, bf16[256,2048]{1,0:T(8,128)(2,1)}, u32[]{:S(2)}, u32[]{:S(2)}) collective-permute-start(bf16[256,2048]{1,0:T(8,128)(2,1)} %get-tuple-element.118), channel_id=1, source_target_pairs={{0,16},{8,24},{16,0},{24,8},{1,17},{9,25},{17,1},{25,9},{2,18},{10... | collective-permute-start | bytes 3145736 | tf_op jit(solution)/shard_map/ppermute | solution.py:391
  723.7 18.6 %collective-permute-start.53 = (bf16[128,384]{0,1:T(8,128)(2,1)S(1)}, bf16[128,384]{0,1:T(8,128)(2,1)S(1)}, u32[]{:S(2)}, u32[]{:S(2)}) collective-permute-start(bf16[128,384]{0,1:T(8,128)(2,1)S(1)} %fusion.51), channel_id=1, source_target_pairs={{0,16},{8,24},{16,0},{24,8},{1,17},{9,25},{17,1},{25,9},{2,18},{10... | collective-permute-start | bytes 294920 | tf_op jit(solution)/shard_map/ppermute | solution.py:391
  728.4 22.7 %collective-permute-start.55 = (bf16[128,384]{0,1:T(8,128)(2,1)S(1)}, bf16[128,384]{0,1:T(8,128)(2,1)S(1)}, u32[]{:S(2)}, u32[]{:S(2)}) collective-permute-start(bf16[128,384]{0,1:T(8,128)(2,1)S(1)} %fusion.51), channel_id=1, source_target_pairs={{0,8},{8,0},{16,24},{24,16},{1,9},{9,1},{17,25},{25,17},{2,10},{10... | collective-permute-start | bytes 294920 | tf_op jit(solution)/shard_map/ppermute | solution.py:391
  766.4 18.2 %collective-permute-start.48 = (bf16[256,1024]{1,0:T(8,128)(2,1)S(1)}, bf16[256,1024]{1,0:T(8,128)(2,1)S(1)}, u32[]{:S(2)}, u32[]{:S(2)}) collective-permute-start(bf16[256,1024]{1,0:T(8,128)(2,1)S(1)} %copy-done.30), channel_id=1, source_target_pairs={{0,8},{8,0},{16,24},{24,16},{1,9},{9,1},{17,25},{25,17},{2,10},{10... | collective-permute-start | bytes 1572872 | tf_op jit(solution)/shard_map/ppermute | solution.py:391
  (90 other events, 868.2 us)
Sparse Core Ops, SparseCore 0:
  10.7 84.5 all-gather.3
  97.4 72.3 all-gather.5
  171.9 73.8 all-gather.7
  413.7 148.2 reduce-scatter.2
  652.4 106.6 reduce-scatter.4

commit v6 on v5

--- a/solution.py
+++ b/solution.py
@@ -299,7 +299,7 @@
     o_ref[...] = (pre * jax.nn.sigmoid(pre)).astype(BF16)
 
 
-def conv_pass(conv_in, edge, wb, Q, at, prev, EB=256):
+def conv_pass(conv_in, edge, wb, Q, at, prev, EB=512):
     T, E = conv_in.shape
     L = T // Q
     at = at * (E // EB)
@@ -347,7 +347,7 @@
     tail_ref[...] = g_in[L - 8:, :]
 
 
-def conv_back(g_projected, x_proj, gx, conv_in, edge, wb, Q, at, EB=256):
+def conv_back(g_projected, x_proj, gx, conv_in, edge, wb, Q, at, EB=512):
     T, E = conv_in.shape
     L = T // Q
     at = at * (E // EB)

time: 808 us -> 808 us (level)
  transfers between devices with their start and end apart: 61 -> 61, of which waited for: 22 -> 22; matrix products, arithmetic and copies ran while one was open for 31% -> 30% of each run, Pallas kernels for 26% -> 26%
where the time goes in v6:
time: 808 us; the launch traced here: 799 us
  Pallas kernels  289 us (36%)
  matrix products  153 us (19%)
  waiting for transfers between devices  97.3 us (12%)
  other arithmetic  89 us (11%)
  starting transfers between devices  62.4 us (8%)
  local copies, waits for them, and re-layouts  56.7 us (7%)
  blocking collectives  36.7 us (5%)
  between operations  15.5 us (2%)
    pallas_call x2, Pallas kernels, bwd_pass(): pl.pallas_call(partial(bwd_kernel, U, TB, n_in), grid=(Q, 1, NC), in_spec...  132 us
    pallas_call x1, Pallas kernels, fwd_pass(): pl.pallas_call(partial(fwd_kernel, U, TB), grid=(Q, NE, NC), in_specs=[ro...  72.7 us
    dot_general x6, matrix products, contract_cols(): lax.dot_general(left, right, (((1,), (1,)), ((), ())), preferred_element_...  54.1 us
    dot_general x7, matrix products, contract_rows(): lax.dot_general(left, right, (((0,), (0,)), ((), ())), preferred_element_...  51.3 us
    ppermute x36, waiting for transfers between devices, swap(): lax.ppermute(value, 'rep', [(i, i ^ flip) for i in range(lax.axis_size('r...  37.7 us
    all_gather x1, blocking collectives, on_device(): small_all = lax.all_gather(small, 'shard', axis=0, tiled=True)  36.7 us
    pallas_call x1, Pallas kernels, first_pass(): pl.pallas_call(partial(first_kernel, U), grid=(Q, NE, NC), in_specs=[row,...  30.6 us
    pallas_call x1, Pallas kernels, conv_back(): pl.pallas_call(conv_back_kernel, grid=(Q, E // EB), in_specs=[pl.BlockSpe...  23.8 us
  transfers between devices with their start and end apart: 61, of which 22 were waited for; matrix products, arithmetic and copies ran while one was open for 30% of the time, Pallas kernels for 26%

profile of v6, /device:TPU:0, one launch (start us, length us, event | category | flops | bytes accessed | tf_op | source)
XLA Modules:
  0.0 799.0 jit_solution(3746667263630137325)
XLA Ops:
  23.3 36.7 %all_gather.12 = bf16[1024,313]{0,1:T(8,128)(2,1)S(1)} all-gather(bf16[128,313]{0,1:T(8,128)(2,1)S(1)} %concatenate.75), channel_id=1, replica_groups=mesh['rep'=4,'shard'=8] {'shard'}, dimensions={0}, use_global_device_ids=true | all-gather | bytes 721152 | tf_op jit(solution)/shard_map/all_gather | solution.py:562
  80.1 15.2 %all-gather.4.cloned.1.call-done = bf16[2048,1024]{1,0:T(8,128)(2,1)} async-done(((bf16[256,1024]{1,0:T(8,128)(2,1)}), bf16[2048,1024]{1,0:T(8,128)(2,1)}) %all-gather.4.cloned.1.call-update) | async-done | bytes 4194320 | tf_op jit(solution)/shard_map/all_gather | solution.py:565
  95.3 12.5 %convolution_convert_fusion.x_ref = bf16[2048,1024]{1,0:T(8,128)(2,1)S(1)} fusion(bf16[2048,2048]{1,0:T(8,128)(2,1)} %pad_maximum_fusion, bf16[2048,1024]{1,0:T(8,128)(2,1)} %all-gather.4.cloned.1.call-done), kind=kOutput, calls=%fused_computation.51 | convolution fusion | flops 8592031744 | bytes 16777216 | tf_op jit(solution)/shard_map/dot_general | solution.py:591
  114.5 12.0 %conv_pass.1.x_ref.refs_1_ = bf16[2048,1024]{1,0:T(8,128)(2,1)} custom-call(bf16[2048,1024]{1,0:T(8,128)(2,1)} %copy-done.6, f32[4,8,1024]{2,1,0:T(8,128)} %concatenate.77.edge_ref, f32[5,1024]{1,0:T(8,128)} %convert_bitcast_fusion.1.w_ref), custom_call_target="tpu_custom_call" | custom-call | flops 25165824 | bytes 8388608 | tf_op jit(solution)/shard_map/conv_pass/pallas_call | solution.py:307
  166.6 9.0 %broadcast_in_dim.23.b_ref.refs_3_ = f32[2048,16,128]{2,1,0:T(8,128)} broadcast(f32[2048,16]{1,0:T(8,128)S(1)} %copy-done.12), dimensions={0,1} | broadcast | bytes 16908288 | tf_op jit(solution)/shard_map/broadcast_in_dim | solution.py:599
  175.6 8.9 %broadcast_in_dim.24.refs_0_.c_ref.refs_4_ = f32[2048,16,128]{2,1,0:T(8,128)} broadcast(f32[2048,16]{1,0:T(8,128)S(1)} %copy-done.13), dimensions={0,1} | broadcast | bytes 16908288 | tf_op jit(solution)/shard_map/broadcast_in_dim | solution.py:600
  184.5 30.6 %first_pass.1 = f32[4,16,1024]{2,1,0:T(8,128)} custom-call(f32[2048,1024]{1,0:T(8,128)} %get-tuple-element.175.dt_ref.refs_0_, bf16[2048,1024]{1,0:T(8,128)(2,1)} %conv_pass.1.x_ref.refs_1_, f32[2048,16,128]{2,1,0:T(8,128)} %broadcast_in_dim.23.b_ref.refs_3_, f32[16,1024]{1,0:T(8,128)} %get-tuple-element.143.a_ref.refs_5_, ...), custom_call_target="tpu_custom_call" | custom-call | flops 167772160 | bytes 20971520 | tf_op jit(solution)/shard_map/first_pass/pallas_call | solution.py:47
  219.1 14.6 %fusion.87.gate_ref = f32[2048,1024]{1,0:T(8,128)} fusion(bf16[2048,2048]{1,0:T(8,128)(2,1)} %pad_maximum_fusion, bf16[2048,1024]{1,0:T(8,128)(2,1)} %all-gather.6.cloned.1.call-done), kind=kOutput, calls=%fused_computation.207 | convolution fusion | flops 8589934592 | bytes 20971520 | tf_op jit(solution)/shard_map/dot_general | solution.py:604
  247.7 14.5 %fusion.88.gg_ref = f32[2048,1024]{1,0:T(8,128)} fusion(bf16[2048,2048]{1,0:T(8,128)(2,1)} %pad_maximum_fusion.1.refs_1_, bf16[1024,2048]{1,0:T(8,128)(2,1)} %all-gather.8.cloned.1.call-done), kind=kOutput, calls=%fused_computation.208 | convolution fusion | flops 8589934592 | bytes 20971520 | tf_op jit(solution)/shard_map/dot_general | solution.py:387
  262.1 8.0 collective-permute-start.16
  273.7 72.7 %fwd_pass.1 = (bf16[2048,1024]{1,0:T(8,128)(2,1)}, bf16[2048,1024]{1,0:T(8,128)(2,1)}, f32[2048,1024]{1,0:T(8,128)}, f32[8,16,1024]{2,1,0:T(8,128)}, f32[4,16,1024]{2,1,0:T(8,128)}) custom-call(f32[2048,1024]{1,0:T(8,128)} %get-tuple-element.175.dt_ref.refs_0_, bf16[2048,1024]{1,0:T(8,128)(2,1)} %conv_pass.1.x_ref.refs_1_, f32[2048,1024]{1,0:T(8,128)} %fusion.87.gate_ref, ...), custom_call_target="tpu_custom_call" | custom-call | flops 369098752 | bytes 46137344 | tf_op jit(solution)/shard_map/fwd_pass/pallas_call | solution.py:115
  346.4 8.2 %fusion.31 = bf16[1024,1024]{1,0:T(8,128)(2,1)S(1)} fusion(bf16[2048,1024]{1,0:T(8,128)(2,1)} %get-tuple-element.69, bf16[2048,2048]{1,0:T(8,128)(2,1)} %pad_maximum_fusion.1.refs_1_), kind=kOutput, calls=%fused_computation.65 | convolution fusion | flops 4296015872 | bytes 10485760 | tf_op jit(solution)/shard_map/dot_general | solution.py:383
  354.6 11.7 %convolution_convert_fusion.2 = bf16[2048,1024]{1,0:T(8,128)(2,1)S(1)} fusion(bf16[2048,2048]{1,0:T(8,128)(2,1)} %pad_maximum_fusion, bf16[2048,1024]{1,0:T(8,128)(2,1)S(1)} %copy-done.14), kind=kOutput, calls=%fused_computation.53 | convolution fusion | flops 8592031744 | bytes 16777216 | tf_op jit(solution)/shard_map/dot_general | solution.py:383
  366.3 16.7 %fusion.84 = (bf16[2048,2048]{1,0:T(8,128)(2,1)}, f32[2048,2048]{1,0:T(8,128)}) fusion(bf16[2048,1024]{1,0:T(8,128)(2,1)} %get-tuple-element.69, bf16[1024,2048]{1,0:T(8,128)(2,1)S(1)} %copy-done.48), kind=kOutput, calls=%fused_computation.204 | convolution fusion | flops 8594128896 | bytes 33554432 | tf_op jit(solution)/shard_map/dot_general | solution.py:617
  401.3 7.9 collective-permute-done.21
  418.2 66.1 %bwd_pass.2 = (bf16[2048,1024]{1,0:T(8,128)(2,1)}, f32[2048,1024]{1,0:T(8,128)}, f32[2,1,32768]{2,1,0:T(1,128)}, f32[2,1,32768]{2,1,0:T(1,128)}, f32[4,16,1024]{2,1,0:T(8,128)}, /*index=5*/f32[4,2,1024]{2,1,0:T(2,128)}) custom-call(f32[2048,1024]{1,0:T(8,128)} %get-tuple-element.175.dt_ref.refs_0_, bf16[2048,1024]{1,0:T(8,128)(2,1)} %conv_pass.1.x_ref.refs_1_, ...), custom_call_target="tpu_custom_call" | custom-call | flops 335544320 | bytes 23068672 | tf_op jit(solution)/shard_map/bwd_pass/pallas_call | solution.py:220
  491.6 66.0 %bwd_pass.3 = (bf16[2048,1024]{1,0:T(8,128)(2,1)}, f32[2048,1024]{1,0:T(8,128)}, f32[2,1,32768]{2,1,0:T(1,128)}, f32[2,1,32768]{2,1,0:T(1,128)}, f32[4,16,1024]{2,1,0:T(8,128)}, /*index=5*/f32[4,2,1024]{2,1,0:T(2,128)}) custom-call(f32[2048,1024]{1,0:T(8,128)} %get-tuple-element.175.dt_r, ...), custom_call_target="tpu_custom_call", output_to_operand_aliasing={{0}: (9, {}), {1}: (10, {}), {2}: (11, {}), {3}: (12, {}), ... | custom-call | flops 335544320 | bytes 23068672 | tf_op jit(solution)/shard_map/bwd_pass/pallas_call | solution.py:220
  594.6 23.8 %conv_back.1 = (bf16[2048,1024]{1,0:T(8,128)(2,1)}, f32[4,8,1024]{2,1,0:T(8,128)}, f32[4,8,1024]{2,1,0:T(8,128)}, f32[4,5,1024]{2,1,0:T(8,128)}) custom-call(bf16[2048,160]{1,0:T(8,128)(2,1)} %maximum_bitcast_fusion.gp_ref, bf16[1024,160]{1,0:T(8,128)(2,1)} %copy.49.xp_ref, f32[2048,1024]{1,0:T(8,128)} %get-tuple-element.87.gx_ref, ...), custom_call_target="tpu_custom_call" | custom-call | flops 838860800 | bytes 20971520 | tf_op jit(solution)/shard_map/conv_back/pallas_call | solution.py:357
  627.8 14.0 %convolution_convert_fusion.1 = bf16[2048,1024]{1,0:T(8,128)(2,1)} fusion(bf16[2048,2048]{1,0:T(8,128)(2,1)} %pad_maximum_fusion, bf16[2048,1024]{1,0:T(8,128)(2,1)} %bitcast.156), kind=kOutput, calls=%fused_computation.52 | convolution fusion | flops 8592031744 | bytes 16777216 | tf_op jit(solution)/shard_map/dot_general | solution.py:383
  652.8 9.8 %fusion.86 = (bf16[1024,2048]{1,0:T(8,128)(2,1)S(1)}, f32[1024,2048]{1,0:T(8,128)S(1)}) fusion(f32[1024,2048]{1,0:T(8,128)} %fusion.89, bf16[1024,1024]{1,0:T(8,128)(2,1)} %bitcast.174, bf16[2048,1024]{1,0:T(8,128)(2,1)} %all-gather.6.cloned.1.call-done), kind=kOutput, calls=%fused_computation.206 | convolution fusion | flops 4299161600 | bytes 27262976 | tf_op jit(solution)/shard_map/dot_general | solution.py:387
  670.0 9.1 %fusion.90 = f32[1024,2048]{1,0:T(8,128)} fusion(bf16[1024,1024]{1,0:T(8,128)(2,1)S(1)} %bitcast.175, bf16[2048,1024]{1,0:T(8,128)(2,1)} %all-gather.4.cloned.1.call-done), kind=kOutput, calls=%fused_computation.210 | convolution fusion | flops 4294967296 | bytes 14680064 | tf_op jit(solution)/shard_map/dot_general | solution.py:387
  682.1 10.2 %fusion.85 = (bf16[1024,2048]{1,0:T(8,128)(2,1)S(1)}, f32[1024,2048]{1,0:T(8,128)}) fusion(f32[1024,2048]{1,0:T(8,128)} %fusion.90, bf16[1024,1024]{1,0:T(8,128)(2,1)S(1)} %bitcast.173, bf16[2048,1024]{1,0:T(8,128)(2,1)} %all-gather.6.cloned.1.call-done), kind=kOutput, calls=%fused_computation.205 | convolution fusion | flops 4299161600 | bytes 27262976 | tf_op jit(solution)/shard_map/dot_general | solution.py:387
  694.3 12.9 %collective-permute-done.34 = bf16[4,128,384]{1,2,0:T(8,128)(2,1)S(1)} collective-permute-done((bf16[4,128,384]{1,2,0:T(8,128)(2,1)}, bf16[4,128,384]{1,2,0:T(8,128)(2,1)S(1)}, u32[]{:S(2)}, u32[]{:S(2)}) %collective-permute-start.34) | collective-permute-done | bytes 393248 | tf_op jit(solution)/shard_map/ppermute | solution.py:436
  729.0 14.0 %collective-permute-done.53 = bf16[128,384]{0,1:T(8,128)(2,1)S(1)} collective-permute-done((bf16[128,384]{0,1:T(8,128)(2,1)S(1)}, bf16[128,384]{0,1:T(8,128)(2,1)S(1)}, u32[]{:S(2)}, u32[]{:S(2)}) %collective-permute-start.53) | collective-permute-done | bytes 98336 | tf_op jit(solution)/shard_map/ppermute | solution.py:391
  (386 shorter events, 278.4 us)
Async XLA Ops:
  7.2 88.1 %all-gather.4.cloned.1.call-start = ((), (), s32[]{:S(2)}) async-start(), calls=%async_computation.2 | async-start | bytes 4718592 | tf_op jit(solution)/shard_map/all_gather | solution.py:565
  9.8 209.3 %all-gather.6.cloned.1.call-start = ((), (), s32[]{:S(2)}) async-start(), calls=%async_computation.3 | async-start | bytes 4718592 | tf_op jit(solution)/shard_map/all_gather | solution.py:566
  12.2 235.4 %all-gather.8.cloned.1.call-start = ((), (), s32[]{:S(2)}) async-start(), calls=%async_computation.4 | async-start | bytes 4718592 | tf_op jit(solution)/shard_map/all_gather | solution.py:567
  12.3 48.8 %collective-permute-start = (bf16[512,2048]{1,0:T(8,128)(2,1)S(1)}, bf16[512,2048]{1,0:T(8,128)(2,1)}, u32[]{:S(2)}, u32[]{:S(2)}) collective-permute-start(bf16[512,2048]{1,0:T(8,128)(2,1)S(1)} %copy-done.2), channel_id=1, source_target_pairs={{0,16},{8,24},{16,0},{24,8},{1,17},{9,25},{17,1},{25,9},{2,18},{10... | collective-permute-start | bytes 6291464 | tf_op jit(solution)/shard_map/ppermute | solution.py:391
  15.3 47.6 %collective-permute-start.1 = (bf16[512,2048]{1,0:T(8,128)(2,1)S(1)}, bf16[512,2048]{1,0:T(8,128)(2,1)}, u32[]{:S(2)}, u32[]{:S(2)}) collective-permute-start(bf16[512,2048]{1,0:T(8,128)(2,1)S(1)} %copy-done.2), channel_id=1, source_target_pairs={{0,8},{8,0},{16,24},{24,16},{1,9},{9,1},{17,25},{25,17},{2,10},{10... | collective-permute-start | bytes 6291464 | tf_op jit(solution)/shard_map/ppermute | solution.py:391
  17.2 576.6 %reduce-scatter.3.cloned.1.call-start = ((), (), s32[]{:S(2)}) async-start(), calls=%async_computation.5 | async-start | bytes 9437184 | tf_op jit(solution)/shard_map/reduce_scatter | solution.py:632
  78.4 53.8 %collective-permute-start.11 = (bf16[512,2048]{1,0:T(8,128)(2,1)S(1)}, bf16[512,2048]{1,0:T(8,128)(2,1)}, u32[]{:S(2)}, u32[]{:S(2)}) collective-permute-start(bf16[512,2048]{1,0:T(8,128)(2,1)S(1)} %copy-done.7), channel_id=1, source_target_pairs={{0,16},{8,24},{16,0},{24,8},{1,17},{9,25},{17,1},{25,9},{2,18},{10... | collective-permute-start | bytes 6291464 | tf_op jit(solution)/shard_map/ppermute | solution.py:391
  113.3 32.2 %collective-permute-start.10 = (bf16[512,2048]{1,0:T(8,128)(2,1)S(1)}, bf16[512,2048]{1,0:T(8,128)(2,1)}, u32[]{:S(2)}, u32[]{:S(2)}) collective-permute-start(bf16[512,2048]{1,0:T(8,128)(2,1)S(1)} %copy-done.7), channel_id=1, source_target_pairs={{0,8},{8,0},{16,24},{24,16},{1,9},{9,1},{17,25},{25,17},{2,10},{10... | collective-permute-start | bytes 6291464 | tf_op jit(solution)/shard_map/ppermute | solution.py:391
  132.2 27.6 %collective-permute-start.12 = (bf16[512,2048]{1,0:T(8,128)(2,1)}, bf16[512,2048]{1,0:T(8,128)(2,1)}, u32[]{:S(2)}, u32[]{:S(2)}) collective-permute-start(bf16[512,2048]{1,0:T(8,128)(2,1)} %collective-permute-done.11), channel_id=1, source_target_pairs={{0,8},{8,0},{16,24},{24,16},{1,9},{9,1},{17,25},{25,17},{2,10},{10... | collective-permute-start | bytes 6291464 | tf_op jit(solution)/shard_map/ppermute | solution.py:391
  233.9 36.3 %collective-permute-start.15 = (bf16[68,1024]{1,0:T(8,128)(2,1)S(1)}, bf16[68,1024]{1,0:T(8,128)(2,1)S(1)}, u32[]{:S(2)}, u32[]{:S(2)}) collective-permute-start(bf16[68,1024]{1,0:T(8,128)(2,1)S(1)} %pad_maximum_fusion.8), channel_id=1, source_target_pairs={{0,4},{1,5},{2,6},{3,7},{8,12},{9,13},{10,14},{11,15},{16,20},{17,... | collective-permute-start | bytes 417800 | tf_op jit(solution)/shard_map/ppermute | solution.py:471
  239.4 30.9 %collective-permute-start.14 = (bf16[68,1024]{1,0:T(8,128)(2,1)S(1)}, bf16[68,1024]{1,0:T(8,128)(2,1)S(1)}, u32[]{:S(2)}, u32[]{:S(2)}) collective-permute-start(bf16[68,1024]{1,0:T(8,128)(2,1)S(1)} %pad_maximum_fusion.8), channel_id=1, source_target_pairs={{0,2},{1,3},{2,4},{3,5},{4,6},{5,7},{8,10},{9,11},{10,12},{11,13},... | collective-permute-start | bytes 417800 | tf_op jit(solution)/shard_map/ppermute | solution.py:471
  387.1 23.2 %collective-permute-start.18 = (bf16[512,2048]{1,0:T(8,128)(2,1)S(1)}, bf16[512,2048]{1,0:T(8,128)(2,1)S(1)}, u32[]{:S(2)}, u32[]{:S(2)}) collective-permute-start(bf16[512,2048]{1,0:T(8,128)(2,1)S(1)} %get-tuple-element.121), channel_id=1, source_target_pairs={{0,8},{8,0},{16,24},{24,16},{1,9},{9,1},{17,25},{25,17},{2,10},{10... | collective-permute-start | bytes 6291464 | tf_op jit(solution)/shard_map/ppermute | solution.py:391
  414.6 345.1 %reduce-scatter.5.cloned.1.call-start = ((), (), s32[]{:S(2)}) async-start(), calls=%async_computation.6 | async-start | bytes 4718592 | tf_op jit(solution)/shard_map/reduce_scatter | solution.py:632
  414.7 69.6 %collective-permute-start.17 = (bf16[512,2048]{1,0:T(8,128)(2,1)}, bf16[512,2048]{1,0:T(8,128)(2,1)}, u32[]{:S(2)}, u32[]{:S(2)}) collective-permute-start(bf16[512,2048]{1,0:T(8,128)(2,1)} %get-tuple-element.120), channel_id=1, source_target_pairs={{0,8},{8,0},{16,24},{24,16},{1,9},{9,1},{17,25},{25,17},{2,10},{10... | collective-permute-start | bytes 6291464 | tf_op jit(solution)/shard_map/ppermute | solution.py:391
  414.7 69.5 %collective-permute-start.23 = (bf16[512,2048]{1,0:T(8,128)(2,1)}, bf16[512,2048]{1,0:T(8,128)(2,1)}, u32[]{:S(2)}, u32[]{:S(2)}) collective-permute-start(bf16[512,2048]{1,0:T(8,128)(2,1)} %fusion.18.refs_10_), channel_id=1, source_target_pairs={{0,16},{8,24},{16,0},{24,8},{1,17},{9,25},{17,1},{25,9},{2,18},{10... | collective-permute-start | bytes 6291464 | tf_op jit(solution)/shard_map/ppermute | solution.py:391
  593.9 58.9 %collective-permute-start.35 = (bf16[512,1024]{1,0:T(8,128)(2,1)}, bf16[512,1024]{1,0:T(8,128)(2,1)}, u32[]{:S(2)}, u32[]{:S(2)}) collective-permute-start(bf16[512,1024]{1,0:T(8,128)(2,1)} %reduce-scatter.3.cloned.1.call-done), channel_id=1, source_target_pairs={{0,8},{8,0},{16,24},{24,16},{1,9},{9,1},{17,25},{25,17},{2,10},{10... | collective-permute-start | bytes 3145736 | tf_op jit(solution)/shard_map/ppermute | solution.py:391
  594.0 47.8 %collective-permute-start.36 = (bf16[512,1024]{1,0:T(8,128)(2,1)}, bf16[512,1024]{1,0:T(8,128)(2,1)}, u32[]{:S(2)}, u32[]{:S(2)}) collective-permute-start(bf16[512,1024]{1,0:T(8,128)(2,1)} %reduce-scatter.3.cloned.1.call-done), channel_id=1, source_target_pairs={{0,16},{8,24},{16,0},{24,8},{1,17},{9,25},{17,1},{25,9},{2,18},{10... | collective-permute-start | bytes 3145736 | tf_op jit(solution)/shard_map/ppermute | solution.py:391
  664.9 42.2 %collective-permute-start.34 = (bf16[4,128,384]{1,2,0:T(8,128)(2,1)}, bf16[4,128,384]{1,2,0:T(8,128)(2,1)S(1)}, u32[]{:S(2)}, u32[]{:S(2)}) collective-permute-start(bf16[4,128,384]{1,2,0:T(8,128)(2,1)} %dynamic-slice_convert_fusion), channel_id=1, source_target_pairs={{0,4},{1,5},{2,6},{3,7},{4,0},{5,1},{6,2},{7,3},{8,12},{9,13},{10,... | collective-permute-start | bytes 1179656 | tf_op jit(solution)/shard_map/ppermute | solution.py:436
  670.0 37.3 %collective-permute-start.31 = (bf16[256,2048]{1,0:T(8,128)(2,1)}, bf16[256,2048]{1,0:T(8,128)(2,1)}, u32[]{:S(2)}, u32[]{:S(2)}) collective-permute-start(bf16[256,2048]{1,0:T(8,128)(2,1)} %get-tuple-element.122), channel_id=1, source_target_pairs={{0,8},{8,0},{16,24},{24,16},{1,9},{9,1},{17,25},{25,17},{2,10},{10... | collective-permute-start | bytes 3145736 | tf_op jit(solution)/shard_map/ppermute | solution.py:391
  680.4 26.9 %collective-permute-start.33 = (bf16[256,2048]{1,0:T(8,128)(2,1)}, bf16[256,2048]{1,0:T(8,128)(2,1)}, u32[]{:S(2)}, u32[]{:S(2)}) collective-permute-start(bf16[256,2048]{1,0:T(8,128)(2,1)} %fusion.26), channel_id=1, source_target_pairs={{0,16},{8,24},{16,0},{24,8},{1,17},{9,25},{17,1},{25,9},{2,18},{10... | collective-permute-start | bytes 3145736 | tf_op jit(solution)/shard_map/ppermute | solution.py:391
  715.6 44.1 %collective-permute-start.40 = (bf16[256,2048]{1,0:T(8,128)(2,1)}, bf16[256,2048]{1,0:T(8,128)(2,1)}, u32[]{:S(2)}, u32[]{:S(2)}) collective-permute-start(bf16[256,2048]{1,0:T(8,128)(2,1)} %get-tuple-element.118), channel_id=1, source_target_pairs={{0,16},{8,24},{16,0},{24,8},{1,17},{9,25},{17,1},{25,9},{2,18},{10... | collective-permute-start | bytes 3145736 | tf_op jit(solution)/shard_map/ppermute | solution.py:391
  724.2 18.7 %collective-permute-start.53 = (bf16[128,384]{0,1:T(8,128)(2,1)S(1)}, bf16[128,384]{0,1:T(8,128)(2,1)S(1)}, u32[]{:S(2)}, u32[]{:S(2)}) collective-permute-start(bf16[128,384]{0,1:T(8,128)(2,1)S(1)} %fusion.51), channel_id=1, source_target_pairs={{0,16},{8,24},{16,0},{24,8},{1,17},{9,25},{17,1},{25,9},{2,18},{10... | collective-permute-start | bytes 294920 | tf_op jit(solution)/shard_map/ppermute | solution.py:391
  728.9 22.9 %collective-permute-start.55 = (bf16[128,384]{0,1:T(8,128)(2,1)S(1)}, bf16[128,384]{0,1:T(8,128)(2,1)S(1)}, u32[]{:S(2)}, u32[]{:S(2)}) collective-permute-start(bf16[128,384]{0,1:T(8,128)(2,1)S(1)} %fusion.51), channel_id=1, source_target_pairs={{0,8},{8,0},{16,24},{24,16},{1,9},{9,1},{17,25},{25,17},{2,10},{10... | collective-permute-start | bytes 294920 | tf_op jit(solution)/shard_map/ppermute | solution.py:391
  767.0 18.2 %collective-permute-start.48 = (bf16[256,1024]{1,0:T(8,128)(2,1)S(1)}, bf16[256,1024]{1,0:T(8,128)(2,1)S(1)}, u32[]{:S(2)}, u32[]{:S(2)}) collective-permute-start(bf16[256,1024]{1,0:T(8,128)(2,1)S(1)} %copy-done.30), channel_id=1, source_target_pairs={{0,8},{8,0},{16,24},{24,16},{1,9},{9,1},{17,25},{25,17},{2,10},{10... | collective-permute-start | bytes 1572872 | tf_op jit(solution)/shard_map/ppermute | solution.py:391
  (90 other events, 864.5 us)
Sparse Core Ops, SparseCore 0:
  10.7 84.5 all-gather.3
  97.4 72.4 all-gather.5
  172.0 75.5 all-gather.7
  414.7 148.3 reduce-scatter.2
  652.9 106.7 reduce-scatter.4

commit v7 on v6

--- a/solution.py
+++ b/solution.py
@@ -39,7 +39,7 @@
     def _():
         hend_ref[...] = h_s[...]
 
-def first_pass(dt, x, bx, a2, waits, Q, TC=256, EG=GROUP, U=8):
+def first_pass(dt, x, bx, a2, waits, Q, TC=512, EG=GROUP, U=8):
     T,E = dt.shape; N = a2.shape[0]; L=T//Q; NC=L//TC; NE=E//EG
     row = pl.BlockSpec((TC,EG), lambda q,e,c:(q*NC+c, e))
     sp = pl.BlockSpec((TC,N,LN), lambda q,e,c:(q*NC+c,0,0))

time: 808 us -> 808 us (level)
  no operation moved by 1% of the time
where the time goes in v7:
time: 808 us; the launch traced here: 800 us
  Pallas kernels  287 us (36%)
  matrix products  153 us (19%)
  waiting for transfers between devices  99.5 us (12%)
  other arithmetic  89 us (11%)
  starting transfers between devices  61.8 us (8%)
  local copies, waits for them, and re-layouts  56.7 us (7%)
  blocking collectives  36.7 us (5%)
  between operations  15.5 us (2%)
    pallas_call x2, Pallas kernels, bwd_pass(): pl.pallas_call(partial(bwd_kernel, U, TB, n_in), grid=(Q, 1, NC), in_spec...  132 us
    pallas_call x1, Pallas kernels, fwd_pass(): pl.pallas_call(partial(fwd_kernel, U, TB), grid=(Q, NE, NC), in_specs=[ro...  72.7 us
    dot_general x6, matrix products, contract_cols(): lax.dot_general(left, right, (((1,), (1,)), ((), ())), preferred_element_...  54.1 us
    dot_general x7, matrix products, contract_rows(): lax.dot_general(left, right, (((0,), (0,)), ((), ())), preferred_element_...  51.3 us
    ppermute x36, waiting for transfers between devices, swap(): lax.ppermute(value, 'rep', [(i, i ^ flip) for i in range(lax.axis_size('r...  37.2 us
    all_gather x1, blocking collectives, on_device(): small_all = lax.all_gather(small, 'shard', axis=0, tiled=True)  36.7 us
    pallas_call x1, Pallas kernels, first_pass(): pl.pallas_call(partial(first_kernel, U), grid=(Q, NE, NC), in_specs=[row,...  29.5 us
    pallas_call x1, Pallas kernels, conv_back(): pl.pallas_call(conv_back_kernel, grid=(Q, E // EB), in_specs=[pl.BlockSpe...  23.8 us
  transfers between devices with their start and end apart: 61, of which 22 were waited for; matrix products, arithmetic and copies ran while one was open for 30% of the time, Pallas kernels for 26%

profile of v7, /device:TPU:0, one launch (start us, length us, event | category | flops | bytes accessed | tf_op | source)
XLA Modules:
  0.0 799.5 jit_solution(10354680164622789182)
XLA Ops:
  23.3 36.7 %all_gather.12 = bf16[1024,313]{0,1:T(8,128)(2,1)S(1)} all-gather(bf16[128,313]{0,1:T(8,128)(2,1)S(1)} %concatenate.75), channel_id=1, replica_groups=mesh['rep'=4,'shard'=8] {'shard'}, dimensions={0}, use_global_device_ids=true | all-gather | bytes 721152 | tf_op jit(solution)/shard_map/all_gather | solution.py:562
  80.1 15.2 %all-gather.4.cloned.1.call-done = bf16[2048,1024]{1,0:T(8,128)(2,1)} async-done(((bf16[256,1024]{1,0:T(8,128)(2,1)}), bf16[2048,1024]{1,0:T(8,128)(2,1)}) %all-gather.4.cloned.1.call-update) | async-done | bytes 4194320 | tf_op jit(solution)/shard_map/all_gather | solution.py:565
  95.3 12.5 %convolution_convert_fusion.x_ref = bf16[2048,1024]{1,0:T(8,128)(2,1)S(1)} fusion(bf16[2048,2048]{1,0:T(8,128)(2,1)} %pad_maximum_fusion, bf16[2048,1024]{1,0:T(8,128)(2,1)} %all-gather.4.cloned.1.call-done), kind=kOutput, calls=%fused_computation.51 | convolution fusion | flops 8592031744 | bytes 16777216 | tf_op jit(solution)/shard_map/dot_general | solution.py:591
  114.5 12.0 %conv_pass.1.x_ref.refs_1_ = bf16[2048,1024]{1,0:T(8,128)(2,1)} custom-call(bf16[2048,1024]{1,0:T(8,128)(2,1)} %copy-done.6, f32[4,8,1024]{2,1,0:T(8,128)} %concatenate.77.edge_ref, f32[5,1024]{1,0:T(8,128)} %convert_bitcast_fusion.1.w_ref), custom_call_target="tpu_custom_call" | custom-call | flops 25165824 | bytes 8388608 | tf_op jit(solution)/shard_map/conv_pass/pallas_call | solution.py:307
  166.6 9.0 %broadcast_in_dim.23.b_ref.refs_3_ = f32[2048,16,128]{2,1,0:T(8,128)} broadcast(f32[2048,16]{1,0:T(8,128)S(1)} %copy-done.12), dimensions={0,1} | broadcast | bytes 16908288 | tf_op jit(solution)/shard_map/broadcast_in_dim | solution.py:599
  175.6 8.9 %broadcast_in_dim.24.refs_0_.c_ref.refs_4_ = f32[2048,16,128]{2,1,0:T(8,128)} broadcast(f32[2048,16]{1,0:T(8,128)S(1)} %copy-done.13), dimensions={0,1} | broadcast | bytes 16908288 | tf_op jit(solution)/shard_map/broadcast_in_dim | solution.py:600
  184.5 29.5 %first_pass.1 = f32[4,16,1024]{2,1,0:T(8,128)} custom-call(f32[2048,1024]{1,0:T(8,128)} %get-tuple-element.175.dt_ref.refs_0_, bf16[2048,1024]{1,0:T(8,128)(2,1)} %conv_pass.1.x_ref.refs_1_, f32[2048,16,128]{2,1,0:T(8,128)} %broadcast_in_dim.23.b_ref.refs_3_, f32[16,1024]{1,0:T(8,128)} %get-tuple-element.143.a_ref.refs_5_, ...), custom_call_target="tpu_custom_call" | custom-call | flops 167772160 | bytes 20971520 | tf_op jit(solution)/shard_map/first_pass/pallas_call | solution.py:47
  217.8 14.6 %fusion.87.gate_ref = f32[2048,1024]{1,0:T(8,128)} fusion(bf16[2048,2048]{1,0:T(8,128)(2,1)} %pad_maximum_fusion, bf16[2048,1024]{1,0:T(8,128)(2,1)} %all-gather.6.cloned.1.call-done), kind=kOutput, calls=%fused_computation.207 | convolution fusion | flops 8589934592 | bytes 20971520 | tf_op jit(solution)/shard_map/dot_general | solution.py:604
  241.1 7.6 all-gather.8.cloned.1.call-done
  248.8 14.5 %fusion.88.gg_ref = f32[2048,1024]{1,0:T(8,128)} fusion(bf16[2048,2048]{1,0:T(8,128)(2,1)} %pad_maximum_fusion.1.refs_1_, bf16[1024,2048]{1,0:T(8,128)(2,1)} %all-gather.8.cloned.1.call-done), kind=kOutput, calls=%fused_computation.208 | convolution fusion | flops 8589934592 | bytes 20971520 | tf_op jit(solution)/shard_map/dot_general | solution.py:387
  274.3 72.7 %fwd_pass.1 = (bf16[2048,1024]{1,0:T(8,128)(2,1)}, bf16[2048,1024]{1,0:T(8,128)(2,1)}, f32[2048,1024]{1,0:T(8,128)}, f32[8,16,1024]{2,1,0:T(8,128)}, f32[4,16,1024]{2,1,0:T(8,128)}) custom-call(f32[2048,1024]{1,0:T(8,128)} %get-tuple-element.175.dt_ref.refs_0_, bf16[2048,1024]{1,0:T(8,128)(2,1)} %conv_pass.1.x_ref.refs_1_, f32[2048,1024]{1,0:T(8,128)} %fusion.87.gate_ref, ...), custom_call_target="tpu_custom_call" | custom-call | flops 369098752 | bytes 46137344 | tf_op jit(solution)/shard_map/fwd_pass/pallas_call | solution.py:115
  347.0 8.2 %fusion.31 = bf16[1024,1024]{1,0:T(8,128)(2,1)S(1)} fusion(bf16[2048,1024]{1,0:T(8,128)(2,1)} %get-tuple-element.69, bf16[2048,2048]{1,0:T(8,128)(2,1)} %pad_maximum_fusion.1.refs_1_), kind=kOutput, calls=%fused_computation.65 | convolution fusion | flops 4296015872 | bytes 10485760 | tf_op jit(solution)/shard_map/dot_general | solution.py:383
  355.2 11.7 %convolution_convert_fusion.2 = bf16[2048,1024]{1,0:T(8,128)(2,1)S(1)} fusion(bf16[2048,2048]{1,0:T(8,128)(2,1)} %pad_maximum_fusion, bf16[2048,1024]{1,0:T(8,128)(2,1)S(1)} %copy-done.14), kind=kOutput, calls=%fused_computation.53 | convolution fusion | flops 8592031744 | bytes 16777216 | tf_op jit(solution)/shard_map/dot_general | solution.py:383
  367.0 16.7 %fusion.84 = (bf16[2048,2048]{1,0:T(8,128)(2,1)}, f32[2048,2048]{1,0:T(8,128)}) fusion(bf16[2048,1024]{1,0:T(8,128)(2,1)} %get-tuple-element.69, bf16[1024,2048]{1,0:T(8,128)(2,1)S(1)} %copy-done.48), kind=kOutput, calls=%fused_computation.204 | convolution fusion | flops 8594128896 | bytes 33554432 | tf_op jit(solution)/shard_map/dot_general | solution.py:617
  402.0 7.9 collective-permute-done.21
  418.7 66.1 %bwd_pass.2 = (bf16[2048,1024]{1,0:T(8,128)(2,1)}, f32[2048,1024]{1,0:T(8,128)}, f32[2,1,32768]{2,1,0:T(1,128)}, f32[2,1,32768]{2,1,0:T(1,128)}, f32[4,16,1024]{2,1,0:T(8,128)}, /*index=5*/f32[4,2,1024]{2,1,0:T(2,128)}) custom-call(f32[2048,1024]{1,0:T(8,128)} %get-tuple-element.175.dt_ref.refs_0_, bf16[2048,1024]{1,0:T(8,128)(2,1)} %conv_pass.1.x_ref.refs_1_, ...), custom_call_target="tpu_custom_call" | custom-call | flops 335544320 | bytes 23068672 | tf_op jit(solution)/shard_map/bwd_pass/pallas_call | solution.py:220
  492.1 66.0 %bwd_pass.3 = (bf16[2048,1024]{1,0:T(8,128)(2,1)}, f32[2048,1024]{1,0:T(8,128)}, f32[2,1,32768]{2,1,0:T(1,128)}, f32[2,1,32768]{2,1,0:T(1,128)}, f32[4,16,1024]{2,1,0:T(8,128)}, /*index=5*/f32[4,2,1024]{2,1,0:T(2,128)}) custom-call(f32[2048,1024]{1,0:T(8,128)} %get-tuple-element.175.dt_r, ...), custom_call_target="tpu_custom_call", output_to_operand_aliasing={{0}: (9, {}), {1}: (10, {}), {2}: (11, {}), {3}: (12, {}), ... | custom-call | flops 335544320 | bytes 23068672 | tf_op jit(solution)/shard_map/bwd_pass/pallas_call | solution.py:220
  595.3 23.8 %conv_back.1 = (bf16[2048,1024]{1,0:T(8,128)(2,1)}, f32[4,8,1024]{2,1,0:T(8,128)}, f32[4,8,1024]{2,1,0:T(8,128)}, f32[4,5,1024]{2,1,0:T(8,128)}) custom-call(bf16[2048,160]{1,0:T(8,128)(2,1)} %maximum_bitcast_fusion.gp_ref, bf16[1024,160]{1,0:T(8,128)(2,1)} %copy.49.xp_ref, f32[2048,1024]{1,0:T(8,128)} %get-tuple-element.87.gx_ref, ...), custom_call_target="tpu_custom_call" | custom-call | flops 838860800 | bytes 20971520 | tf_op jit(solution)/shard_map/conv_back/pallas_call | solution.py:357
  628.5 14.0 %convolution_convert_fusion.1 = bf16[2048,1024]{1,0:T(8,128)(2,1)} fusion(bf16[2048,2048]{1,0:T(8,128)(2,1)} %pad_maximum_fusion, bf16[2048,1024]{1,0:T(8,128)(2,1)} %bitcast.156), kind=kOutput, calls=%fused_computation.52 | convolution fusion | flops 8592031744 | bytes 16777216 | tf_op jit(solution)/shard_map/dot_general | solution.py:383
  653.5 9.8 %fusion.86 = (bf16[1024,2048]{1,0:T(8,128)(2,1)S(1)}, f32[1024,2048]{1,0:T(8,128)S(1)}) fusion(f32[1024,2048]{1,0:T(8,128)} %fusion.89, bf16[1024,1024]{1,0:T(8,128)(2,1)} %bitcast.174, bf16[2048,1024]{1,0:T(8,128)(2,1)} %all-gather.6.cloned.1.call-done), kind=kOutput, calls=%fused_computation.206 | convolution fusion | flops 4299161600 | bytes 27262976 | tf_op jit(solution)/shard_map/dot_general | solution.py:387
  670.5 9.1 %fusion.90 = f32[1024,2048]{1,0:T(8,128)} fusion(bf16[1024,1024]{1,0:T(8,128)(2,1)S(1)} %bitcast.175, bf16[2048,1024]{1,0:T(8,128)(2,1)} %all-gather.4.cloned.1.call-done), kind=kOutput, calls=%fused_computation.210 | convolution fusion | flops 4294967296 | bytes 14680064 | tf_op jit(solution)/shard_map/dot_general | solution.py:387
  682.6 10.2 %fusion.85 = (bf16[1024,2048]{1,0:T(8,128)(2,1)S(1)}, f32[1024,2048]{1,0:T(8,128)}) fusion(f32[1024,2048]{1,0:T(8,128)} %fusion.90, bf16[1024,1024]{1,0:T(8,128)(2,1)S(1)} %bitcast.173, bf16[2048,1024]{1,0:T(8,128)(2,1)} %all-gather.6.cloned.1.call-done), kind=kOutput, calls=%fused_computation.205 | convolution fusion | flops 4299161600 | bytes 27262976 | tf_op jit(solution)/shard_map/dot_general | solution.py:387
  694.8 12.9 %collective-permute-done.34 = bf16[4,128,384]{1,2,0:T(8,128)(2,1)S(1)} collective-permute-done((bf16[4,128,384]{1,2,0:T(8,128)(2,1)}, bf16[4,128,384]{1,2,0:T(8,128)(2,1)S(1)}, u32[]{:S(2)}, u32[]{:S(2)}) %collective-permute-start.34) | collective-permute-done | bytes 393248 | tf_op jit(solution)/shard_map/ppermute | solution.py:436
  729.7 13.7 %collective-permute-done.53 = bf16[128,384]{0,1:T(8,128)(2,1)S(1)} collective-permute-done((bf16[128,384]{0,1:T(8,128)(2,1)S(1)}, bf16[128,384]{0,1:T(8,128)(2,1)S(1)}, u32[]{:S(2)}, u32[]{:S(2)}) %collective-permute-start.53) | collective-permute-done | bytes 98336 | tf_op jit(solution)/shard_map/ppermute | solution.py:391
  (386 shorter events, 280.6 us)
Async XLA Ops:
  7.2 88.1 %all-gather.4.cloned.1.call-start = ((), (), s32[]{:S(2)}) async-start(), calls=%async_computation.2 | async-start | bytes 4718592 | tf_op jit(solution)/shard_map/all_gather | solution.py:565
  9.8 208.0 %all-gather.6.cloned.1.call-start = ((), (), s32[]{:S(2)}) async-start(), calls=%async_computation.3 | async-start | bytes 4718592 | tf_op jit(solution)/shard_map/all_gather | solution.py:566
  12.2 236.5 %all-gather.8.cloned.1.call-start = ((), (), s32[]{:S(2)}) async-start(), calls=%async_computation.4 | async-start | bytes 4718592 | tf_op jit(solution)/shard_map/all_gather | solution.py:567
  12.3 48.8 %collective-permute-start = (bf16[512,2048]{1,0:T(8,128)(2,1)S(1)}, bf16[512,2048]{1,0:T(8,128)(2,1)}, u32[]{:S(2)}, u32[]{:S(2)}) collective-permute-start(bf16[512,2048]{1,0:T(8,128)(2,1)S(1)} %copy-done.2), channel_id=1, source_target_pairs={{0,16},{8,24},{16,0},{24,8},{1,17},{9,25},{17,1},{25,9},{2,18},{10... | collective-permute-start | bytes 6291464 | tf_op jit(solution)/shard_map/ppermute | solution.py:391
  15.3 47.6 %collective-permute-start.1 = (bf16[512,2048]{1,0:T(8,128)(2,1)S(1)}, bf16[512,2048]{1,0:T(8,128)(2,1)}, u32[]{:S(2)}, u32[]{:S(2)}) collective-permute-start(bf16[512,2048]{1,0:T(8,128)(2,1)S(1)} %copy-done.2), channel_id=1, source_target_pairs={{0,8},{8,0},{16,24},{24,16},{1,9},{9,1},{17,25},{25,17},{2,10},{10... | collective-permute-start | bytes 6291464 | tf_op jit(solution)/shard_map/ppermute | solution.py:391
  17.2 577.2 %reduce-scatter.3.cloned.1.call-start = ((), (), s32[]{:S(2)}) async-start(), calls=%async_computation.5 | async-start | bytes 9437184 | tf_op jit(solution)/shard_map/reduce_scatter | solution.py:632
  78.4 53.8 %collective-permute-start.11 = (bf16[512,2048]{1,0:T(8,128)(2,1)S(1)}, bf16[512,2048]{1,0:T(8,128)(2,1)}, u32[]{:S(2)}, u32[]{:S(2)}) collective-permute-start(bf16[512,2048]{1,0:T(8,128)(2,1)S(1)} %copy-done.7), channel_id=1, source_target_pairs={{0,16},{8,24},{16,0},{24,8},{1,17},{9,25},{17,1},{25,9},{2,18},{10... | collective-permute-start | bytes 6291464 | tf_op jit(solution)/shard_map/ppermute | solution.py:391
  113.3 32.2 %collective-permute-start.10 = (bf16[512,2048]{1,0:T(8,128)(2,1)S(1)}, bf16[512,2048]{1,0:T(8,128)(2,1)}, u32[]{:S(2)}, u32[]{:S(2)}) collective-permute-start(bf16[512,2048]{1,0:T(8,128)(2,1)S(1)} %copy-done.7), channel_id=1, source_target_pairs={{0,8},{8,0},{16,24},{24,16},{1,9},{9,1},{17,25},{25,17},{2,10},{10... | collective-permute-start | bytes 6291464 | tf_op jit(solution)/shard_map/ppermute | solution.py:391
  132.2 27.6 %collective-permute-start.12 = (bf16[512,2048]{1,0:T(8,128)(2,1)}, bf16[512,2048]{1,0:T(8,128)(2,1)}, u32[]{:S(2)}, u32[]{:S(2)}) collective-permute-start(bf16[512,2048]{1,0:T(8,128)(2,1)} %collective-permute-done.11), channel_id=1, source_target_pairs={{0,8},{8,0},{16,24},{24,16},{1,9},{9,1},{17,25},{25,17},{2,10},{10... | collective-permute-start | bytes 6291464 | tf_op jit(solution)/shard_map/ppermute | solution.py:391
  232.6 38.2 %collective-permute-start.15 = (bf16[68,1024]{1,0:T(8,128)(2,1)S(1)}, bf16[68,1024]{1,0:T(8,128)(2,1)S(1)}, u32[]{:S(2)}, u32[]{:S(2)}) collective-permute-start(bf16[68,1024]{1,0:T(8,128)(2,1)S(1)} %pad_maximum_fusion.8), channel_id=1, source_target_pairs={{0,4},{1,5},{2,6},{3,7},{8,12},{9,13},{10,14},{11,15},{16,20},{17,... | collective-permute-start | bytes 417800 | tf_op jit(solution)/shard_map/ppermute | solution.py:471
  238.4 32.5 %collective-permute-start.14 = (bf16[68,1024]{1,0:T(8,128)(2,1)S(1)}, bf16[68,1024]{1,0:T(8,128)(2,1)S(1)}, u32[]{:S(2)}, u32[]{:S(2)}) collective-permute-start(bf16[68,1024]{1,0:T(8,128)(2,1)S(1)} %pad_maximum_fusion.8), channel_id=1, source_target_pairs={{0,2},{1,3},{2,4},{3,5},{4,6},{5,7},{8,10},{9,11},{10,12},{11,13},... | collective-permute-start | bytes 417800 | tf_op jit(solution)/shard_map/ppermute | solution.py:471
  387.8 23.2 %collective-permute-start.18 = (bf16[512,2048]{1,0:T(8,128)(2,1)S(1)}, bf16[512,2048]{1,0:T(8,128)(2,1)S(1)}, u32[]{:S(2)}, u32[]{:S(2)}) collective-permute-start(bf16[512,2048]{1,0:T(8,128)(2,1)S(1)} %get-tuple-element.121), channel_id=1, source_target_pairs={{0,8},{8,0},{16,24},{24,16},{1,9},{9,1},{17,25},{25,17},{2,10},{10... | collective-permute-start | bytes 6291464 | tf_op jit(solution)/shard_map/ppermute | solution.py:391
  415.2 345.0 %reduce-scatter.5.cloned.1.call-start = ((), (), s32[]{:S(2)}) async-start(), calls=%async_computation.6 | async-start | bytes 4718592 | tf_op jit(solution)/shard_map/reduce_scatter | solution.py:632
  415.3 69.5 %collective-permute-start.17 = (bf16[512,2048]{1,0:T(8,128)(2,1)}, bf16[512,2048]{1,0:T(8,128)(2,1)}, u32[]{:S(2)}, u32[]{:S(2)}) collective-permute-start(bf16[512,2048]{1,0:T(8,128)(2,1)} %get-tuple-element.120), channel_id=1, source_target_pairs={{0,8},{8,0},{16,24},{24,16},{1,9},{9,1},{17,25},{25,17},{2,10},{10... | collective-permute-start | bytes 6291464 | tf_op jit(solution)/shard_map/ppermute | solution.py:391
  415.4 69.4 %collective-permute-start.23 = (bf16[512,2048]{1,0:T(8,128)(2,1)}, bf16[512,2048]{1,0:T(8,128)(2,1)}, u32[]{:S(2)}, u32[]{:S(2)}) collective-permute-start(bf16[512,2048]{1,0:T(8,128)(2,1)} %fusion.18.refs_10_), channel_id=1, source_target_pairs={{0,16},{8,24},{16,0},{24,8},{1,17},{9,25},{17,1},{25,9},{2,18},{10... | collective-permute-start | bytes 6291464 | tf_op jit(solution)/shard_map/ppermute | solution.py:391
  594.4 59.0 %collective-permute-start.35 = (bf16[512,1024]{1,0:T(8,128)(2,1)}, bf16[512,1024]{1,0:T(8,128)(2,1)}, u32[]{:S(2)}, u32[]{:S(2)}) collective-permute-start(bf16[512,1024]{1,0:T(8,128)(2,1)} %reduce-scatter.3.cloned.1.call-done), channel_id=1, source_target_pairs={{0,8},{8,0},{16,24},{24,16},{1,9},{9,1},{17,25},{25,17},{2,10},{10... | collective-permute-start | bytes 3145736 | tf_op jit(solution)/shard_map/ppermute | solution.py:391
  594.5 48.0 %collective-permute-start.36 = (bf16[512,1024]{1,0:T(8,128)(2,1)}, bf16[512,1024]{1,0:T(8,128)(2,1)}, u32[]{:S(2)}, u32[]{:S(2)}) collective-permute-start(bf16[512,1024]{1,0:T(8,128)(2,1)} %reduce-scatter.3.cloned.1.call-done), channel_id=1, source_target_pairs={{0,16},{8,24},{16,0},{24,8},{1,17},{9,25},{17,1},{25,9},{2,18},{10... | collective-permute-start | bytes 3145736 | tf_op jit(solution)/shard_map/ppermute | solution.py:391
  665.6 42.1 %collective-permute-start.34 = (bf16[4,128,384]{1,2,0:T(8,128)(2,1)}, bf16[4,128,384]{1,2,0:T(8,128)(2,1)S(1)}, u32[]{:S(2)}, u32[]{:S(2)}) collective-permute-start(bf16[4,128,384]{1,2,0:T(8,128)(2,1)} %dynamic-slice_convert_fusion), channel_id=1, source_target_pairs={{0,4},{1,5},{2,6},{3,7},{4,0},{5,1},{6,2},{7,3},{8,12},{9,13},{10,... | collective-permute-start | bytes 1179656 | tf_op jit(solution)/shard_map/ppermute | solution.py:436
  670.5 37.3 %collective-permute-start.31 = (bf16[256,2048]{1,0:T(8,128)(2,1)}, bf16[256,2048]{1,0:T(8,128)(2,1)}, u32[]{:S(2)}, u32[]{:S(2)}) collective-permute-start(bf16[256,2048]{1,0:T(8,128)(2,1)} %get-tuple-element.122), channel_id=1, source_target_pairs={{0,8},{8,0},{16,24},{24,16},{1,9},{9,1},{17,25},{25,17},{2,10},{10... | collective-permute-start | bytes 3145736 | tf_op jit(solution)/shard_map/ppermute | solution.py:391
  681.0 26.9 %collective-permute-start.33 = (bf16[256,2048]{1,0:T(8,128)(2,1)}, bf16[256,2048]{1,0:T(8,128)(2,1)}, u32[]{:S(2)}, u32[]{:S(2)}) collective-permute-start(bf16[256,2048]{1,0:T(8,128)(2,1)} %fusion.26), channel_id=1, source_target_pairs={{0,16},{8,24},{16,0},{24,8},{1,17},{9,25},{17,1},{25,9},{2,18},{10... | collective-permute-start | bytes 3145736 | tf_op jit(solution)/shard_map/ppermute | solution.py:391
  716.1 44.2 %collective-permute-start.40 = (bf16[256,2048]{1,0:T(8,128)(2,1)}, bf16[256,2048]{1,0:T(8,128)(2,1)}, u32[]{:S(2)}, u32[]{:S(2)}) collective-permute-start(bf16[256,2048]{1,0:T(8,128)(2,1)} %get-tuple-element.118), channel_id=1, source_target_pairs={{0,16},{8,24},{16,0},{24,8},{1,17},{9,25},{17,1},{25,9},{2,18},{10... | collective-permute-start | bytes 3145736 | tf_op jit(solution)/shard_map/ppermute | solution.py:391
  724.9 18.6 %collective-permute-start.53 = (bf16[128,384]{0,1:T(8,128)(2,1)S(1)}, bf16[128,384]{0,1:T(8,128)(2,1)S(1)}, u32[]{:S(2)}, u32[]{:S(2)}) collective-permute-start(bf16[128,384]{0,1:T(8,128)(2,1)S(1)} %fusion.51), channel_id=1, source_target_pairs={{0,16},{8,24},{16,0},{24,8},{1,17},{9,25},{17,1},{25,9},{2,18},{10... | collective-permute-start | bytes 294920 | tf_op jit(solution)/shard_map/ppermute | solution.py:391
  729.6 22.6 %collective-permute-start.55 = (bf16[128,384]{0,1:T(8,128)(2,1)S(1)}, bf16[128,384]{0,1:T(8,128)(2,1)S(1)}, u32[]{:S(2)}, u32[]{:S(2)}) collective-permute-start(bf16[128,384]{0,1:T(8,128)(2,1)S(1)} %fusion.51), channel_id=1, source_target_pairs={{0,8},{8,0},{16,24},{24,16},{1,9},{9,1},{17,25},{25,17},{2,10},{10... | collective-permute-start | bytes 294920 | tf_op jit(solution)/shard_map/ppermute | solution.py:391
  767.6 18.2 %collective-permute-start.48 = (bf16[256,1024]{1,0:T(8,128)(2,1)S(1)}, bf16[256,1024]{1,0:T(8,128)(2,1)S(1)}, u32[]{:S(2)}, u32[]{:S(2)}) collective-permute-start(bf16[256,1024]{1,0:T(8,128)(2,1)S(1)} %copy-done.30), channel_id=1, source_target_pairs={{0,8},{8,0},{16,24},{24,16},{1,9},{9,1},{17,25},{25,17},{2,10},{10... | collective-permute-start | bytes 1572872 | tf_op jit(solution)/shard_map/ppermute | solution.py:391
  (90 other events, 863.8 us)
Sparse Core Ops, SparseCore 0:
  10.7 84.5 all-gather.3
  97.4 72.4 all-gather.5
  172.0 76.6 all-gather.7
  415.4 148.2 reduce-scatter.2
  653.6 106.5 reduce-scatter.4
